TPU v7x, 32 devices: a whole 2x2x4 slice. The times are simulated.
32 devices in a mesh: groups: 2 (over y), seq: 8 (over z, core), dp: 2 (over x).
Axes of the slice: x: 2, y: 2, z: 4, core: 2. Of those that a mesh axis runs over, the one named last changes fastest.
Arguments:
- tokens: bfloat16 [4, 1024, 1024], P(('groups', 'dp'), 'seq'), parts along dimension 0, may hold values from -6 to 6
- w_query: bfloat16 [1024, 1024], replicated, may hold values from -0.1875 to 0.1875
- w_key: bfloat16 [1024, 1024], replicated, may hold values from -0.1875 to 0.1875
- w_value: bfloat16 [1024, 1024], replicated, may hold values from -0.1875 to 0.1875
- w_output: bfloat16 [1024, 1024], replicated, may hold values from -0.1875 to 0.1875
- out_cotangent: bfloat16 [4, 1024, 1024], P(('groups', 'dp'), 'seq'), parts along dimension 0, may hold values from -6 to 6
Outputs:
- attended: bfloat16 [4, 1024, 1024], P(('groups', 'dp'), 'seq'), parts along dimension 0
- d_tokens: bfloat16 [4, 1024, 1024], P(('groups', 'dp'), 'seq'), parts along dimension 0
- weight_grads: float32 [2048, 4096], P(('groups', 'seq', 'dp')), parts along dimension 0
There are 2 independent parts, one for each index of `groups`. A program takes and returns all parts, laid end to end along the dimension named above; an argument that names none is the same for every part. Nothing has to cross between parts.
All inputs are finite; a program needn't handle non-finite values.
Results may differ from a plain program's by a relative error of at most 0.008.
Values sent between devices are 32-bit elements; how exact they have to be, the bound alone decides.
No kernel may reach another device: no remote copies, remote signals or barrier semaphores. Data moves between devices by JAX's collectives and lax.ppermute only.
A program may use at most 128 MiB of HBM per device.

v0:
```python
import math

import jax
import jax.numpy as jnp
from jax import lax
from jax.sharding import PartitionSpec as P

H = 8


EPSILON = 1e-05


def entering(value, axis, combine, identity, reverse):
    devices, place = (lax.axis_size(axis), lax.axis_index(axis))
    everything = lax.all_gather(value, axis)
    start = jnp.broadcast_to(jnp.asarray(identity, value.dtype), value.shape)

    def hop(k, before):
        at = devices - 1 - k if reverse else k
        reached = at > place if reverse else at < place
        new = combine(before, everything[at])
        return jnp.where(reached, new, before)

    return lax.fori_loop(0, devices, hop, start)


def causal_mask(row_count):
    rows = lax.broadcasted_iota(jnp.int32, (row_count, row_count), 0)
    cols = lax.broadcasted_iota(jnp.int32, (row_count, row_count), 1)
    return rows >= cols


def add_states(earlier, later_part):
    return earlier + later_part


def local(tokens, w_query, w_key, w_value, w_output, out_cotangent):
    clip_count, row_count, model_width = tokens.shape
    head_count = H
    head_size = model_width // head_count
    flattened = tokens.reshape(clip_count * row_count, model_width)

    def project(weight):
        product = jnp.dot(flattened, weight, preferred_element_type=jnp.float32).astype(
            jnp.bfloat16
        )
        return product.reshape(clip_count, row_count, head_count, head_size)

    queries = project(w_query)
    key_rows = project(w_key)
    value_rows = project(w_value)
    own_state = jnp.einsum(
        "cshd,cshe->chde", key_rows, value_rows, preferred_element_type=jnp.float32
    )
    carried = entering(own_state, "seq", add_states, jnp.zeros_like(own_state), False)
    carried = carried.astype(jnp.bfloat16)
    causal = causal_mask(row_count)
    scores = jnp.einsum("cthd,cshd->chts", queries, key_rows, preferred_element_type=jnp.float32)
    attn_weights = jnp.where(causal, scores, 0.0).astype(jnp.bfloat16)
    mixed = jnp.einsum(
        "chts,cshd->cthd", attn_weights, value_rows, preferred_element_type=jnp.float32
    )
    mixed = mixed + jnp.einsum(
        "cthd,chde->cthe", queries, carried, preferred_element_type=jnp.float32
    )
    mixed = mixed.reshape(clip_count, row_count, model_width)
    scale_rows = jnp.sqrt(jnp.mean(mixed * mixed, axis=-1, keepdims=True) + EPSILON)
    normed = mixed / scale_rows
    normed_flat = normed.astype(jnp.bfloat16).reshape(-1, model_width)
    attended = jnp.dot(normed_flat, w_output, preferred_element_type=jnp.float32).astype(
        jnp.bfloat16
    )
    attended = attended.reshape(clip_count, row_count, model_width)
    cot_flat = out_cotangent.reshape(-1, model_width)
    back_norm = jnp.einsum("ne,de->nd", cot_flat, w_output, preferred_element_type=jnp.float32)
    back_norm = back_norm.reshape(clip_count, row_count, model_width)
    d_mixed = (
        (back_norm - normed * jnp.mean(back_norm * normed, axis=-1, keepdims=True)) / scale_rows
    ).astype(jnp.bfloat16)
    d_heads = d_mixed.reshape(clip_count, row_count, head_count, head_size)
    own_back = jnp.einsum("cthd,cthe->chde", queries, d_heads, preferred_element_type=jnp.float32)
    later = entering(own_back, "seq", add_states, jnp.zeros_like(own_back), True)
    later = later.astype(jnp.bfloat16)
    back_scores = jnp.einsum(
        "cthe,cshe->chts", d_heads, value_rows, preferred_element_type=jnp.float32
    )
    back_scores = jnp.where(causal, back_scores, 0.0).astype(jnp.bfloat16)
    d_query = jnp.einsum(
        "chts,cshd->cthd", back_scores, key_rows, preferred_element_type=jnp.float32
    )
    d_query = d_query + jnp.einsum(
        "cthe,chde->cthd", d_heads, carried, preferred_element_type=jnp.float32
    )
    d_key = jnp.einsum("chts,cthd->cshd", back_scores, queries, preferred_element_type=jnp.float32)
    d_key = d_key + jnp.einsum(
        "cshe,chde->cshd", value_rows, later, preferred_element_type=jnp.float32
    )
    d_value = jnp.einsum(
        "chts,cthe->cshe", attn_weights, d_heads, preferred_element_type=jnp.float32
    )
    d_value = d_value + jnp.einsum(
        "cshd,chde->cshe", key_rows, later, preferred_element_type=jnp.float32
    )
    d_query = d_query.astype(jnp.bfloat16).reshape(-1, model_width)
    d_key = d_key.astype(jnp.bfloat16).reshape(-1, model_width)
    d_value = d_value.astype(jnp.bfloat16).reshape(-1, model_width)
    d_tokens = jnp.einsum("nd,ed->ne", d_query, w_query, preferred_element_type=jnp.float32)
    d_tokens = d_tokens + jnp.einsum("nd,ed->ne", d_key, w_key, preferred_element_type=jnp.float32)
    d_tokens = d_tokens + jnp.einsum(
        "nd,ed->ne", d_value, w_value, preferred_element_type=jnp.float32
    )
    d_tokens = d_tokens.astype(jnp.bfloat16).reshape(clip_count, row_count, model_width)
    joined = jnp.concatenate([d_query, d_key, d_value], axis=1)
    summed = lax.psum_scatter(
        jnp.concatenate(
            [
                jnp.einsum("nd,ne->de", flattened, joined, preferred_element_type=jnp.float32),
                jnp.einsum("nd,ne->de", normed_flat, cot_flat, preferred_element_type=jnp.float32),
            ],
            axis=1,
        ),
        ("seq", "dp"),
        scatter_dimension=0,
        tiled=True,
    )
    token_total = clip_count * lax.axis_size("dp") * row_count * lax.axis_size("seq")
    weight_grads = summed * (1.0 / math.sqrt(token_total))
    return (attended, d_tokens, weight_grads)


def solution(mesh):
    return jax.shard_map(
        local,
        mesh=mesh,
        in_specs=(
            P(("groups", "dp"), "seq", None),
            P(),
            P(),
            P(),
            P(),
            P(("groups", "dp"), "seq", None),
        ),
        out_specs=(
            P(("groups", "dp"), "seq", None),
            P(("groups", "dp"), "seq", None),
            P(("groups", "seq", "dp"), None),
        ),
        check_vma=False,
    )
```

profile of v0, /device:TPU:0, one launch (start us, length us, event | category | flops | bytes accessed | tf_op | source)
XLA Modules:
  0.0 358.0 jit_solution(14721868097175616498)
XLA Ops:
  7.2 2.3 fusion.7
  10.5 1.0 fusion.22
  11.6 2.7 convolution_convert_fusion.2
  14.4 1.1 copy.57
  15.5 1.4 fusion
  17.6 1.1 fusion.18
  18.7 42.8 %all-gather.5.cloned.1.call-done = f32[64,128,128]{2,1,0:T(8,128)} async-done(((f32[8,128,128]{2,1,0:T(8,128)}), f32[64,128,128]{2,1,0:T(8,128)}) %all-gather.5.cloned.1.call-update) | async-done | bytes 4194320 | tf_op jit(solution)/shard_map/all_gather | solution.py:16
  61.5 10.0 %while.30 = (s32[]{:T(128)}, f32[1,8,128,128]{3,2,1,0:T(8,128)S(1)}, s32[]{:T(128)}, f32[8,1,8,128,128]{4,3,2,1,0:T(8,128)}, s32[]{:T(128)}, /*index=5*/s32[]{:T(128)}) while((s32[]{:T(128)}, f32[1,8,128,128]{3,2,1,0:T(8,128)S(1)}, s32[]{:T(128)}, f32[8,1,8,128,128]{4,3,2,1,0:T(8,128)}, s32[]{:T(128)}, /*index=5*/s32[]{:T(128)}) %tuple.92), condition=%wide.region_1.2_spmd.clone, body=%wide.region_0.1_spmd.clone.sunk | while | flops 393220 | bytes 1572965 | solution.py:25
  61.5 1.2 add_select_fusion.4
  62.8 1.2 add_select_fusion.4
  64.0 1.2 add_select_fusion.4
  65.3 1.2 add_select_fusion.4
  66.5 1.2 add_select_fusion.4
  67.8 1.2 add_select_fusion.4
  69.0 1.2 add_select_fusion.4
  70.3 1.2 add_select_fusion.4
  71.5 1.5 fusion.15
  73.0 1.0 copy.39
  74.0 2.1 multiply_reduce_fusion
  76.5 2.1 fusion.51
  78.8 1.2 fusion.14
  79.9 1.4 fusion.1
  81.3 1.2 fusion.48
  82.6 1.1 fusion.50
  83.7 1.0 fusion.52
  85.6 2.8 fusion.26
  88.4 36.3 %all-gather.7.cloned.1.call-done = f32[64,128,128]{2,1,0:T(8,128)} async-done(((f32[8,128,128]{2,1,0:T(8,128)}), f32[64,128,128]{2,1,0:T(8,128)}) %all-gather.7.cloned.1.call-update) | async-done | bytes 4194320 | tf_op jit(solution)/shard_map/all_gather | solution.py:16
  124.7 10.1 %while.31 = (s32[]{:T(128)}, f32[1,8,128,128]{3,2,1,0:T(8,128)S(1)}, s32[]{:T(128)}, f32[8,1,8,128,128]{4,3,2,1,0:T(8,128)}, s32[]{:T(128)}, /*index=5*/s32[]{:T(128)}, s32[]{:T(128)}, s32[]{:T(128)}) while((s32[]{:T(128)}, f32[1,8,128,128]{3,2,1,0:T(8,128)S(1)}, s32[]{:T(128)}, f32[8,1,8,128,128]{4,3,2,1,0:T(8,128)}, s32[]{:T(128)}, ...), condition=%wide.region_5.6_spmd.clone, body=%wide.region_4.5_spmd.clone.sunk | while | flops 393224 | bytes 1573027 | solution.py:25
  124.7 1.3 add_select_fusion.5
  126.0 1.2 add_select_fusion.5
  127.2 1.2 add_select_fusion.5
  128.5 1.2 add_select_fusion.5
  129.8 1.2 add_select_fusion.5
  131.0 1.2 add_select_fusion.5
  132.3 1.2 add_select_fusion.5
  133.5 1.2 add_select_fusion.5
  134.8 1.4 fusion.3
  136.2 1.5 fusion.4
  137.7 1.8 convolution_bitcast_fusion
  139.9 7.1 %pad_maximum_fusion = f32[1024,4096]{0,1:T(8,128)} fusion(f32[1024,1024]{0,1:T(8,128)S(1)} %copy-done.1, f32[1024,3072]{0,1:T(8,128)S(1)} %convolution_bitcast_fusion), kind=kLoop, calls=%fused_computation.2 | loop fusion | flops 4194304 | bytes 33554432 | tf_op jit(solution)/shard_map/concatenate | solution.py:116
  147.1 17.5 %copy.55 = f32[1024,4096]{1,0:T(8,128)} copy(f32[1024,4096]{0,1:T(8,128)} %pad_maximum_fusion) | data formatting | bytes 33554432
  164.6 1.0 copy-done.20
  165.6 1.2 fusion.8
  170.6 1.6 fusion.6
  172.2 169.9 %reduce-scatter.4.cloned.1.call-done = f32[64,4096]{1,0:T(8,128)} async-done(((f32[1024,4096]{1,0:T(8,128)}), f32[64,4096]{1,0:T(8,128)}) %reduce-scatter.4.cloned.1.call-update) | async-done | bytes 1048592
  342.0 3.2 copy.56
  345.2 3.1 broadcast_multiply_fusion
  348.3 3.1 copy.52
  (66 shorter events, 7.4 us)
Async XLA Ops:
  7.2 66.9 %copy-start = (bf16[1024,1024]{1,0:T(8,128)(2,1)S(1)}, bf16[1024,1024]{1,0:T(8,128)(2,1)}, u32[]{:S(2)}) copy-start(bf16[1024,1024]{1,0:T(8,128)(2,1)} %param.14) | copy-start | bytes 6291460
  7.2 2.3 copy-start.7
  7.2 54.3 %all-gather.5.cloned.1.call-start = ((), (), s32[]{:S(2)}) async-start(), calls=%async_computation.1 | async-start | bytes 4718592 | tf_op jit(solution)/shard_map/all_gather | solution.py:16
  7.2 2.5 copy-start.4
  9.7 7.2 %copy-start.8 = (bf16[16,8,8,128]{3,2,1,0:T(8,128)(2,1)}, bf16[16,8,8,128]{3,2,1,0:T(8,128)(2,1)S(1)}, u32[]{:S(2)}) copy-start(bf16[16,8,8,128]{3,2,1,0:T(8,128)(2,1)S(1)} %fusion.7) | copy-start | bytes 786436
  10.2 1.4 copy-start.17
  10.5 1.1 copy-start.18
  11.5 113.2 %all-gather.7.cloned.1.call-start = ((), (), s32[]{:S(2)}) async-start(), calls=%async_computation.2 | async-start | bytes 4718592 | tf_op jit(solution)/shard_map/all_gather | solution.py:16
  15.5 46.0 %copy-start.10 = (bf16[128,1024]{0,1:T(8,128)(2,1)}, bf16[128,1024]{0,1:T(8,128)(2,1)S(1)}, u32[]{:S(2)}) copy-start(bf16[128,1024]{0,1:T(8,128)(2,1)S(1)} %copy.57) | copy-start | bytes 786436
  16.9 0.7 copy-start.21
  73.0 3.1 copy-start.6
  74.0 2.1 copy-start.19
  76.5 2.2 copy-start.12
  78.7 263.3 %reduce-scatter.4.cloned.1.call-start = ((), (), s32[]{:S(2)}) async-start(), calls=%async_computation.3 | async-start | bytes 17825792
  78.7 3.8 %copy-start.11 = (bf16[128,1024]{0,1:T(8,128)(2,1)S(1)}, bf16[128,1024]{0,1:T(8,128)(2,1)}, u32[]{:S(2)}) copy-start(bf16[128,1024]{0,1:T(8,128)(2,1)} %copy-done.10) | copy-start | bytes 786436
  78.7 4.9 %copy-start.13 = (bf16[128,1024]{0,1:T(8,128)(2,1)S(1)}, bf16[128,1024]{0,1:T(8,128)(2,1)}, u32[]{:S(2)}) copy-start(bf16[128,1024]{0,1:T(8,128)(2,1)} %copy-done.12) | copy-start | bytes 786436
  78.8 4.9 %copy-start.22 = (bf16[8,128,128]{2,1,0:T(8,128)(2,1)S(1)}, bf16[8,128,128]{2,1,0:T(8,128)(2,1)}, u32[]{:S(2)}) copy-start(bf16[8,128,128]{2,1,0:T(8,128)(2,1)} %copy-done.21) | copy-start | bytes 786436
  82.6 3.1 copy-start.23
  124.7 10.1 %copy-start.9 = (bf16[16,8,8,128]{3,2,1,0:T(8,128)(2,1)S(1)}, bf16[16,8,8,128]{3,2,1,0:T(8,128)(2,1)}, u32[]{:S(2)}) copy-start(bf16[16,8,8,128]{3,2,1,0:T(8,128)(2,1)} %copy-done.8) | copy-start | bytes 786436
  134.8 3.0 copy-start.14
  136.2 1.6 copy-start.15
  137.7 2.2 copy-start.1
  164.5 1.0 copy-start.20
  165.6 1.7 copy-start.3
  167.3 1.6 copy-start.5
  167.3 1.7 copy-start.16
  169.0 1.6 copy-start.2
Sparse Core Ops, SparseCore 0:
  11.7 49.8 all-gather.4
  78.8 45.8 all-gather.6
  164.7 177.2 reduce-scatter.3
where the time goes:
time: 360 us; the launch traced here: 358 us
  waiting for transfers between devices  249 us (69%)
  matrix products  32.2 us (9%)
  other arithmetic  31.3 us (9%)
  local copies, waits for them, and re-layouts  30.9 us (9%)
  between operations  14.1 us (4%)
    unnamed x4, waiting for transfers between devices  170 us
    all_gather x2, waiting for transfers between devices, entering(): everything = lax.all_gather(value, axis)  79.1 us
    unnamed x52, local copies, waits for them, and re-layouts  28.4 us
    select_n x16, other arithmetic, hop(): return jnp.where(reached, new, before)  19.7 us
  transfers between devices with their start and end apart: 3, of which 3 were waited for; matrix products, arithmetic and copies ran while one was open for 6% of the time, Pallas kernels for 0%

commit v1 on v0

v1 whole, which is shorter than its diff:
```python
import functools
import math

import jax
import jax.numpy as jnp
from jax import lax
from jax.experimental import pallas as pl
from jax.experimental.pallas import tpu as pltpu
from jax.sharding import PartitionSpec as P

H = 8
EPSILON = 1e-05
PIECES = 4
F32, BF16 = jnp.float32, jnp.bfloat16
WHOLE = pl.BlockSpec(memory_space=pltpu.VMEM)


def call(body, info, outs, ins, scratch=(), name=None, flops=0):
    arrays, specs, moved = [], [], 0
    for entry in ins:
        if isinstance(entry, tuple):
            array, block, index = entry
            arrays.append(array)
            specs.append(pl.BlockSpec(block, index))
            moved += math.prod(block) * array.dtype.itemsize
        else:
            arrays.append(entry)
            specs.append(WHOLE)
            moved += entry.size * entry.dtype.itemsize
    shapes = [jax.ShapeDtypeStruct(shape, dtype) for shape, dtype in outs]
    moved += sum(math.prod(shape) * jnp.dtype(dtype).itemsize for shape, dtype in outs)
    return pl.pallas_call(
        body,
        name=name,
        out_shape=shapes,
        grid_spec=pltpu.PrefetchScalarGridSpec(
            num_scalar_prefetch=1,
            grid=(1,),
            in_specs=specs,
            out_specs=[WHOLE] * len(shapes),
            scratch_shapes=list(scratch),
        ),
        compiler_params=pltpu.CompilerParams(vmem_limit_bytes=40 * 2**20),
        cost_estimate=pl.CostEstimate(flops=flops, bytes_accessed=moved, transcendentals=0),
    )(info, *arrays)


def dot(a, b, over=(1, 0)):
    return lax.dot_general(
        a, b, (((over[0],), (over[1],)), ((), ())), preferred_element_type=F32
    )


def head(array, h, size):
    return array[:, h * size : (h + 1) * size]


def causal(info_ref, rows, count):
    seq = info_ref[0]

    def position(dim):
        at = lax.broadcasted_iota(jnp.int32, (count, count), dim)
        piece = jnp.bitwise_xor(at // rows, seq)
        return piece * rows + at % rows

    return position(0) >= position(1)


def across(ref, rows):
    order = [piece ^ 1 for piece in range(PIECES)]
    return jnp.concatenate([ref[piece * rows : (piece + 1) * rows] for piece in order], axis=0)


def project_body(size, info, first, second, w_q, w_k, w_v, *rest):
    if len(rest) == 6:
        before, q_out, k_out, v_out, state_out, rows_out = rest
    else:
        before = None
        q_out, k_out, v_out, state_out, rows_out = rest
    rows = jnp.concatenate([first[...].astype(BF16), second[...].astype(BF16)], axis=0)
    rows_out[...] = rows
    q_out[...] = dot(rows, w_q[...]).astype(BF16)
    keys = dot(rows, w_k[...]).astype(BF16)
    k_out[...] = keys
    values = dot(rows, w_v[...]).astype(BF16)
    v_out[...] = values
    for h in range(keys.shape[1] // size):
        state = dot(head(keys, h, size), head(values, h, size), (0, 0))
        if before is not None:
            state = state + before[h * size : (h + 1) * size]
        state_out[h * size : (h + 1) * size] = state


def inside_body(rows, size, info, q0, q1, k0, k1, v0, v1, c0, c1, c2, c3, w_o, *outs):
    q_out, k_out, v_out, attn_out, mixed_out, back_out, cot_out = outs
    q = jnp.concatenate([q0[...], q1[...]], axis=0)
    k = jnp.concatenate([k0[...], k1[...]], axis=0)
    v = jnp.concatenate([v0[...], v1[...]], axis=0)
    q_out[...], k_out[...], v_out[...] = q, k, v
    mask = causal(info, rows, q.shape[0])
    for h in range(q.shape[1] // size):
        scores = dot(head(q, h, size), head(k, h, size), (1, 1))
        attn = jnp.where(mask, scores, 0.0).astype(BF16)
        attn_out[h] = attn
        mixed_out[:, h * size : (h + 1) * size] = dot(attn, head(v, h, size))
    cot = jnp.concatenate([c[...].astype(BF16) for c in (c0, c1, c2, c3)], axis=0)
    cot_out[...] = cot
    back_out[...] = dot(cot, w_o[...], (1, 1))


def stats_body(size, info, q, carried, inner, back, mixed_out, stats_out):
    for h in range(q.shape[1] // size):
        state = carried[h * size : (h + 1) * size].astype(BF16)
        mixed_out[:, h * size : (h + 1) * size] = inner[:, h * size : (h + 1) * size] + dot(
            head(q, h, size), state
        )
    mixed = mixed_out[...]
    squares = jnp.sum(mixed * mixed, axis=1, keepdims=True)
    cross = jnp.sum(mixed * back[...], axis=1, keepdims=True)
    lane = lax.broadcasted_iota(jnp.int32, stats_out.shape, 1)
    stats_out[...] = jnp.where(lane == 0, squares, cross)


def norm_body(rows, size, width, info, q, mixed, back, mine, other, normed_out, d_out, state_out):
    total = mine[...] + across(other, rows)
    squares, cross = total[:, 0:1], total[:, 1:2]
    scale = jnp.sqrt(squares * (1.0 / width) + EPSILON)
    normed = mixed[...] / scale
    normed_out[...] = normed.astype(BF16).astype(F32)
    mean = cross / scale * (1.0 / width)
    d_mixed = ((back[...] - normed * mean) / scale).astype(BF16)
    d_out[...] = d_mixed
    for h in range(q.shape[1] // size):
        state_out[h * size : (h + 1) * size] = dot(head(q, h, size), head(d_mixed, h, size), (0, 0))


def back_body(rows, size, info, q, k, v, d_mixed, attn, carried, dq_out, dk_out, dv_out):
    mask = causal(info, rows, q.shape[0])
    for h in range(q.shape[1] // size):
        at = slice(h * size, (h + 1) * size)
        d_head = d_mixed[:, at]
        scores = dot(d_head, v[:, at], (1, 1))
        scores = jnp.where(mask, scores, 0.0).astype(BF16)
        state = carried[at].astype(BF16)
        dq_out[:, at] = (dot(scores, k[:, at]) + dot(d_head, state, (1, 1))).astype(BF16)
        dk_out[:, at] = dot(scores, q[:, at], (0, 0))
        dv_out[:, at] = dot(attn[h], d_head, (0, 0))


def finish_body(size, info, k, v, later, dk_in, dv_in, dk_out, dv_out):
    for h in range(k.shape[1] // size):
        at = slice(h * size, (h + 1) * size)
        state = later[at].astype(BF16)
        dk_out[:, at] = (dk_in[:, at] + dot(v[:, at], state, (1, 1))).astype(BF16)
        dv_out[:, at] = (dv_in[:, at] + dot(k[:, at], state)).astype(BF16)


def split_rows(info, n_seq, n_dp, total, keep_out, send_out):
    block = total.shape[0] // (n_seq * n_dp)
    kept = keep_out.shape[0] // block
    for slot in range(n_seq * n_dp):
        i, j = slot // n_seq, slot % n_seq
        owner = jnp.bitwise_xor(info[0], j) * n_dp + jnp.bitwise_xor(info[1], i)
        part = total[pl.ds(pl.multiple_of(owner * block, block), block), :]
        if slot < kept:
            keep_out[slot * block : (slot + 1) * block] = part
        else:
            send_out[(slot - kept) * block : (slot - kept + 1) * block] = part


def grad_body(n_seq, n_dp, factor, info, r0, r1, grad, keep_out, send_out, total):
    half = r0.shape[0]
    total[...] = (
        dot(r0[...], grad[:half], (0, 0)) + dot(r1[...], grad[half:], (0, 0))
    ) * factor
    split_rows(info, n_seq, n_dp, total, keep_out, send_out)


def grad_out_body(rows, n_seq, n_dp, factor, info, mine, other, cot, keep_out, send_out, total):
    half = mine.shape[1]
    core = info[2]
    for array, at in ((mine[...], core), (across(other, rows), 1 - core)):
        total[pl.ds(pl.multiple_of(at * half, half), half), :] = (
            dot(array.astype(BF16), cot[...], (0, 0)) * factor
        )
    split_rows(info, n_seq, n_dp, total, keep_out, send_out)


def attended_body(rows, info, mine, other, w_o, out):
    half = mine.shape[1]
    core = info[2]
    total = None
    for array, at in ((mine[:rows], core), (other[rows : 2 * rows], 1 - core)):
        weight = w_o[pl.ds(pl.multiple_of(at * half, half), half), :]
        part = dot(array.astype(BF16), weight)
        total = part if total is None else total + part
    out[...] = total.astype(BF16)


def tokens_body(rows, info, dq, dk, dv, w_q, w_k, w_v, mine_out, other_out):
    total = dot(dq[: 2 * rows], w_q[...], (1, 1))
    total = total + dot(dk[: 2 * rows], w_k[...], (1, 1))
    total = total + dot(dv[: 2 * rows], w_v[...], (1, 1))
    mine_out[...] = total[:rows]
    other_out[...] = total[rows:]


def assemble_body(width, info, *refs):
    out = refs[-1]
    block = refs[0].shape[1]
    for at, ref in enumerate(refs[:-1]):
        tensor, piece = at // PIECES, at % PIECES
        source = jnp.bitwise_xor(info[0], piece)
        column = tensor * width + (source % 2) * (width // 2) + (source // 2 % 2) * block
        out[:, pl.ds(pl.multiple_of(column, block), block)] = ref[...]


def partners(count, bit):
    return [(i, i ^ bit) for i in range(count)]


def local(tokens, w_query, w_key, w_value, w_output, out_cotangent):
    clip_count, rows, width = tokens.shape
    assert clip_count == 1
    size = width // H
    half = width // 2
    quarter = width // 4
    count = PIECES * rows
    n_seq, n_dp = lax.axis_size("seq"), lax.axis_size("dp")
    pairs = n_seq // PIECES
    seq, place = lax.axis_index("seq"), lax.axis_index("dp")
    core = seq % 2
    info = jnp.stack([seq, place, core, seq // 2 % 2]).astype(jnp.int32)
    swap = functools.partial(lax.ppermute, axis_name="seq")

    def gather(array):
        near = swap(array, perm=partners(n_seq, 1))
        far = swap(array, perm=partners(n_seq, 2))
        return near, far, swap(far, perm=partners(n_seq, 1))

    tok = tokens.reshape(rows, width)
    tok1, tok2, tok3 = gather(tok.astype(F32))
    cot = out_cotangent.reshape(rows, width)
    cot1, cot2, cot3 = gather(cot.astype(F32))

    columns = lambda i, info: (0, info[2])
    weights = [(w, (width, half), columns) for w in (w_query, w_key, w_value)]
    narrow = (2 * rows, half)
    outs = [(narrow, BF16)] * 3 + [((half, size), F32), ((2 * rows, width), BF16)]
    body = functools.partial(project_body, size)
    flops = 2 * 2 * rows * width * half * 3
    q0, k0, v0, state0, rows0 = call(body, info, outs, [tok, tok1, *weights], name="proj0", flops=flops)
    q1, k1, v1, state, rows1 = call(
        body, info, outs, [tok2, tok3, *weights, state0], name="proj1", flops=flops
    )

    def arriving(value, forward):
        total = None
        for d in range(1, pairs):
            shift = PIECES * d
            links = [(i, i + shift) for i in range(n_seq - shift)]
            if not forward:
                links = [(j, i) for i, j in links]
            got = swap(value, perm=links)
            total = got if total is None else total + got
        return total

    carried = arriving(state, True)
    wide = (count, half)
    q, k, v, attn, inner, back, cot_all = call(
        functools.partial(inside_body, rows, size),
        info,
        [(wide, BF16)] * 3
        + [((H // 2, count, count), BF16), (wide, F32), (wide, F32), ((count, width), BF16)],
        [q0, q1, k0, k1, v0, v1, cot, cot1, cot2, cot3, (w_output, (half, width), lambda i, info: (info[2], 0))],
        name="inside",
        flops=2 * count * width * half + 4 * 4 * count * count * size,
    )
    mixed, stats = call(
        functools.partial(stats_body, size),
        info,
        [(wide, F32), ((count, 128), F32)],
        [q, carried, inner, back],
        name="stats",
        flops=2 * count * half * size,
    )
    stats_other = swap(stats, perm=partners(n_seq, 1))
    normed, d_mixed, own_back = call(
        functools.partial(norm_body, rows, size, width),
        info,
        [(wide, F32), (wide, BF16), ((half, size), F32)],
        [q, mixed, back, stats, stats_other],
        name="norm",
        flops=2 * count * half * size,
    )
    later = arriving(own_back, False)
    normed_other = swap(normed, perm=partners(n_seq, 1))
    dq, dk_inner, dv_inner = call(
        functools.partial(back_body, rows, size),
        info,
        [(wide, BF16), (wide, F32), (wide, F32)],
        [q, k, v, d_mixed, attn, carried],
        name="back",
        flops=8 * 4 * count * count * size,
    )

    factor = 1.0 / math.sqrt(clip_count * n_dp * rows * n_seq)
    chunk = [((width // 2, quarter), F32)] * 2
    scratch = [pltpu.VMEM((width, quarter), F32)]
    grad_flops = 2 * count * width * quarter

    def reduce_rows(keep, send):
        bit = n_dp // 2
        while bit:
            keep = keep + lax.ppermute(send, "dp", partners(n_dp, bit))
            bit //= 2
            if bit:
                middle = keep.shape[0] // 2
                keep, send = keep[:middle], keep[middle:]
        bit = n_seq // 2
        while bit >= PIECES:
            middle = keep.shape[0] // 2
            keep = keep[:middle] + swap(keep[middle:], perm=partners(n_seq, bit))
            bit //= 2
        block = keep.shape[0] // PIECES
        parts = [keep[i * block : (i + 1) * block] for i in range(PIECES)]
        return parts[:1] + [swap(parts[i], perm=partners(n_seq, i)) for i in range(1, PIECES)]

    def weight_grad(grad, name):
        return call(
            functools.partial(grad_body, n_seq, n_dp, factor),
            info,
            chunk,
            [rows0, rows1, (grad, (count, quarter), lambda i, info: (0, info[3]))],
            scratch,
            name=name,
            flops=grad_flops,
        )

    parts_q = reduce_rows(*weight_grad(dq, "grad_q"))
    parts_o = reduce_rows(
        *call(
            functools.partial(grad_out_body, rows, n_seq, n_dp, factor),
            info,
            chunk,
            [normed, normed_other, (cot_all, (count, quarter), lambda i, info: (0, 2 * info[2] + info[3]))],
            scratch,
            name="grad_o",
            flops=grad_flops,
        )
    )
    (attended,) = call(
        functools.partial(attended_body, rows),
        info,
        [((rows, width), BF16)],
        [normed, normed_other, w_output],
        name="attended",
        flops=2 * rows * width * width,
    )
    dk, dv = call(
        functools.partial(finish_body, size),
        info,
        [(wide, BF16)] * 2,
        [k, v, later, dk_inner, dv_inner],
        name="finish",
        flops=4 * count * half * size,
    )
    parts_k = reduce_rows(*weight_grad(dk, "grad_k"))
    parts_v = reduce_rows(*weight_grad(dv, "grad_v"))
    mine, other = call(
        functools.partial(tokens_body, rows),
        info,
        [((rows, width), F32)] * 2,
        [dq, dk, dv, *weights],
        name="d_tokens",
        flops=6 * 2 * rows * width * half,
    )
    d_tokens = (mine + swap(other, perm=partners(n_seq, 1))).astype(BF16)
    (grads,) = call(
        functools.partial(assemble_body, width),
        info,
        [((width // (n_seq * n_dp), 4 * width), F32)],
        parts_q + parts_k + parts_v + parts_o,
        name="assemble",
    )
    return (
        attended.reshape(tokens.shape),
        d_tokens.reshape(tokens.shape),
        grads,
    )


def solution(mesh):
    return jax.shard_map(
        local,
        mesh=mesh,
        in_specs=(
            P(("groups", "dp"), "seq", None),
            P(),
            P(),
            P(),
            P(),
            P(("groups", "dp"), "seq", None),
        ),
        out_specs=(
            P(("groups", "dp"), "seq", None),
            P(("groups", "dp"), "seq", None),
            P(("groups", "seq", "dp"), None),
        ),
        check_vma=False,
    )
```

time: 360 us -> 142 us (0.39)
  waiting for transfers between devices: 249 us -> 57.2 us
  starting transfers between devices: 0.12 us -> 45.8 us
  matrix products: 32.2 us -> 0 us
  other arithmetic: 31.3 us -> 4.84 us
  Pallas kernels: 0 us -> 22.1 us
  local copies, waits for them, and re-layouts: 30.9 us -> 10.6 us
  between operations: 14.1 us -> 0.91 us
    unnamed x4 -> x0, waiting for transfers between devices: 170 us -> none
    all_gather x2 -> x0, waiting for transfers between devices: 79.1 us -> none  [entering(): everything = lax.all_gather(value, axis)]
    ppermute x0 -> x31, waiting for transfers between devices: none -> 57.2 us  [the longest x4 21.8 us: reduce_rows(): keep = keep + lax.ppermute(send, 'dp', partners(n_dp, bit))]
    ppermute x0 -> x31, starting transfers between devices: none -> 45.8 us  [the longest x12 19.4 us: reduce_rows(): swap(parts[i], perm=partners(n_seq, i))]
    dot_general x22 -> x0, matrix products: 32.2 us -> none  [the longest x3 5.46 us: project(): jnp.dot(flattened, weight, preferred_element_type=jnp.float32)]
    pallas_call x0 -> x14, Pallas kernels: none -> 22.1 us  [call(): pl.pallas_call(body, name=name, out_shape=shapes, grid_spec=pltpu.Prefetc...]
    select_n x16 -> x0, other arithmetic: 19.7 us -> none  [hop(): return jnp.where(reached, new, before)]
    unnamed x52 -> x26, local copies, waits for them, and re-layouts: 28.4 us -> 10.5 us
  transfers between devices with their start and end apart: 3 -> 31, of which waited for: 3 -> 11; matrix products, arithmetic and copies ran while one was open for 6% -> 2% of each run, Pallas kernels for 0% -> 13%
where the time goes in v1:
time: 142 us; the launch traced here: 141 us
  waiting for transfers between devices  57.2 us (40%)
  starting transfers between devices  45.8 us (32%)
  Pallas kernels  22.1 us (16%)
  local copies, waits for them, and re-layouts  10.6 us (7%)
  other arithmetic  4.84 us (3%)
    pallas_call x14, Pallas kernels, call(): pl.pallas_call(body, name=name, out_shape=shapes, grid_spec=pltpu.Prefetc...  22.1 us
    ppermute x4, waiting for transfers between devices, reduce_rows(): keep = keep + lax.ppermute(send, 'dp', partners(n_dp, bit))  21.8 us
    ppermute x2, waiting for transfers between devices, gather(): far = swap(array, perm=partners(n_seq, 2))  21 us
    ppermute x12, starting transfers between devices, reduce_rows(): swap(parts[i], perm=partners(n_seq, i))  19.4 us
    ppermute x4, starting transfers between devices, reduce_rows(): keep = keep[:middle] + swap(keep[middle:], perm=partners(n_seq, bit))  10.8 us
    unnamed x26, local copies, waits for them, and re-layouts  10.5 us
    ppermute x4, waiting for transfers between devices, reduce_rows(): keep = keep[:middle] + swap(keep[middle:], perm=partners(n_seq, bit))  7.27 us
    ppermute x2, starting transfers between devices, arriving(): got = swap(value, perm=links)  6.15 us
  transfers between devices with their start and end apart: 31, of which 11 were waited for; matrix products, arithmetic and copies ran while one was open for 2% of the time, Pallas kernels for 13%

profile of v1, /device:TPU:0, one launch (start us, length us, event | category | flops | bytes accessed | tf_op | source)
XLA Modules:
  0.0 141.5 jit_solution(333674368074211992)
XLA Ops:
  0.6 1.8 %bitcast_convert_fusion.1 = f32[128,1024]{1,0:T(8,128)} fusion(bf16[1,128,1024]{2,1,0:T(8,128)(2,1)} %param.6), kind=kLoop, calls=%fused_computation.8 | loop fusion | flops 131072 | bytes 786432 | tf_op jit(solution)/shard_map/convert_element_type | solution.py:242
  2.4 3.0 %collective-permute-start.1 = (f32[128,1024]{1,0:T(8,128)}, f32[128,1024]{1,0:T(8,128)S(1)}, u32[]{:S(2)}, u32[]{:S(2)}) collective-permute-start(f32[128,1024]{1,0:T(8,128)} %bitcast_convert_fusion.1), channel_id=1, source_target_pairs={{0,4},{2,6},{4,0},{6,2},{8,12},{10,14},{12,8},{14,10},{1,5},{3,7},... | collective-permute-start | bytes 1572872 | tf_op jit(solution)/shard_map/ppermute | solution.py:238
  5.4 1.8 %bitcast_convert_fusion = f32[128,1024]{1,0:T(8,128)} fusion(bf16[1,128,1024]{2,1,0:T(8,128)(2,1)} %param.11), kind=kLoop, calls=%fused_computation.7 | loop fusion | flops 131072 | bytes 786432 | tf_op jit(solution)/shard_map/convert_element_type | solution.py:244
  7.3 11.1 %collective-permute-done.1.first = f32[128,1024]{1,0:T(8,128)S(1)} collective-permute-done((f32[128,1024]{1,0:T(8,128)}, f32[128,1024]{1,0:T(8,128)S(1)}, u32[]{:S(2)}, u32[]{:S(2)}) %collective-permute-start.1) | collective-permute-done | bytes 524320 | tf_op jit(solution)/shard_map/ppermute | solution.py:238
  18.9 9.9 %collective-permute-done.4.c2 = f32[128,1024]{1,0:T(8,128)S(1)} collective-permute-done((f32[128,1024]{1,0:T(8,128)}, f32[128,1024]{1,0:T(8,128)S(1)}, u32[]{:S(2)}, u32[]{:S(2)}) %collective-permute-start.4) | collective-permute-done | bytes 524320 | tf_op jit(solution)/shard_map/ppermute | solution.py:238
  28.9 1.6 %copy-done = bf16[1024,1024]{1,0:T(8,128)(2,1)S(1)} copy-done((bf16[1024,1024]{1,0:T(8,128)(2,1)S(1)}, bf16[1024,1024]{1,0:T(8,128)(2,1)}, u32[]{:S(2)}) %copy-start) | copy-done | bytes 2097176
  30.5 1.6 %copy-done.2 = bf16[1024,1024]{1,0:T(8,128)(2,1)S(1)} copy-done((bf16[1024,1024]{1,0:T(8,128)(2,1)S(1)}, bf16[1024,1024]{1,0:T(8,128)(2,1)}, u32[]{:S(2)}) %copy-start.2) | copy-done | bytes 2097176
  32.1 1.6 %copy-done.4 = bf16[1024,1024]{1,0:T(8,128)(2,1)S(1)} copy-done((bf16[1024,1024]{1,0:T(8,128)(2,1)S(1)}, bf16[1024,1024]{1,0:T(8,128)(2,1)}, u32[]{:S(2)}) %copy-start.4) | copy-done | bytes 2097176
  33.7 0.9 copy-done.7
  34.6 1.8 %proj0.1 = (bf16[256,512]{1,0:T(8,128)(2,1)S(1)}, bf16[256,512]{1,0:T(8,128)(2,1)S(1)}, bf16[256,512]{1,0:T(8,128)(2,1)S(1)}, f32[512,128]{1,0:T(8,128)S(1)}, bf16[256,1024]{1,0:T(8,128)(2,1)S(1)}) custom-call(s32[4]{0:T(128)S(1)} %pad_add_fusion.info, bf16[128,1024]{1,0:T(8,128)(2,1)S(1)} %bitcast.11, f32[128,1024]{1,0:T(8,128)S(1)} %collective-permute-done.second, ...), custom_call_target="tpu_custom_call" | custom-call | flops 805306368 | bytes 5505024 | tf_op jit(solution)/shard_map/proj0/pallas_call | solution.py:32
  37.5 1.8 %proj1.1 = (bf16[256,512]{1,0:T(8,128)(2,1)S(1)}, bf16[256,512]{1,0:T(8,128)(2,1)S(1)}, bf16[256,512]{1,0:T(8,128)(2,1)S(1)}, f32[512,128]{1,0:T(8,128)S(1)}, bf16[256,1024]{1,0:T(8,128)(2,1)S(1)}) custom-call(s32[4]{0:T(128)S(1)} %pad_add_fusion.info, f32[128,1024]{1,0:T(8,128)S(1)} %collective-permute-done.1.first, ...), custom_call_target="tpu_custom_call" | custom-call | flops 805306368 | bytes 6029312 | tf_op jit(solution)/shard_map/proj1/pallas_call | solution.py:32
  39.3 4.7 %collective-permute-start.6 = (f32[512,128]{1,0:T(8,128)S(1)}, f32[512,128]{1,0:T(8,128)S(1)}, u32[]{:S(2)}, u32[]{:S(2)}) collective-permute-start(f32[512,128]{1,0:T(8,128)S(1)} %get-tuple-element.48), channel_id=1, source_target_pairs={{0,8},{2,10},{4,12},{6,14},{1,9},{3,11},{5,13},{7,15},{16,24},{18,... | collective-permute-start | bytes 786440 | tf_op jit(solution)/shard_map/ppermute | solution.py:264
  44.7 0.8 copy-done.11
  45.6 1.0 copy-done.10
  46.6 1.0 copy-done.12
  47.6 2.5 %inside.1 = (bf16[512,512]{1,0:T(8,128)(2,1)S(1)}, bf16[512,512]{1,0:T(8,128)(2,1)S(1)}, bf16[512,512]{1,0:T(8,128)(2,1)S(1)}, bf16[4,512,512]{2,1,0:T(8,128)(2,...) custom-call(s32[4]{0:T(128)S(1)} %pad_add_fusion.info, ...), custom_call_target="tpu_custom_call" | custom-call | flops 1073741824 | bytes 11272192 | tf_op jit(solution)/shard_map/inside/pallas_call | solution.py:32
  50.2 1.0 stats.1
  51.5 1.3 collective-permute-done.7.other
  52.8 1.4 norm.1
  54.1 1.5 %collective-permute-start.9 = (f32[512,128]{1,0:T(8,128)S(1)}, f32[512,128]{1,0:T(8,128)S(1)}, u32[]{:S(2)}, u32[]{:S(2)}) collective-permute-start(f32[512,128]{1,0:T(8,128)S(1)} %get-tuple-element.59), channel_id=1, source_target_pairs={{8,0},{10,2},{12,4},{14,6},{9,1},{11,3},{13,5},{15,7},{24,16},{26,... | collective-permute-start | bytes 786440 | tf_op jit(solution)/shard_map/ppermute | solution.py:264
  55.9 3.3 %back.1 = (bf16[512,512]{1,0:T(8,128)(2,1)S(1)}, f32[512,512]{1,0:T(8,128)S(1)}, f32[512,512]{1,0:T(8,128)S(1)}) custom-call(s32[4]{0:T(128)S(1)} %pad_add_fusion.info, bf16[512,512]{1,0:T(8,128)(2,1)S(1)} %get-tuple-element.47.q, bf16[512,512]{1,0:T(8,128)(2,1)S(1)} %get-tuple-element.54.k, bf16[512,512]{1,0:T(8,128)(2,1)S(1)} %get-tuple-element.55.v, ...), custom_call_target="tpu_custom_call" | custom-call | flops 1073741824 | bytes 7077888 | tf_op jit(solution)/shard_map/back/pallas_call | solution.py:32
  59.2 1.1 grad_q.1
  60.4 1.6 %collective-permute-start.11 = (f32[512,256]{1,0:T(8,128)S(1)}, f32[512,256]{1,0:T(8,128)S(1)}, u32[]{:S(2)}, u32[]{:S(2)}) collective-permute-start(f32[512,256]{1,0:T(8,128)S(1)} %get-tuple-element.69), channel_id=1, source_target_pairs={{0,1},{1,0},{2,3},{3,2},{4,5},{5,4},{6,7},{7,6},{8,9},{9,8},{10,11... | collective-permute-start | bytes 1572872 | tf_op jit(solution)/shard_map/ppermute | solution.py:315
  61.9 3.5 %collective-permute-done.9.later = f32[512,128]{1,0:T(8,128)S(1)} collective-permute-done((f32[512,128]{1,0:T(8,128)S(1)}, f32[512,128]{1,0:T(8,128)S(1)}, u32[]{:S(2)}, u32[]{:S(2)}) %collective-permute-start.9) | collective-permute-done | bytes 262176 | tf_op jit(solution)/shard_map/ppermute | solution.py:264
  65.5 1.0 finish.1
  66.4 1.1 grad_v.1
  67.6 1.6 %collective-permute-start.21 = (f32[512,256]{1,0:T(8,128)S(1)}, f32[512,256]{1,0:T(8,128)S(1)}, u32[]{:S(2)}, u32[]{:S(2)}) collective-permute-start(f32[512,256]{1,0:T(8,128)S(1)} %get-tuple-element.73), channel_id=1, source_target_pairs={{0,1},{1,0},{2,3},{3,2},{4,5},{5,4},{6,7},{7,6},{8,9},{9,8},{10,11... | collective-permute-start | bytes 1572872 | tf_op jit(solution)/shard_map/ppermute | solution.py:315
  69.1 1.1 grad_k.1
  70.9 4.3 %collective-permute-done.11 = f32[512,256]{1,0:T(8,128)S(1)} collective-permute-done((f32[512,256]{1,0:T(8,128)S(1)}, f32[512,256]{1,0:T(8,128)S(1)}, u32[]{:S(2)}, u32[]{:S(2)}) %collective-permute-start.11) | collective-permute-done | bytes 524320 | tf_op jit(solution)/shard_map/ppermute | solution.py:315
  75.3 3.4 %collective-permute-start.12 = (f32[256,256]{1,0:T(8,128)S(1)}, f32[256,256]{1,0:T(8,128)S(1)}, u32[]{:S(2)}, u32[]{:S(2)}) collective-permute-start(f32[256,256]{1,0:T(8,128)S(1)} %slice.97), channel_id=1, source_target_pairs={{0,8},{2,10},{4,12},{6,14},{8,0},{10,2},{12,4},{14,6},{1,9},{3,11}... | collective-permute-start | bytes 786440 | tf_op jit(solution)/shard_map/ppermute | solution.py:323
  78.7 1.6 %d_tokens.1 = (f32[128,1024]{1,0:T(8,128)S(1)}, f32[128,1024]{1,0:T(8,128)S(1)}) custom-call(s32[4]{0:T(128)S(1)} %pad_add_fusion.info, bf16[512,512]{1,0:T(8,128)(2,1)S(1)} %get-tuple-element.58.dq.grad, bf16[512,512]{1,0:T(8,128)(2,1)S(1)} %get-tuple-element.62.dk.grad, bf16[512,512]{1,0:T(8,128)(2,1)S(1)} %get-tuple-element.63.dv.grad, ...), custom_call_target="tpu_custom_call" | custom-call | flops 805306368 | bytes 5767168 | tf_op jit(solution)/shard_map/d_tokens/pallas_call | solution.py:32
  80.3 6.1 %collective-permute-done.21 = f32[512,256]{1,0:T(8,128)S(1)} collective-permute-done((f32[512,256]{1,0:T(8,128)S(1)}, f32[512,256]{1,0:T(8,128)S(1)}, u32[]{:S(2)}, u32[]{:S(2)}) %collective-permute-start.21) | collective-permute-done | bytes 524320 | tf_op jit(solution)/shard_map/ppermute | solution.py:315
  86.5 3.4 %collective-permute-start.22 = (f32[256,256]{1,0:T(8,128)S(1)}, f32[256,256]{1,0:T(8,128)S(1)}, u32[]{:S(2)}, u32[]{:S(2)}) collective-permute-start(f32[256,256]{1,0:T(8,128)S(1)} %slice.109), channel_id=1, source_target_pairs={{0,8},{2,10},{4,12},{6,14},{8,0},{10,2},{12,4},{14,6},{1,9},{3,11}... | collective-permute-start | bytes 786440 | tf_op jit(solution)/shard_map/ppermute | solution.py:323
  90.0 7.1 %collective-permute-done.16 = f32[512,256]{1,0:T(8,128)S(1)} collective-permute-done((f32[512,256]{1,0:T(8,128)S(1)}, f32[512,256]{1,0:T(8,128)S(1)}, u32[]{:S(2)}, u32[]{:S(2)}) %collective-permute-start.16) | collective-permute-done | bytes 524320 | tf_op jit(solution)/shard_map/ppermute | solution.py:315
  97.1 3.6 %collective-permute-start.17 = (f32[256,256]{1,0:T(8,128)S(1)}, f32[256,256]{1,0:T(8,128)S(1)}, u32[]{:S(2)}, u32[]{:S(2)}) collective-permute-start(f32[256,256]{1,0:T(8,128)S(1)} %slice.103), channel_id=1, source_target_pairs={{0,8},{2,10},{4,12},{6,14},{8,0},{10,2},{12,4},{14,6},{1,9},{3,11}... | collective-permute-start | bytes 786440 | tf_op jit(solution)/shard_map/ppermute | solution.py:323
  100.8 1.1 grad_o.1
  101.9 1.6 %collective-permute-start.26 = (f32[512,256]{1,0:T(8,128)S(1)}, f32[512,256]{1,0:T(8,128)S(1)}, u32[]{:S(2)}, u32[]{:S(2)}) collective-permute-start(f32[512,256]{1,0:T(8,128)S(1)} %get-tuple-element.76), channel_id=1, source_target_pairs={{0,1},{1,0},{2,3},{3,2},{4,5},{5,4},{6,7},{7,6},{8,9},{9,8},{10,11... | collective-permute-start | bytes 1572872 | tf_op jit(solution)/shard_map/ppermute | solution.py:315
  103.4 5.9 %collective-permute-start.15 = (f32[64,256]{1,0:T(8,128)S(1)}, f32[64,256]{1,0:T(8,128)S(1)}, u32[]{:S(2)}, u32[]{:S(2)}) collective-permute-start(f32[64,256]{1,0:T(8,128)S(1)} %get-tuple-element.89), channel_id=1, source_target_pairs={{0,6},{2,4},{4,2},{6,0},{8,14},{10,12},{12,10},{14,8},{1,7},{3,5},... | collective-permute-start | bytes 196616 | tf_op jit(solution)/shard_map/ppermute | solution.py:327
  109.3 1.3 collective-permute-start.14
  110.9 4.3 %collective-permute-done.26 = f32[512,256]{1,0:T(8,128)S(1)} collective-permute-done((f32[512,256]{1,0:T(8,128)S(1)}, f32[512,256]{1,0:T(8,128)S(1)}, u32[]{:S(2)}, u32[]{:S(2)}) %collective-permute-start.26) | collective-permute-done | bytes 524320 | tf_op jit(solution)/shard_map/ppermute | solution.py:315
  115.7 7.3 %collective-permute-done.27 = f32[256,256]{1,0:T(8,128)S(1)} collective-permute-done((f32[256,256]{1,0:T(8,128)S(1)}, f32[256,256]{1,0:T(8,128)S(1)}, u32[]{:S(2)}, u32[]{:S(2)}) %collective-permute-start.27) | collective-permute-done | bytes 262176 | tf_op jit(solution)/shard_map/ppermute | solution.py:323
  123.0 4.2 %collective-permute-start.25 = (f32[64,256]{1,0:T(8,128)S(1)}, f32[64,256]{1,0:T(8,128)S(1)}, u32[]{:S(2)}, u32[]{:S(2)}) collective-permute-start(f32[64,256]{1,0:T(8,128)S(1)} %get-tuple-element.81), channel_id=1, source_target_pairs={{0,6},{2,4},{4,2},{6,0},{8,14},{10,12},{12,10},{14,8},{1,7},{3,5},... | collective-permute-start | bytes 196616 | tf_op jit(solution)/shard_map/ppermute | solution.py:327
  127.3 3.4 %collective-permute-start.24 = (f32[64,256]{1,0:T(8,128)S(1)}, f32[64,256]{1,0:T(8,128)S(1)}, u32[]{:S(2)}, u32[]{:S(2)}) collective-permute-start(f32[64,256]{1,0:T(8,128)S(1)} %get-tuple-element.82), channel_id=1, source_target_pairs={{0,4},{2,6},{4,0},{6,2},{8,12},{10,14},{12,8},{14,10},{1,5},{3,7},... | collective-permute-start | bytes 196616 | tf_op jit(solution)/shard_map/ppermute | solution.py:327
  130.9 1.3 collective-permute-start.20
  133.6 1.7 %collective-permute-start.30 = (f32[64,256]{1,0:T(8,128)S(1)}, f32[64,256]{1,0:T(8,128)S(1)}, u32[]{:S(2)}, u32[]{:S(2)}) collective-permute-start(f32[64,256]{1,0:T(8,128)S(1)} %get-tuple-element.77), channel_id=1, source_target_pairs={{0,6},{2,4},{4,2},{6,0},{8,14},{10,12},{12,10},{14,8},{1,7},{3,5},... | collective-permute-start | bytes 196616 | tf_op jit(solution)/shard_map/ppermute | solution.py:327
  136.6 1.7 %attended.1 = bf16[128,1024]{1,0:T(8,128)(2,1)} custom-call(s32[4]{0:T(128)S(1)} %pad_add_fusion.info, f32[512,512]{1,0:T(8,128)S(1)} %get-tuple-element.53.mine, f32[512,512]{1,0:T(8,128)S(1)} %collective-permute-done.8.other, bf16[1024,1024]{1,0:T(8,128)(2,1)S(1)} %copy-done.6), custom_call_target="tpu_custom_call" | custom-call | flops 268435456 | bytes 4456448 | tf_op jit(solution)/shard_map/attended/pallas_call | solution.py:32
  138.3 1.6 %collective-permute-done.29.refs_14_ = f32[64,256]{1,0:T(8,128)S(1)} collective-permute-done((f32[64,256]{1,0:T(8,128)S(1)}, f32[64,256]{1,0:T(8,128)S(1)}, u32[]{:S(2)}, u32[]{:S(2)}) %collective-permute-start.29) | collective-permute-done | bytes 65568 | tf_op jit(solution)/shard_map/ppermute | solution.py:327
  139.9 1.6 %assemble.1 = f32[64,4096]{1,0:T(8,128)} custom-call(s32[4]{0:T(128)S(1)} %pad_add_fusion.info, f32[64,256]{1,0:T(8,128)S(1)} %get-tuple-element.92.refs_0_, f32[64,256]{1,0:T(8,128)S(1)} %collective-permute-done.13.refs_1_, f32[64,256]{1,0:T(8,128)S(1)} %collective-permute-done.14.refs_2_, f32[64,256]{1,0:T(8,128)S(1)} %collective-permute-done.15.refs_3_, ...), custom_call_target="tpu_custom_call" | custom-call | bytes 2097152 | tf_op jit(solution)/shard_map/assemble/pallas_call | solution.py:32
  (74 shorter events, 7.6 us)
Async XLA Ops:
  2.4 16.0 %collective-permute-start.1 = (f32[128,1024]{1,0:T(8,128)}, f32[128,1024]{1,0:T(8,128)S(1)}, u32[]{:S(2)}, u32[]{:S(2)}) collective-permute-start(f32[128,1024]{1,0:T(8,128)} %bitcast_convert_fusion.1), channel_id=1, source_target_pairs={{0,4},{2,6},{4,0},{6,2},{8,12},{10,14},{12,8},{14,10},{1,5},{3,7},... | collective-permute-start | bytes 1572872 | tf_op jit(solution)/shard_map/ppermute | solution.py:238
  7.3 21.6 %collective-permute-start.4 = (f32[128,1024]{1,0:T(8,128)}, f32[128,1024]{1,0:T(8,128)S(1)}, u32[]{:S(2)}, u32[]{:S(2)}) collective-permute-start(f32[128,1024]{1,0:T(8,128)} %bitcast_convert_fusion), channel_id=1, source_target_pairs={{0,4},{2,6},{4,0},{6,2},{8,12},{10,14},{12,8},{14,10},{1,5},{3,7},... | collective-permute-start | bytes 1572872 | tf_op jit(solution)/shard_map/ppermute | solution.py:238
  7.3 21.6 %collective-permute-start = (f32[128,1024]{1,0:T(8,128)}, f32[128,1024]{1,0:T(8,128)S(1)}, u32[]{:S(2)}, u32[]{:S(2)}) collective-permute-start(f32[128,1024]{1,0:T(8,128)} %bitcast_convert_fusion.1), channel_id=1, source_target_pairs={{0,2},{2,0},{4,6},{6,4},{8,10},{10,8},{12,14},{14,12},{1,3},{3,1},... | collective-permute-start | bytes 1572872 | tf_op jit(solution)/shard_map/ppermute | solution.py:237
  18.4 18.0 %collective-permute-start.2 = (f32[128,1024]{1,0:T(8,128)S(1)}, f32[128,1024]{1,0:T(8,128)S(1)}, u32[]{:S(2)}, u32[]{:S(2)}) collective-permute-start(f32[128,1024]{1,0:T(8,128)S(1)} %collective-permute-done.1.first), channel_id=1, source_target_pairs={{0,2},{2,0},{4,6},{6,4},{8,10},{10,8},{12,14},{14,12},{1,3},{3,1},... | collective-permute-start | bytes 1572872 | tf_op jit(solution)/shard_map/ppermute | solution.py:239
  18.4 25.5 %collective-permute-start.3 = (f32[128,1024]{1,0:T(8,128)}, f32[128,1024]{1,0:T(8,128)S(1)}, u32[]{:S(2)}, u32[]{:S(2)}) collective-permute-start(f32[128,1024]{1,0:T(8,128)} %bitcast_convert_fusion), channel_id=1, source_target_pairs={{0,2},{2,0},{4,6},{6,4},{8,10},{10,8},{12,14},{14,12},{1,3},{3,1},... | collective-permute-start | bytes 1572872 | tf_op jit(solution)/shard_map/ppermute | solution.py:237
  28.8 15.9 %collective-permute-start.5 = (f32[128,1024]{1,0:T(8,128)S(1)}, f32[128,1024]{1,0:T(8,128)S(1)}, u32[]{:S(2)}, u32[]{:S(2)}) collective-permute-start(f32[128,1024]{1,0:T(8,128)S(1)} %collective-permute-done.4.c2), channel_id=1, source_target_pairs={{0,2},{2,0},{4,6},{6,4},{8,10},{10,8},{12,14},{14,12},{1,3},{3,1},... | collective-permute-start | bytes 1572872 | tf_op jit(solution)/shard_map/ppermute | solution.py:239
  28.9 1.6 %copy-start = (bf16[1024,1024]{1,0:T(8,128)(2,1)S(1)}, bf16[1024,1024]{1,0:T(8,128)(2,1)}, u32[]{:S(2)}) copy-start(bf16[1024,1024]{1,0:T(8,128)(2,1)} %w_q.5) | copy-start | bytes 6291460
  30.5 1.6 %copy-start.2 = (bf16[1024,1024]{1,0:T(8,128)(2,1)S(1)}, bf16[1024,1024]{1,0:T(8,128)(2,1)}, u32[]{:S(2)}) copy-start(bf16[1024,1024]{1,0:T(8,128)(2,1)} %w_k.5) | copy-start | bytes 6291460
  32.1 1.6 %copy-start.4 = (bf16[1024,1024]{1,0:T(8,128)(2,1)S(1)}, bf16[1024,1024]{1,0:T(8,128)(2,1)}, u32[]{:S(2)}) copy-start(bf16[1024,1024]{1,0:T(8,128)(2,1)} %w_v.5) | copy-start | bytes 6291460
  33.7 0.9 copy-start.7
  34.6 1.8 %copy-start.1 = (bf16[1024,1024]{1,0:T(8,128)(2,1)S(1)}, bf16[1024,1024]{1,0:T(8,128)(2,1)}, u32[]{:S(2)}) copy-start(bf16[1024,1024]{1,0:T(8,128)(2,1)} %w_q.5) | copy-start | bytes 6291460
  34.6 2.2 %copy-start.3 = (bf16[1024,1024]{1,0:T(8,128)(2,1)S(1)}, bf16[1024,1024]{1,0:T(8,128)(2,1)}, u32[]{:S(2)}) copy-start(bf16[1024,1024]{1,0:T(8,128)(2,1)} %w_k.5) | copy-start | bytes 6291460
  34.6 2.9 %copy-start.5 = (bf16[1024,1024]{1,0:T(8,128)(2,1)S(1)}, bf16[1024,1024]{1,0:T(8,128)(2,1)}, u32[]{:S(2)}) copy-start(bf16[1024,1024]{1,0:T(8,128)(2,1)} %w_v.5) | copy-start | bytes 6291460
  37.5 8.1 %copy-start.6 = (bf16[1024,1024]{1,0:T(8,128)(2,1)S(1)}, bf16[1024,1024]{1,0:T(8,128)(2,1)}, u32[]{:S(2)}) copy-start(bf16[1024,1024]{1,0:T(8,128)(2,1)} %w_o.3) | copy-start | bytes 6291460
  37.5 8.1 %copy-start.8 = (bf16[1,128,1024]{2,1,0:T(8,128)(2,1)S(1)}, bf16[1,128,1024]{2,1,0:T(8,128)(2,1)}, u32[]{:S(2)}) copy-start(bf16[1,128,1024]{2,1,0:T(8,128)(2,1)} %param.11) | copy-start | bytes 786436
  39.3 10.9 %collective-permute-start.6 = (f32[512,128]{1,0:T(8,128)S(1)}, f32[512,128]{1,0:T(8,128)S(1)}, u32[]{:S(2)}, u32[]{:S(2)}) collective-permute-start(f32[512,128]{1,0:T(8,128)S(1)} %get-tuple-element.48), channel_id=1, source_target_pairs={{0,8},{2,10},{4,12},{6,14},{1,9},{3,11},{5,13},{7,15},{16,24},{18,... | collective-permute-start | bytes 786440 | tf_op jit(solution)/shard_map/ppermute | solution.py:264
  43.9 0.8 copy-start.9
  44.7 0.8 copy-start.11
  45.6 1.0 copy-start.10
  46.6 1.0 copy-start.12
  51.2 1.6 %collective-permute-start.7 = (f32[512,128]{1,0:T(8,128)S(1)}, f32[512,128]{1,0:T(8,128)S(1)}, u32[]{:S(2)}, u32[]{:S(2)}) collective-permute-start(f32[512,128]{1,0:T(8,128)S(1)} %get-tuple-element.52.mine), channel_id=1, source_target_pairs={{0,2},{2,0},{4,6},{6,4},{8,10},{10,8},{12,14},{14,12},{1,3},{3,1},... | collective-permute-start | bytes 786440 | tf_op jit(solution)/shard_map/ppermute | solution.py:287
  54.1 11.3 %collective-permute-start.9 = (f32[512,128]{1,0:T(8,128)S(1)}, f32[512,128]{1,0:T(8,128)S(1)}, u32[]{:S(2)}, u32[]{:S(2)}) collective-permute-start(f32[512,128]{1,0:T(8,128)S(1)} %get-tuple-element.59), channel_id=1, source_target_pairs={{8,0},{10,2},{12,4},{14,6},{9,1},{11,3},{13,5},{15,7},{24,16},{26,... | collective-permute-start | bytes 786440 | tf_op jit(solution)/shard_map/ppermute | solution.py:264
  55.6 45.1 %collective-permute-start.8 = (f32[512,512]{1,0:T(8,128)S(1)}, f32[512,512]{1,0:T(8,128)S(1)}, u32[]{:S(2)}, u32[]{:S(2)}) collective-permute-start(f32[512,512]{1,0:T(8,128)S(1)} %get-tuple-element.53.mine), channel_id=1, source_target_pairs={{0,2},{2,0},{4,6},{6,4},{8,10},{10,8},{12,14},{14,12},{1,3},{3,1},... | collective-permute-start | bytes 3145736 | tf_op jit(solution)/shard_map/ppermute | solution.py:297
  60.4 14.8 %collective-permute-start.11 = (f32[512,256]{1,0:T(8,128)S(1)}, f32[512,256]{1,0:T(8,128)S(1)}, u32[]{:S(2)}, u32[]{:S(2)}) collective-permute-start(f32[512,256]{1,0:T(8,128)S(1)} %get-tuple-element.69), channel_id=1, source_target_pairs={{0,1},{1,0},{2,3},{3,2},{4,5},{5,4},{6,7},{7,6},{8,9},{9,8},{10,11... | collective-permute-start | bytes 1572872 | tf_op jit(solution)/shard_map/ppermute | solution.py:315
  67.6 18.9 %collective-permute-start.21 = (f32[512,256]{1,0:T(8,128)S(1)}, f32[512,256]{1,0:T(8,128)S(1)}, u32[]{:S(2)}, u32[]{:S(2)}) collective-permute-start(f32[512,256]{1,0:T(8,128)S(1)} %get-tuple-element.73), channel_id=1, source_target_pairs={{0,1},{1,0},{2,3},{3,2},{4,5},{5,4},{6,7},{7,6},{8,9},{9,8},{10,11... | collective-permute-start | bytes 1572872 | tf_op jit(solution)/shard_map/ppermute | solution.py:315
  70.3 26.8 %collective-permute-start.16 = (f32[512,256]{1,0:T(8,128)S(1)}, f32[512,256]{1,0:T(8,128)S(1)}, u32[]{:S(2)}, u32[]{:S(2)}) collective-permute-start(f32[512,256]{1,0:T(8,128)S(1)} %get-tuple-element.71), channel_id=1, source_target_pairs={{0,1},{1,0},{2,3},{3,2},{4,5},{5,4},{6,7},{7,6},{8,9},{9,8},{10,11... | collective-permute-start | bytes 1572872 | tf_op jit(solution)/shard_map/ppermute | solution.py:315
  75.3 14.6 %collective-permute-start.12 = (f32[256,256]{1,0:T(8,128)S(1)}, f32[256,256]{1,0:T(8,128)S(1)}, u32[]{:S(2)}, u32[]{:S(2)}) collective-permute-start(f32[256,256]{1,0:T(8,128)S(1)} %slice.97), channel_id=1, source_target_pairs={{0,8},{2,10},{4,12},{6,14},{8,0},{10,2},{12,4},{14,6},{1,9},{3,11}... | collective-permute-start | bytes 786440 | tf_op jit(solution)/shard_map/ppermute | solution.py:323
  80.2 47.0 %collective-permute-start.10 = (f32[128,1024]{1,0:T(8,128)S(1)}, f32[128,1024]{1,0:T(8,128)S(1)}, u32[]{:S(2)}, u32[]{:S(2)}) collective-permute-start(f32[128,1024]{1,0:T(8,128)S(1)} %get-tuple-element.65), channel_id=1, source_target_pairs={{0,2},{2,0},{4,6},{6,4},{8,10},{10,8},{12,14},{14,12},{1,3},{3,1},... | collective-permute-start | bytes 1572872 | tf_op jit(solution)/shard_map/ppermute | solution.py:378
  86.5 22.8 %collective-permute-start.22 = (f32[256,256]{1,0:T(8,128)S(1)}, f32[256,256]{1,0:T(8,128)S(1)}, u32[]{:S(2)}, u32[]{:S(2)}) collective-permute-start(f32[256,256]{1,0:T(8,128)S(1)} %slice.109), channel_id=1, source_target_pairs={{0,8},{2,10},{4,12},{6,14},{8,0},{10,2},{12,4},{14,6},{1,9},{3,11}... | collective-permute-start | bytes 786440 | tf_op jit(solution)/shard_map/ppermute | solution.py:323
  97.1 13.6 %collective-permute-start.17 = (f32[256,256]{1,0:T(8,128)S(1)}, f32[256,256]{1,0:T(8,128)S(1)}, u32[]{:S(2)}, u32[]{:S(2)}) collective-permute-start(f32[256,256]{1,0:T(8,128)S(1)} %slice.103), channel_id=1, source_target_pairs={{0,8},{2,10},{4,12},{6,14},{8,0},{10,2},{12,4},{14,6},{1,9},{3,11}... | collective-permute-start | bytes 786440 | tf_op jit(solution)/shard_map/ppermute | solution.py:323
  101.9 13.3 %collective-permute-start.26 = (f32[512,256]{1,0:T(8,128)S(1)}, f32[512,256]{1,0:T(8,128)S(1)}, u32[]{:S(2)}, u32[]{:S(2)}) collective-permute-start(f32[512,256]{1,0:T(8,128)S(1)} %get-tuple-element.76), channel_id=1, source_target_pairs={{0,1},{1,0},{2,3},{3,2},{4,5},{5,4},{6,7},{7,6},{8,9},{9,8},{10,11... | collective-permute-start | bytes 1572872 | tf_op jit(solution)/shard_map/ppermute | solution.py:315
  103.4 27.3 %collective-permute-start.15 = (f32[64,256]{1,0:T(8,128)S(1)}, f32[64,256]{1,0:T(8,128)S(1)}, u32[]{:S(2)}, u32[]{:S(2)}) collective-permute-start(f32[64,256]{1,0:T(8,128)S(1)} %get-tuple-element.89), channel_id=1, source_target_pairs={{0,6},{2,4},{4,2},{6,0},{8,14},{10,12},{12,10},{14,8},{1,7},{3,5},... | collective-permute-start | bytes 196616 | tf_op jit(solution)/shard_map/ppermute | solution.py:327
  109.3 21.6 %collective-permute-start.14 = (f32[64,256]{1,0:T(8,128)S(1)}, f32[64,256]{1,0:T(8,128)S(1)}, u32[]{:S(2)}, u32[]{:S(2)}) collective-permute-start(f32[64,256]{1,0:T(8,128)S(1)} %get-tuple-element.90), channel_id=1, source_target_pairs={{0,4},{2,6},{4,0},{6,2},{8,12},{10,14},{12,8},{14,10},{1,5},{3,7},... | collective-permute-start | bytes 196616 | tf_op jit(solution)/shard_map/ppermute | solution.py:327
  110.7 21.5 %collective-permute-start.13 = (f32[64,256]{1,0:T(8,128)S(1)}, f32[64,256]{1,0:T(8,128)S(1)}, u32[]{:S(2)}, u32[]{:S(2)}) collective-permute-start(f32[64,256]{1,0:T(8,128)S(1)} %get-tuple-element.91), channel_id=1, source_target_pairs={{0,2},{2,0},{4,6},{6,4},{8,10},{10,8},{12,14},{14,12},{1,3},{3,1},... | collective-permute-start | bytes 196616 | tf_op jit(solution)/shard_map/ppermute | solution.py:327
  115.3 7.7 %collective-permute-start.27 = (f32[256,256]{1,0:T(8,128)S(1)}, f32[256,256]{1,0:T(8,128)S(1)}, u32[]{:S(2)}, u32[]{:S(2)}) collective-permute-start(f32[256,256]{1,0:T(8,128)S(1)} %slice.115), channel_id=1, source_target_pairs={{0,8},{2,10},{4,12},{6,14},{8,0},{10,2},{12,4},{14,6},{1,9},{3,11}... | collective-permute-start | bytes 786440 | tf_op jit(solution)/shard_map/ppermute | solution.py:323
  123.0 10.0 %collective-permute-start.25 = (f32[64,256]{1,0:T(8,128)S(1)}, f32[64,256]{1,0:T(8,128)S(1)}, u32[]{:S(2)}, u32[]{:S(2)}) collective-permute-start(f32[64,256]{1,0:T(8,128)S(1)} %get-tuple-element.81), channel_id=1, source_target_pairs={{0,6},{2,4},{4,2},{6,0},{8,14},{10,12},{12,10},{14,8},{1,7},{3,5},... | collective-permute-start | bytes 196616 | tf_op jit(solution)/shard_map/ppermute | solution.py:327
  127.3 6.3 %collective-permute-start.24 = (f32[64,256]{1,0:T(8,128)S(1)}, f32[64,256]{1,0:T(8,128)S(1)}, u32[]{:S(2)}, u32[]{:S(2)}) collective-permute-start(f32[64,256]{1,0:T(8,128)S(1)} %get-tuple-element.82), channel_id=1, source_target_pairs={{0,4},{2,6},{4,0},{6,2},{8,12},{10,14},{12,8},{14,10},{1,5},{3,7},... | collective-permute-start | bytes 196616 | tf_op jit(solution)/shard_map/ppermute | solution.py:327
  130.7 4.6 %collective-permute-start.23 = (f32[64,256]{1,0:T(8,128)S(1)}, f32[64,256]{1,0:T(8,128)S(1)}, u32[]{:S(2)}, u32[]{:S(2)}) collective-permute-start(f32[64,256]{1,0:T(8,128)S(1)} %get-tuple-element.83), channel_id=1, source_target_pairs={{0,2},{2,0},{4,6},{6,4},{8,10},{10,8},{12,14},{14,12},{1,3},{3,1},... | collective-permute-start | bytes 196616 | tf_op jit(solution)/shard_map/ppermute | solution.py:327
  130.9 4.8 %collective-permute-start.20 = (f32[64,256]{1,0:T(8,128)S(1)}, f32[64,256]{1,0:T(8,128)S(1)}, u32[]{:S(2)}, u32[]{:S(2)}) collective-permute-start(f32[64,256]{1,0:T(8,128)S(1)} %get-tuple-element.85), channel_id=1, source_target_pairs={{0,6},{2,4},{4,2},{6,0},{8,14},{10,12},{12,10},{14,8},{1,7},{3,5},... | collective-permute-start | bytes 196616 | tf_op jit(solution)/shard_map/ppermute | solution.py:327
  132.3 6.0 %collective-permute-start.19 = (f32[64,256]{1,0:T(8,128)S(1)}, f32[64,256]{1,0:T(8,128)S(1)}, u32[]{:S(2)}, u32[]{:S(2)}) collective-permute-start(f32[64,256]{1,0:T(8,128)S(1)} %get-tuple-element.86), channel_id=1, source_target_pairs={{0,4},{2,6},{4,0},{6,2},{8,12},{10,14},{12,8},{14,10},{1,5},{3,7},... | collective-permute-start | bytes 196616 | tf_op jit(solution)/shard_map/ppermute | solution.py:327
  132.9 5.3 %collective-permute-start.18 = (f32[64,256]{1,0:T(8,128)S(1)}, f32[64,256]{1,0:T(8,128)S(1)}, u32[]{:S(2)}, u32[]{:S(2)}) collective-permute-start(f32[64,256]{1,0:T(8,128)S(1)} %get-tuple-element.87), channel_id=1, source_target_pairs={{0,2},{2,0},{4,6},{6,4},{8,10},{10,8},{12,14},{14,12},{1,3},{3,1},... | collective-permute-start | bytes 196616 | tf_op jit(solution)/shard_map/ppermute | solution.py:327
  133.6 4.7 %collective-permute-start.30 = (f32[64,256]{1,0:T(8,128)S(1)}, f32[64,256]{1,0:T(8,128)S(1)}, u32[]{:S(2)}, u32[]{:S(2)}) collective-permute-start(f32[64,256]{1,0:T(8,128)S(1)} %get-tuple-element.77), channel_id=1, source_target_pairs={{0,6},{2,4},{4,2},{6,0},{8,14},{10,12},{12,10},{14,8},{1,7},{3,5},... | collective-permute-start | bytes 196616 | tf_op jit(solution)/shard_map/ppermute | solution.py:327
  135.3 4.5 %collective-permute-start.29 = (f32[64,256]{1,0:T(8,128)S(1)}, f32[64,256]{1,0:T(8,128)S(1)}, u32[]{:S(2)}, u32[]{:S(2)}) collective-permute-start(f32[64,256]{1,0:T(8,128)S(1)} %get-tuple-element.78), channel_id=1, source_target_pairs={{0,4},{2,6},{4,0},{6,2},{8,12},{10,14},{12,8},{14,10},{1,5},{3,7},... | collective-permute-start | bytes 196616 | tf_op jit(solution)/shard_map/ppermute | solution.py:327
  135.7 4.2 %collective-permute-start.28 = (f32[64,256]{1,0:T(8,128)S(1)}, f32[64,256]{1,0:T(8,128)S(1)}, u32[]{:S(2)}, u32[]{:S(2)}) collective-permute-start(f32[64,256]{1,0:T(8,128)S(1)} %get-tuple-element.79), channel_id=1, source_target_pairs={{0,2},{2,0},{4,6},{6,4},{8,10},{10,8},{12,14},{14,12},{1,3},{3,1},... | collective-permute-start | bytes 196616 | tf_op jit(solution)/shard_map/ppermute | solution.py:327

commit v2 on v1

v2 whole, which is shorter than its diff:
```python
import functools
import math

import jax
import jax.numpy as jnp
from jax import lax
from jax.experimental import pallas as pl
from jax.experimental.pallas import tpu as pltpu
from jax.sharding import PartitionSpec as P

H = 8
LAG, WINDOW, AHEAD = 2.5, 2, 2
EPSILON = 1e-05
PIECES = 4
F32, BF16 = jnp.float32, jnp.bfloat16
WHOLE = pl.BlockSpec(memory_space=pltpu.VMEM)


def call(body, info, outs, ins, scratch=(), name=None, flops=0):
    arrays, specs, moved = [], [], 0
    for entry in ins:
        if isinstance(entry, tuple):
            array, block, index = entry
            arrays.append(array)
            specs.append(pl.BlockSpec(block, index))
            moved += math.prod(block) * array.dtype.itemsize
        else:
            arrays.append(entry)
            specs.append(WHOLE)
            moved += entry.size * entry.dtype.itemsize
    shapes = [jax.ShapeDtypeStruct(shape, dtype) for shape, dtype in outs]
    moved += sum(math.prod(shape) * jnp.dtype(dtype).itemsize for shape, dtype in outs)
    return pl.pallas_call(
        body,
        name=name,
        out_shape=shapes,
        grid_spec=pltpu.PrefetchScalarGridSpec(
            num_scalar_prefetch=1,
            grid=(1,),
            in_specs=specs,
            out_specs=[WHOLE] * len(shapes),
            scratch_shapes=list(scratch),
        ),
        compiler_params=pltpu.CompilerParams(vmem_limit_bytes=24 * 2**20),
        cost_estimate=pl.CostEstimate(flops=1, bytes_accessed=1, transcendentals=0),
    )(info, *arrays)


def dot(a, b, over=(1, 0)):
    return lax.dot_general(
        a, b, (((over[0],), (over[1],)), ((), ())), preferred_element_type=F32
    )


def head(array, h, size):
    return array[:, h * size : (h + 1) * size]


def causal(info_ref, rows, count):
    seq = info_ref[0]

    def position(dim):
        at = lax.broadcasted_iota(jnp.int32, (count, count), dim)
        piece = jnp.bitwise_xor(at // rows, seq)
        return piece * rows + at % rows

    return position(0) >= position(1)


def across(ref, rows):
    order = [piece ^ 1 for piece in range(PIECES)]
    return jnp.concatenate([ref[piece * rows : (piece + 1) * rows] for piece in order], axis=0)


def project_body(n_seq, size, info, first, second, w_q, w_k, w_v, *rest):
    if len(rest) == 6:
        before, q_out, k_out, v_out, state_out, rows_out = rest
    else:
        before = None
        q_out, k_out, v_out, state_out, rows_out = rest
    width = first.shape[1]
    rows = jnp.concatenate([first[...].astype(BF16), second[...].astype(BF16)], axis=0)
    block = 2 * width // n_seq
    for pair in range(n_seq // PIECES):
        at = pl.ds(pl.multiple_of((pair * 2 + info[3]) * block, block), block)
        for i, ref in enumerate((first, second)):
            count = ref.shape[0]
            rows_out[i * count : (i + 1) * count, pair * block : (pair + 1) * block] = ref[:, at].astype(BF16)
    q_out[...] = dot(rows, w_q[...]).astype(BF16)
    keys = dot(rows, w_k[...]).astype(BF16)
    k_out[...] = keys
    values = dot(rows, w_v[...]).astype(BF16)
    v_out[...] = values
    for h in range(keys.shape[1] // size):
        state = dot(head(keys, h, size), head(values, h, size), (0, 0))
        if before is not None:
            state = state + before[h * size : (h + 1) * size]
        state_out[h * size : (h + 1) * size] = state


def inside_body(rows, size, info, q0, q1, k0, k1, v0, v1, *outs):
    q_out, k_out, v_out, attn_out, mixed_out = outs
    q = jnp.concatenate([q0[...], q1[...]], axis=0)
    k = jnp.concatenate([k0[...], k1[...]], axis=0)
    v = jnp.concatenate([v0[...], v1[...]], axis=0)
    q_out[...], k_out[...], v_out[...] = q, k, v
    mask = causal(info, rows, q.shape[0])
    for h in range(q.shape[1] // size):
        scores = dot(head(q, h, size), head(k, h, size), (1, 1))
        attn = jnp.where(mask, scores, 0.0).astype(BF16)
        attn_out[h] = attn
        mixed_out[:, h * size : (h + 1) * size] = dot(attn, head(v, h, size))


def cotangent_body(info, c0, c1, c2, c3, w_o, cot_out, back_out):
    cot = jnp.concatenate([c[...].astype(BF16) for c in (c0, c1, c2, c3)], axis=0)
    cot_out[...] = cot
    back_out[...] = dot(cot, w_o[...], (1, 1))


def stats_body(size, info, q, carried, inner, back, mixed_out, stats_out):
    for h in range(q.shape[1] // size):
        state = carried[h * size : (h + 1) * size].astype(BF16)
        mixed_out[:, h * size : (h + 1) * size] = inner[:, h * size : (h + 1) * size] + dot(
            head(q, h, size), state
        )
    mixed = mixed_out[...]
    squares = jnp.sum(mixed * mixed, axis=1, keepdims=True)
    cross = jnp.sum(mixed * back[...], axis=1, keepdims=True)
    lane = lax.broadcasted_iota(jnp.int32, stats_out.shape, 1)
    stats_out[...] = jnp.where(lane == 0, squares, cross)


def norm_body(rows, size, width, info, q, mixed, back, mine, other, normed_out, d_out, state_out):
    total = mine[...] + across(other, rows)
    squares, cross = total[:, 0:1], total[:, 1:2]
    scale = jnp.sqrt(squares * (1.0 / width) + EPSILON)
    normed = mixed[...] / scale
    normed_out[...] = normed.astype(BF16).astype(F32)
    mean = cross / scale * (1.0 / width)
    d_mixed = ((back[...] - normed * mean) / scale).astype(BF16)
    d_out[...] = d_mixed
    for h in range(q.shape[1] // size):
        state_out[h * size : (h + 1) * size] = dot(head(q, h, size), head(d_mixed, h, size), (0, 0))


def back_query_body(rows, size, info, k, v, d_mixed, carried, dq_out, scores_out):
    mask = causal(info, rows, k.shape[0])
    for h in range(k.shape[1] // size):
        at = slice(h * size, (h + 1) * size)
        d_head = d_mixed[:, at]
        scores = dot(d_head, v[:, at], (1, 1))
        scores = jnp.where(mask, scores, 0.0).astype(BF16)
        state = carried[at].astype(BF16)
        scores_out[h] = scores
        dq_out[:, at] = (dot(scores, k[:, at]) + dot(d_head, state, (1, 1))).astype(BF16)


def back_rest_body(size, info, q, d_mixed, attn, scores, dk_out, dv_out):
    for h in range(q.shape[1] // size):
        at = slice(h * size, (h + 1) * size)
        dk_out[:, at] = dot(scores[h], q[:, at], (0, 0))
        dv_out[:, at] = dot(attn[h], d_mixed[:, at], (0, 0))


def finish_body(size, info, k, v, later, dk_in, dv_in, dk_out, dv_out):
    for h in range(k.shape[1] // size):
        at = slice(h * size, (h + 1) * size)
        state = later[at].astype(BF16)
        dk_out[:, at] = (dk_in[:, at] + dot(v[:, at], state, (1, 1))).astype(BF16)
        dv_out[:, at] = (dv_in[:, at] + dot(k[:, at], state)).astype(BF16)


def split_rows(info, pairs, n_dp, total, *outs):
    keep_outs, send_outs = outs[: len(outs) // 2], outs[len(outs) // 2 :]
    columns = keep_outs[0].shape[1]
    kept = keep_outs[0].shape[0]
    block = total.shape[0] // (pairs * 2 * n_dp)
    seq, place = info[0], info[1]
    for slot in range(pairs * 2 * n_dp):
        i, pair, core = slot // (2 * pairs), slot // 2 % pairs, slot % 2
        owner = jnp.bitwise_xor(seq // PIECES, pair) * 2 + jnp.bitwise_xor(seq % 2, core)
        owner = owner * n_dp + jnp.bitwise_xor(place, i)
        rows = pl.ds(pl.multiple_of(owner * block, block), block)
        at = slot * block
        targets = keep_outs if at < kept else send_outs
        at = at % kept
        for chunk, target in enumerate(targets):
            target[at : at + block] = total[rows, chunk * columns : (chunk + 1) * columns]


def grad_body(pairs, n_dp, factor, info, r0, r1, grad, *outs):
    outs, total = outs[:-1], outs[-1]
    half = r0.shape[0]
    total[...] = (
        dot(r0[...], grad[:half], (0, 0)) + dot(r1[...], grad[half:], (0, 0))
    ) * factor
    split_rows(info, pairs, n_dp, total, *outs)


def grad_out_body(rows, pairs, n_dp, factor, info, mine, other, cot, *outs):
    outs, total = outs[:-1], outs[-1]
    core, chip = info[2], info[3]
    block = 2 * mine.shape[1] // (2 * pairs)
    per_core = mine.shape[1] // block
    order = [piece ^ 1 for piece in range(PIECES)]
    for pair in range(pairs):
        index = pair * 2 + chip
        at = pl.ds(pl.multiple_of(index % per_core * block, block), block)
        is_mine = index // per_core == core
        parts = [
            jnp.where(is_mine, mine[p * rows : (p + 1) * rows, at], other[order[p] * rows : (order[p] + 1) * rows, at])
            for p in range(PIECES)
        ]
        left = jnp.concatenate(parts, axis=0).astype(BF16)
        total[pair * block : (pair + 1) * block] = dot(left, cot[...], (0, 0)) * factor
    split_rows(info, pairs, n_dp, total, *outs)


def attended_body(rows, info, mine, other, w_o, out):
    half = mine.shape[1]
    core = info[2]
    total = None
    for array, at in ((mine[:rows], core), (other[rows : 2 * rows], 1 - core)):
        weight = w_o[pl.ds(pl.multiple_of(at * half, half), half), :]
        part = dot(array.astype(BF16), weight)
        total = part if total is None else total + part
    out[...] = total.astype(BF16)


def tokens_body(rows, info, dq, dk, dv, w_q, w_k, w_v, mine_out, other_out):
    total = dot(dq[: 2 * rows], w_q[...], (1, 1))
    total = total + dot(dk[: 2 * rows], w_k[...], (1, 1))
    total = total + dot(dv[: 2 * rows], w_v[...], (1, 1))
    mine_out[...] = total[:rows]
    other_out[...] = total[rows:]


def assemble_body(width, chunks, order, info, *refs):
    pieces, others, out = refs[:-2], refs[-2], refs[-1]
    rows, block = pieces[0].shape
    for at, ref in enumerate(pieces):
        start = order[at // chunks] * width + at % chunks * block
        for core, part in ((info[2], ref[...]), (1 - info[2], others[at * rows : (at + 1) * rows])):
            column = pl.multiple_of(start + core * (width // 2), block)
            out[:, pl.ds(column, block)] = part


def after(value, *others):
    return lax.optimization_barrier((value, *others))[0]


def partners(count, bit):
    return [(i, i ^ bit) for i in range(count)]


def local(tokens, w_query, w_key, w_value, w_output, out_cotangent):
    clip_count, rows, width = tokens.shape
    assert clip_count == 1
    size = width // H
    half = width // 2
    count = PIECES * rows
    n_seq, n_dp = lax.axis_size("seq"), lax.axis_size("dp")
    pairs = n_seq // PIECES
    seq, place = lax.axis_index("seq"), lax.axis_index("dp")
    info = jnp.stack([seq, place, seq % 2, seq // 2 % 2]).astype(jnp.int32)
    swap = functools.partial(lax.ppermute, axis_name="seq")
    core_links, chip_links = partners(n_seq, 1), partners(n_seq, 2)

    def shift(value, forward):
        total = None
        for d in range(1, pairs):
            links = [(i, i + PIECES * d) for i in range(n_seq - PIECES * d)]
            if not forward:
                links = [(j, i) for i, j in links]
            got = swap(value, perm=links)
            total = got if total is None else total + got
        return total

    tok = tokens.reshape(rows, width)
    cot = out_cotangent.reshape(rows, width)
    tok_f32 = tok.astype(F32)
    tok2 = swap(tok_f32, perm=chip_links)
    tok1 = swap(tok_f32, perm=core_links)
    cot_f32 = after(cot, tok_f32).astype(F32)
    cot2 = swap(cot_f32, perm=chip_links)
    cot1 = swap(cot_f32, perm=core_links)

    columns = lambda i, info: (0, info[2])
    weights = [(w, (width, half), columns) for w in (w_query, w_key, w_value)]
    narrow, wide = (2 * rows, half), (count, half)
    outs = [(narrow, BF16)] * 3 + [((half, size), F32), (narrow, BF16)]
    body = functools.partial(project_body, n_seq, size)
    flops = 2 * 2 * rows * width * half * 3
    q0, k0, v0, state0, rows0 = call(body, info, outs, [tok, tok1, *weights], name="proj0", flops=flops)
    tok2 = after(tok2, state0)
    tok3 = swap(tok2, perm=core_links)
    q1, k1, v1, state, rows1 = call(
        body, info, outs, [tok2, tok3, *weights, state0], name="proj1", flops=flops
    )
    carried = shift(state, True)
    q, k, v, attn, inner = call(
        functools.partial(inside_body, rows, size),
        info,
        [(wide, BF16)] * 3 + [((H // 2, count, count), BF16), (wide, F32)],
        [q0, q1, k0, k1, v0, v1],
        name="inside",
        flops=4 * 4 * count * count * size,
    )
    cot2 = after(cot2, carried, inner)
    cot3 = swap(cot2, perm=core_links)
    cot_all, back = call(
        cotangent_body,
        info,
        [((count, width), BF16), (wide, F32)],
        [cot, cot1, cot2, cot3, (w_output, (half, width), lambda i, info: (info[2], 0))],
        name="cotangent",
        flops=2 * count * width * half,
    )
    carried = after(carried, back, inner)
    mixed, stats = call(
        functools.partial(stats_body, size),
        info,
        [(wide, F32), ((count, 128), F32)],
        [q, carried, inner, back],
        name="stats",
        flops=2 * count * half * size,
    )
    stats_other = swap(stats, perm=core_links)
    normed, d_mixed, own_back = call(
        functools.partial(norm_body, rows, size, width),
        info,
        [(wide, F32), (wide, BF16), ((half, size), F32)],
        [q, mixed, back, stats, stats_other],
        name="norm",
        flops=2 * count * half * size,
    )
    later = shift(own_back, False)
    normed_other = swap(normed, perm=core_links)
    dq, back_scores = call(
        functools.partial(back_query_body, rows, size),
        info,
        [(wide, BF16), ((H // 2, count, count), BF16)],
        [k, v, d_mixed, carried],
        name="back_query",
        flops=4 * 4 * count * count * size,
    )

    factor = 1.0 / math.sqrt(clip_count * n_dp * rows * n_seq)
    chunks = 2
    chunk = [((half // 2, half // chunks), F32)] * (2 * chunks)
    scratch = [pltpu.VMEM((half, half), F32)]
    grad_flops = 2 * count * half * half

    hops = []
    bit = n_dp // 2
    while bit:
        hops.append(("dp", partners(n_dp, bit)))
        bit //= 2
    bit = n_seq // 2
    while bit >= PIECES:
        hops.append(("seq", partners(n_seq, bit)))
        bit //= 2

    def reduce_all(tensors, fillers):
        total_chunks = len(tensors) * chunks
        keeps, sends, made = {}, {}, {}
        steps = [(p + LAG * hop, hop, p) for p in range(total_chunks) for hop in range(len(hops))]
        last, first_hop = None, {}
        for at, (_, hop, p) in enumerate(sorted(steps)):
            for n in range(len(tensors)):
                if n not in made and chunks * n <= (p if hop == 0 else 0) + AHEAD:
                    made[n] = tensors[n](last)
                    for c in range(chunks):
                        keeps[n * chunks + c] = made[n][c]
                        sends[n * chunks + c] = made[n][chunks + c]
            axis, links = hops[hop]
            if hop == 0 and p - WINDOW in first_hop:
                sends[p] = after(sends[p], first_hop[p - WINDOW])
            if at in fillers:
                last = fillers[at](last)
            got = lax.ppermute(sends[p], axis, links)
            total = (keeps[p] if last is None else after(keeps[p], last)) + got
            last = total
            if hop == 0:
                first_hop[p] = total
            middle = total.shape[0] // 2
            keeps[p], sends[p] = total[:middle], total[middle:]
        out = [keeps[p] for p in range(total_chunks)]
        return out, swap(jnp.concatenate([sends[p] for p in range(total_chunks)]), perm=core_links)

    def weight_grad(grad, name):
        return call(
            functools.partial(grad_body, pairs, n_dp, factor),
            info,
            chunk,
            [rows0, rows1, grad],
            scratch,
            name=name,
            flops=grad_flops,
        )

    results = {}

    def grad_query(last):
        return weight_grad(dq, "grad_q")

    def grad_output(last):
        return call(
            functools.partial(grad_out_body, rows, pairs, n_dp, factor),
            info,
            chunk,
            [normed, normed_other, (cot_all, (count, half), columns)],
            scratch,
            name="grad_o",
            flops=grad_flops,
        )

    def grad_key(last):
        dk_inner, dv_inner = call(
            functools.partial(back_rest_body, size),
            info,
            [(wide, F32), (wide, F32)],
            [q, d_mixed, attn, after(back_scores, normed_other)],
            name="back_rest",
            flops=4 * 4 * count * count * size,
        )
        results["dk"], results["dv"] = call(
            functools.partial(finish_body, size),
            info,
            [(wide, BF16)] * 2,
            [k, v, after(later, last), dk_inner, dv_inner],
            name="finish",
            flops=4 * count * half * size,
        )
        results["key"] = weight_grad(results["dk"], "grad_k")
        return results["key"]

    def grad_value(last):
        return weight_grad(after(results["dv"], results["key"][0]), "grad_v")


    def attend(last):
        (results["attended"],) = call(
            functools.partial(attended_body, rows),
            info,
            [((rows, width), BF16)],
            [after(normed, last), normed_other, w_output],
            name="attended",
            flops=2 * rows * width * width,
        )
        return results["attended"]

    def back_tokens(last):
        results["mine"], results["other"] = call(
            functools.partial(tokens_body, rows),
            info,
            [((rows, width), F32)] * 2,
            [after(dq, last), results["dk"], results["dv"], *weights],
            name="d_tokens",
            flops=6 * 2 * rows * width * half,
        )
        return results["mine"]

    own, other_core = reduce_all(
        [grad_query, grad_output, grad_key, grad_value], {4: attend, 7: back_tokens}
    )
    attended, mine, other = results["attended"], results["mine"], results["other"]
    d_tokens = (mine + swap(other, perm=core_links)).astype(BF16)
    (grads,) = call(
        functools.partial(assemble_body, width, chunks, (0, 3, 1, 2)),
        info,
        [((width // (n_seq * n_dp), 4 * width), F32)],
        own + [other_core],
        name="assemble",
    )
    return (
        attended.reshape(tokens.shape),
        d_tokens.reshape(tokens.shape),
        grads,
    )


def solution(mesh):
    return jax.shard_map(
        local,
        mesh=mesh,
        in_specs=(
            P(("groups", "dp"), "seq", None),
            P(),
            P(),
            P(),
            P(),
            P(("groups", "dp"), "seq", None),
        ),
        out_specs=(
            P(("groups", "dp"), "seq", None),
            P(("groups", "dp"), "seq", None),
            P(("groups", "seq", "dp"), None),
        ),
        check_vma=False,
    )
```

time: 142 us -> 119 us (0.84)
  starting transfers between devices: 45.8 us -> 33.3 us
  waiting for transfers between devices: 57.2 us -> 52.4 us
  local copies, waits for them, and re-layouts: 10.6 us -> 5.98 us
  other arithmetic: 4.84 us -> 2.29 us
    ppermute x31 -> x28, starting transfers between devices: 45.8 us -> 33.3 us  [the longest x16 21.6 us: reduce_all(): got = lax.ppermute(sends[p], axis, links)]
    ppermute x31 -> x28, waiting for transfers between devices: 57.2 us -> 52.4 us  [the longest x16 25.2 us: reduce_all(): got = lax.ppermute(sends[p], axis, links)]
    unnamed x26 -> x25, local copies, waits for them, and re-layouts: 10.5 us -> 5.82 us
    convert_element_type x2, other arithmetic: 3.6 us -> 1.04 us  [the longest x1 0.99 us: local(): tok_f32 = tok.astype(F32)]
    pallas_call x14 -> x16, Pallas kernels: 22.1 us -> 23.3 us  [call(): pl.pallas_call(body, name=name, out_shape=shapes, grid_spec=pltpu.Prefetc...]
  transfers between devices with their start and end apart: 31 -> 28, of which waited for: 11 -> 15; matrix products, arithmetic and copies ran while one was open for 2% -> 1% of each run, Pallas kernels for 13% -> 15%
where the time goes in v2:
time: 119 us; the launch traced here: 118 us
  waiting for transfers between devices  52.4 us (44%)
  starting transfers between devices  33.3 us (28%)
  Pallas kernels  23.3 us (20%)
  local copies, waits for them, and re-layouts  5.98 us (5%)
  other arithmetic  2.29 us (2%)
    ppermute x16, waiting for transfers between devices, reduce_all(): got = lax.ppermute(sends[p], axis, links)  25.2 us
    pallas_call x16, Pallas kernels, call(): pl.pallas_call(body, name=name, out_shape=shapes, grid_spec=pltpu.Prefetc...  23.3 us
    ppermute x16, starting transfers between devices, reduce_all(): got = lax.ppermute(sends[p], axis, links)  21.6 us
    ppermute x2, waiting for transfers between devices, shift(): got = swap(value, perm=links)  13.8 us
    ppermute x2, starting transfers between devices, shift(): got = swap(value, perm=links)  6.15 us
    unnamed x25, local copies, waits for them, and re-layouts  5.82 us
    ppermute x1, waiting for transfers between devices, local(): tok2 = swap(tok_f32, perm=chip_links)  4.9 us
    ppermute x1, waiting for transfers between devices, local(): cot2 = swap(cot_f32, perm=chip_links)  4.01 us
  transfers between devices with their start and end apart: 28, of which 15 were waited for; matrix products, arithmetic and copies ran while one was open for 1% of the time, Pallas kernels for 15%

profile of v2, /device:TPU:0, one launch (start us, length us, event | category | flops | bytes accessed | tf_op | source)
XLA Modules:
  0.0 118.3 jit_solution(15881228172338784631)
XLA Ops:
  0.6 1.0 bitcast_convert_fusion
  2.1 2.6 %collective-permute-start.1 = (f32[128,1024]{1,0:T(8,128)S(1)}, f32[128,1024]{1,0:T(8,128)S(1)}, u32[]{:S(2)}, u32[]{:S(2)}) collective-permute-start(f32[128,1024]{1,0:T(8,128)S(1)} %bitcast_convert_fusion), channel_id=1, source_target_pairs={{0,4},{2,6},{4,0},{6,2},{8,12},{10,14},{12,8},{14,10},{1,5},{3,7},... | collective-permute-start | bytes 1572872 | tf_op jit(solution)/shard_map/ppermute | solution.py:283
  4.9 1.6 %copy-done = bf16[1024,1024]{1,0:T(8,128)(2,1)S(1)} copy-done((bf16[1024,1024]{1,0:T(8,128)(2,1)S(1)}, bf16[1024,1024]{1,0:T(8,128)(2,1)}, u32[]{:S(2)}) %copy-start) | copy-done | bytes 2097176
  6.5 1.6 %copy-done.2 = bf16[1024,1024]{1,0:T(8,128)(2,1)S(1)} copy-done((bf16[1024,1024]{1,0:T(8,128)(2,1)S(1)}, bf16[1024,1024]{1,0:T(8,128)(2,1)}, u32[]{:S(2)}) %copy-start.2) | copy-done | bytes 2097176
  8.1 1.6 %copy-done.4 = bf16[1024,1024]{1,0:T(8,128)(2,1)S(1)} copy-done((bf16[1024,1024]{1,0:T(8,128)(2,1)S(1)}, bf16[1024,1024]{1,0:T(8,128)(2,1)}, u32[]{:S(2)}) %copy-start.4) | copy-done | bytes 2097176
  9.7 0.9 copy-done.7
  10.6 1.8 %proj0.1 = (bf16[256,512]{1,0:T(8,128)(2,1)S(1)}, bf16[256,512]{1,0:T(8,128)(2,1)S(1)}, bf16[256,512]{1,0:T(8,128)(2,1)S(1)}, f32[512,128]{1,0:T(8,128)S(1)}, bf16[256,512]{1,0:T(8,128)(2,1)S(1)}) custom-call(s32[4]{0:T(128)S(1)} %pad_add_fusion.info, bf16[128,1024]{1,0:T(8,128)(2,1)S(1)} %bitcast.10, f32[128,1024]{1,0:T(8,128)S(1)} %collective-permute-done.second, ...), custom_call_target="tpu_custom_call" | custom-call | flops 1 | bytes 1 | tf_op jit(solution)/shard_map/proj0/pallas_call | solution.py:33
  12.4 4.9 %collective-permute-done.1.first = f32[128,1024]{1,0:T(8,128)S(1)} collective-permute-done((f32[128,1024]{1,0:T(8,128)S(1)}, f32[128,1024]{1,0:T(8,128)S(1)}, u32[]{:S(2)}, u32[]{:S(2)}) %collective-permute-start.1) | collective-permute-done | bytes 524320 | tf_op jit(solution)/shard_map/ppermute | solution.py:283
  17.4 1.8 %collective-permute-start.5 = (f32[128,1024]{1,0:T(8,128)S(1)}, f32[128,1024]{1,0:T(8,128)S(1)}, u32[]{:S(2)}, u32[]{:S(2)}) collective-permute-start(f32[128,1024]{1,0:T(8,128)S(1)} %convert_element_type.10), channel_id=1, source_target_pairs={{0,4},{2,6},{4,0},{6,2},{8,12},{10,14},{12,8},{14,10},{1,5},{3,7},... | collective-permute-start | bytes 1572872 | tf_op jit(solution)/shard_map/ppermute | solution.py:286
  19.2 1.8 %proj1.1 = (bf16[256,512]{1,0:T(8,128)(2,1)S(1)}, bf16[256,512]{1,0:T(8,128)(2,1)S(1)}, bf16[256,512]{1,0:T(8,128)(2,1)S(1)}, f32[512,128]{1,0:T(8,128)S(1)}, bf16[256,512]{1,0:T(8,128)(2,1)S(1)}) custom-call(s32[4]{0:T(128)S(1)} %pad_add_fusion.info, f32[128,1024]{1,0:T(8,128)S(1)} %collective-permute-done.1.first, ...), custom_call_target="tpu_custom_call" | custom-call | flops 1 | bytes 1 | tf_op jit(solution)/shard_map/proj1/pallas_call | solution.py:33
  21.1 4.7 %collective-permute-start.3 = (f32[512,128]{1,0:T(8,128)S(1)}, f32[512,128]{1,0:T(8,128)S(1)}, u32[]{:S(2)}, u32[]{:S(2)}) collective-permute-start(f32[512,128]{1,0:T(8,128)S(1)} %get-tuple-element.88), channel_id=1, source_target_pairs={{0,8},{2,10},{4,12},{6,14},{1,9},{3,11},{5,13},{7,15},{16,24},{18,... | collective-permute-start | bytes 786440 | tf_op jit(solution)/shard_map/ppermute | solution.py:276
  25.8 1.9 %inside.1 = (bf16[512,512]{1,0:T(8,128)(2,1)S(1)}, bf16[512,512]{1,0:T(8,128)(2,1)S(1)}, bf16[512,512]{1,0:T(8,128)(2,1)S(1)}, bf16[4,512,512]{2,1,0:T(8,128)(2,1)S(1)}, f32[512,512]{1,0:T(8,128)S(1)}) custom-call(s32[4]{0:T(128)S(1)} %pad_add_fusion.info, bf16[256,512]{1,0:T(8,128)(2,1)S(1)} %get-tuple-element.79.q0, ...), custom_call_target="tpu_custom_call" | custom-call | flops 1 | bytes 1 | tf_op jit(solution)/shard_map/inside/pallas_call | solution.py:33
  27.8 4.0 %collective-permute-done.5.c2 = f32[128,1024]{1,0:T(8,128)S(1)} collective-permute-done((f32[128,1024]{1,0:T(8,128)S(1)}, f32[128,1024]{1,0:T(8,128)S(1)}, u32[]{:S(2)}, u32[]{:S(2)}) %collective-permute-start.5) | collective-permute-done | bytes 524320 | tf_op jit(solution)/shard_map/ppermute | solution.py:286
  31.8 4.9 %collective-permute-done.3.carried = f32[512,128]{1,0:T(8,128)S(1)} collective-permute-done((f32[512,128]{1,0:T(8,128)S(1)}, f32[512,128]{1,0:T(8,128)S(1)}, u32[]{:S(2)}, u32[]{:S(2)}) %collective-permute-start.3) | collective-permute-done | bytes 262176 | tf_op jit(solution)/shard_map/ppermute | solution.py:276
  36.7 1.9 %collective-permute-done.6.c3 = f32[128,1024]{1,0:T(8,128)S(1)} collective-permute-done((f32[128,1024]{1,0:T(8,128)S(1)}, f32[128,1024]{1,0:T(8,128)S(1)}, u32[]{:S(2)}, u32[]{:S(2)}) %collective-permute-start.6) | collective-permute-done | bytes 524320 | tf_op jit(solution)/shard_map/ppermute | solution.py:311
  38.6 1.3 %cotangent.1 = (bf16[512,1024]{1,0:T(8,128)(2,1)S(1)}, f32[512,512]{1,0:T(8,128)S(1)}) custom-call(s32[4]{0:T(128)S(1)} %pad_add_fusion.info, bf16[128,1024]{1,0:T(8,128)(2,1)S(1)} %bitcast.12, f32[128,1024]{1,0:T(8,128)S(1)} %collective-permute-done.4.c1, f32[128,1024]{1,0:T(8,128)S(1)} %collective-permute-done.5.c2, ...), custom_call_target="tpu_custom_call" | custom-call | flops 1 | bytes 1 | tf_op jit(solution)/shard_map/cotangent/pallas_call | solution.py:33
  39.9 1.0 stats.1
  41.1 1.4 %collective-permute-done.7.other = f32[512,128]{1,0:T(8,128)S(1)} collective-permute-done((f32[512,128]{1,0:T(8,128)S(1)}, f32[512,128]{1,0:T(8,128)S(1)}, u32[]{:S(2)}, u32[]{:S(2)}) %collective-permute-start.7) | collective-permute-done | bytes 262176 | tf_op jit(solution)/shard_map/ppermute | solution.py:329
  42.5 1.4 %norm.1 = (f32[512,512]{1,0:T(8,128)S(1)}, bf16[512,512]{1,0:T(8,128)(2,1)S(1)}, f32[512,128]{1,0:T(8,128)S(1)}) custom-call(s32[4]{0:T(128)S(1)} %pad_add_fusion.info, bf16[512,512]{1,0:T(8,128)(2,1)S(1)} %get-tuple-element.87.q, f32[512,512]{1,0:T(8,128)S(1)} %get-tuple-element.94.mixed, f32[512,512]{1,0:T(8,128)S(1)} %get-tuple-element.92.back, ...), custom_call_target="tpu_custom_call" | custom-call | flops 1 | bytes 1 | tf_op jit(solution)/shard_map/norm/pallas_call | solution.py:33
  44.1 2.1 %back_query.1 = (bf16[512,512]{1,0:T(8,128)(2,1)S(1)}, bf16[4,512,512]{2,1,0:T(8,128)(2,1)S(1)}) custom-call(s32[4]{0:T(128)S(1)} %pad_add_fusion.info, bf16[512,512]{1,0:T(8,128)(2,1)S(1)} %get-tuple-element.99.k, bf16[512,512]{1,0:T(8,128)(2,1)S(1)} %get-tuple-element.100.v, bf16[512,512]{1,0:T(8,128)(2,1)S(1)} %get-tuple-element.101.d_mixed, ...), custom_call_target="tpu_custom_call" | custom-call | flops 1 | bytes 1 | tf_op jit(solution)/shard_map/back_query/pallas_call | solution.py:33
  46.2 1.1 grad_q.1
  47.3 1.6 %collective-permute-start.8 = (f32[256,256]{1,0:T(8,128)S(1)}, f32[256,256]{1,0:T(8,128)S(1)}, u32[]{:S(2)}, u32[]{:S(2)}) collective-permute-start(f32[256,256]{1,0:T(8,128)S(1)} %get-tuple-element.104), channel_id=1, source_target_pairs={{0,1},{1,0},{2,3},{3,2},{4,5},{5,4},{6,7},{7,6},{8,9},{9,8},{10,11... | collective-permute-start | bytes 786440 | tf_op jit(solution)/shard_map/ppermute | solution.py:382
  49.4 1.5 %collective-permute-start.13 = (f32[512,128]{1,0:T(8,128)S(1)}, f32[512,128]{1,0:T(8,128)S(1)}, u32[]{:S(2)}, u32[]{:S(2)}) collective-permute-start(f32[512,128]{1,0:T(8,128)S(1)} %get-tuple-element.115), channel_id=1, source_target_pairs={{8,0},{10,2},{12,4},{14,6},{9,1},{11,3},{13,5},{15,7},{24,16},{26,... | collective-permute-start | bytes 786440 | tf_op jit(solution)/shard_map/ppermute | solution.py:276
  50.8 5.6 %collective-permute-done.8 = f32[256,256]{1,0:T(8,128)S(1)} collective-permute-done((f32[256,256]{1,0:T(8,128)S(1)}, f32[256,256]{1,0:T(8,128)S(1)}, u32[]{:S(2)}, u32[]{:S(2)}) %collective-permute-start.8) | collective-permute-done | bytes 262176 | tf_op jit(solution)/shard_map/ppermute | solution.py:382
  56.5 1.2 grad_o.1
  57.7 1.6 %collective-permute-start.11 = (f32[256,256]{1,0:T(8,128)S(1)}, f32[256,256]{1,0:T(8,128)S(1)}, u32[]{:S(2)}, u32[]{:S(2)}) collective-permute-start(f32[256,256]{1,0:T(8,128)S(1)} %get-tuple-element.112), channel_id=1, source_target_pairs={{0,1},{1,0},{2,3},{3,2},{4,5},{5,4},{6,7},{7,6},{8,9},{9,8},{10,11... | collective-permute-start | bytes 786440 | tf_op jit(solution)/shard_map/ppermute | solution.py:382
  59.3 3.5 %collective-permute-start.12 = (f32[128,256]{1,0:T(8,128)S(1)}, f32[128,256]{1,0:T(8,128)S(1)}, u32[]{:S(2)}, u32[]{:S(2)}) collective-permute-start(f32[128,256]{1,0:T(8,128)S(1)} %get-tuple-element.169), channel_id=1, source_target_pairs={{0,8},{2,10},{4,12},{6,14},{8,0},{10,2},{12,4},{14,6},{1,9},{3,11}... | collective-permute-start | bytes 393224 | tf_op jit(solution)/shard_map/ppermute | solution.py:382
  63.7 8.9 %collective-permute-done.13.later = f32[512,128]{1,0:T(8,128)S(1)} collective-permute-done((f32[512,128]{1,0:T(8,128)S(1)}, f32[512,128]{1,0:T(8,128)S(1)}, u32[]{:S(2)}, u32[]{:S(2)}) %collective-permute-start.13) | collective-permute-done | bytes 262176 | tf_op jit(solution)/shard_map/ppermute | solution.py:276
  72.6 1.8 %back_rest.1 = (f32[512,512]{1,0:T(8,128)S(1)}, f32[512,512]{1,0:T(8,128)S(1)}) custom-call(s32[4]{0:T(128)S(1)} %pad_add_fusion.info, bf16[512,512]{1,0:T(8,128)(2,1)S(1)} %get-tuple-element.87.q, bf16[512,512]{1,0:T(8,128)(2,1)S(1)} %get-tuple-element.101.d_mixed, bf16[4,512,512]{2,1,0:T(8,128)(2,1)S(1)} %get-tuple-element.117.attn, ...), custom_call_target="tpu_custom_call" | custom-call | flops 1 | bytes 1 | tf_op jit(solution)/shard_map/back_rest/pallas_call | solution.py:33
  74.4 1.0 finish.1
  75.4 1.1 grad_k.1
  76.5 1.1 grad_v.1
  77.7 1.7 %attended.1 = bf16[128,1024]{1,0:T(8,128)(2,1)} custom-call(s32[4]{0:T(128)S(1)} %pad_add_fusion.info, f32[512,512]{1,0:T(8,128)S(1)} %get-tuple-element.114.mine, f32[512,512]{1,0:T(8,128)S(1)} %collective-permute-done.9.other, bf16[1024,1024]{1,0:T(8,128)(2,1)S(1)} %copy-done.6), custom_call_target="tpu_custom_call" | custom-call | flops 1 | bytes 1 | tf_op jit(solution)/shard_map/attended/pallas_call | solution.py:33
  79.4 3.0 %collective-permute-start.18 = (f32[128,256]{1,0:T(8,128)S(1)}, f32[128,256]{1,0:T(8,128)S(1)}, u32[]{:S(2)}, u32[]{:S(2)}) collective-permute-start(f32[128,256]{1,0:T(8,128)S(1)} %get-tuple-element.165), channel_id=1, source_target_pairs={{0,8},{2,10},{4,12},{6,14},{8,0},{10,2},{12,4},{14,6},{1,9},{3,11}... | collective-permute-start | bytes 393224 | tf_op jit(solution)/shard_map/ppermute | solution.py:382
  82.4 1.6 %collective-permute-start.16 = (f32[256,256]{1,0:T(8,128)S(1)}, f32[256,256]{1,0:T(8,128)S(1)}, u32[]{:S(2)}, u32[]{:S(2)}) collective-permute-start(f32[256,256]{1,0:T(8,128)S(1)} %get-tuple-element.131), channel_id=1, source_target_pairs={{0,1},{1,0},{2,3},{3,2},{4,5},{5,4},{6,7},{7,6},{8,9},{9,8},{10,11... | collective-permute-start | bytes 786440 | tf_op jit(solution)/shard_map/ppermute | solution.py:382
  84.8 4.6 %collective-permute-done.16 = f32[256,256]{1,0:T(8,128)S(1)} collective-permute-done((f32[256,256]{1,0:T(8,128)S(1)}, f32[256,256]{1,0:T(8,128)S(1)}, u32[]{:S(2)}, u32[]{:S(2)}) %collective-permute-start.16) | collective-permute-done | bytes 262176 | tf_op jit(solution)/shard_map/ppermute | solution.py:382
  89.5 1.6 %d_tokens.1 = (f32[128,1024]{1,0:T(8,128)S(1)}, f32[128,1024]{1,0:T(8,128)S(1)}) custom-call(s32[4]{0:T(128)S(1)} %pad_add_fusion.info, bf16[512,512]{1,0:T(8,128)(2,1)S(1)} %get-tuple-element.132.grad.dq, bf16[512,512]{1,0:T(8,128)(2,1)S(1)} %get-tuple-element.122.grad.dk, bf16[512,512]{1,0:T(8,128)(2,1)S(1)} %get-tuple-element.142.dv.grad, ...), custom_call_target="tpu_custom_call" | custom-call | flops 1 | bytes 1 | tf_op jit(solution)/shard_map/d_tokens/pallas_call | solution.py:33
  91.1 3.1 %collective-permute-done.19 = f32[256,256]{1,0:T(8,128)S(1)} collective-permute-done((f32[256,256]{1,0:T(8,128)S(1)}, f32[256,256]{1,0:T(8,128)S(1)}, u32[]{:S(2)}, u32[]{:S(2)}) %collective-permute-start.19) | collective-permute-done | bytes 262176 | tf_op jit(solution)/shard_map/ppermute | solution.py:382
  94.3 1.8 %collective-permute-start.21 = (f32[256,256]{1,0:T(8,128)S(1)}, f32[256,256]{1,0:T(8,128)S(1)}, u32[]{:S(2)}, u32[]{:S(2)}) collective-permute-start(f32[256,256]{1,0:T(8,128)S(1)} %get-tuple-element.146), channel_id=1, source_target_pairs={{0,1},{1,0},{2,3},{3,2},{4,5},{5,4},{6,7},{7,6},{8,9},{9,8},{10,11... | collective-permute-start | bytes 786440 | tf_op jit(solution)/shard_map/ppermute | solution.py:382
  96.7 2.8 %collective-permute-start.24 = (f32[128,256]{1,0:T(8,128)S(1)}, f32[128,256]{1,0:T(8,128)S(1)}, u32[]{:S(2)}, u32[]{:S(2)}) collective-permute-start(f32[128,256]{1,0:T(8,128)S(1)} %get-tuple-element.159), channel_id=1, source_target_pairs={{0,8},{2,10},{4,12},{6,14},{8,0},{10,2},{12,4},{14,6},{1,9},{3,11}... | collective-permute-start | bytes 393224 | tf_op jit(solution)/shard_map/ppermute | solution.py:382
  99.5 1.2 %collective-permute-done.21 = f32[256,256]{1,0:T(8,128)S(1)} collective-permute-done((f32[256,256]{1,0:T(8,128)S(1)}, f32[256,256]{1,0:T(8,128)S(1)}, u32[]{:S(2)}, u32[]{:S(2)}) %collective-permute-start.21) | collective-permute-done | bytes 262176 | tf_op jit(solution)/shard_map/ppermute | solution.py:382
  100.8 1.3 %collective-permute-done.22 = f32[128,256]{1,0:T(8,128)S(1)} collective-permute-done((f32[128,256]{1,0:T(8,128)S(1)}, f32[128,256]{1,0:T(8,128)S(1)}, u32[]{:S(2)}, u32[]{:S(2)}) %collective-permute-start.22) | collective-permute-done | bytes 131104 | tf_op jit(solution)/shard_map/ppermute | solution.py:382
  102.1 1.4 %collective-permute-done.23 = f32[256,256]{1,0:T(8,128)S(1)} collective-permute-done((f32[256,256]{1,0:T(8,128)S(1)}, f32[256,256]{1,0:T(8,128)S(1)}, u32[]{:S(2)}, u32[]{:S(2)}) %collective-permute-start.23) | collective-permute-done | bytes 262176 | tf_op jit(solution)/shard_map/ppermute | solution.py:382
  103.6 2.0 %collective-permute-start.26 = (f32[128,256]{1,0:T(8,128)S(1)}, f32[128,256]{1,0:T(8,128)S(1)}, u32[]{:S(2)}, u32[]{:S(2)}) collective-permute-start(f32[128,256]{1,0:T(8,128)S(1)} %get-tuple-element.155), channel_id=1, source_target_pairs={{0,8},{2,10},{4,12},{6,14},{8,0},{10,2},{12,4},{14,6},{1,9},{3,11}... | collective-permute-start | bytes 393224 | tf_op jit(solution)/shard_map/ppermute | solution.py:382
  105.6 1.2 %collective-permute-start.25 = (f32[128,256]{1,0:T(8,128)S(1)}, f32[128,256]{1,0:T(8,128)S(1)}, u32[]{:S(2)}, u32[]{:S(2)}) collective-permute-start(f32[128,256]{1,0:T(8,128)S(1)} %get-tuple-element.157), channel_id=1, source_target_pairs={{0,8},{2,10},{4,12},{6,14},{8,0},{10,2},{12,4},{14,6},{1,9},{3,11}... | collective-permute-start | bytes 393224 | tf_op jit(solution)/shard_map/ppermute | solution.py:382
  106.9 7.8 %collective-permute-done.25 = f32[128,256]{1,0:T(8,128)S(1)} collective-permute-done((f32[128,256]{1,0:T(8,128)S(1)}, f32[128,256]{1,0:T(8,128)S(1)}, u32[]{:S(2)}, u32[]{:S(2)}) %collective-permute-start.25) | collective-permute-done | bytes 131104 | tf_op jit(solution)/shard_map/ppermute | solution.py:382
  115.6 1.1 collective-permute-done.27.refs_8_
  116.7 1.6 %assemble.1 = f32[64,4096]{1,0:T(8,128)} custom-call(s32[4]{0:T(128)S(1)} %pad_add_fusion.info, f32[64,256]{1,0:T(8,128)S(1)} %get-tuple-element.186.refs_0_, f32[64,256]{1,0:T(8,128)S(1)} %get-tuple-element.184.refs_1_, f32[64,256]{1,0:T(8,128)S(1)} %get-tuple-element.182.refs_2_, f32[64,256]{1,0:T(8,128)S(1)} %get-tuple-element.180.refs_3_, ...), custom_call_target="tpu_custom_call" | custom-call | flops 1 | bytes 1 | tf_op jit(solution)/shard_map/assemble/pallas_call | solution.py:33
  (78 shorter events, 5.4 us)
Async XLA Ops:
  1.6 3.2 %collective-permute-start = (f32[128,1024]{1,0:T(8,128)S(1)}, f32[128,1024]{1,0:T(8,128)S(1)}, u32[]{:S(2)}, u32[]{:S(2)}) collective-permute-start(f32[128,1024]{1,0:T(8,128)S(1)} %bitcast_convert_fusion), channel_id=1, source_target_pairs={{0,2},{2,0},{4,6},{6,4},{8,10},{10,8},{12,14},{14,12},{1,3},{3,1},... | collective-permute-start | bytes 1572872 | tf_op jit(solution)/shard_map/ppermute | solution.py:284
  2.1 15.2 %collective-permute-start.1 = (f32[128,1024]{1,0:T(8,128)S(1)}, f32[128,1024]{1,0:T(8,128)S(1)}, u32[]{:S(2)}, u32[]{:S(2)}) collective-permute-start(f32[128,1024]{1,0:T(8,128)S(1)} %bitcast_convert_fusion), channel_id=1, source_target_pairs={{0,4},{2,6},{4,0},{6,2},{8,12},{10,14},{12,8},{14,10},{1,5},{3,7},... | collective-permute-start | bytes 1572872 | tf_op jit(solution)/shard_map/ppermute | solution.py:283
  4.9 1.6 %copy-start = (bf16[1024,1024]{1,0:T(8,128)(2,1)S(1)}, bf16[1024,1024]{1,0:T(8,128)(2,1)}, u32[]{:S(2)}) copy-start(bf16[1024,1024]{1,0:T(8,128)(2,1)} %w_q.5) | copy-start | bytes 6291460
  6.5 1.6 %copy-start.2 = (bf16[1024,1024]{1,0:T(8,128)(2,1)S(1)}, bf16[1024,1024]{1,0:T(8,128)(2,1)}, u32[]{:S(2)}) copy-start(bf16[1024,1024]{1,0:T(8,128)(2,1)} %w_k.5) | copy-start | bytes 6291460
  8.1 1.6 %copy-start.4 = (bf16[1024,1024]{1,0:T(8,128)(2,1)S(1)}, bf16[1024,1024]{1,0:T(8,128)(2,1)}, u32[]{:S(2)}) copy-start(bf16[1024,1024]{1,0:T(8,128)(2,1)} %w_v.5) | copy-start | bytes 6291460
  9.7 0.9 copy-start.7
  10.6 6.7 %copy-start.8 = (bf16[1,128,1024]{2,1,0:T(8,128)(2,1)S(1)}, bf16[1,128,1024]{2,1,0:T(8,128)(2,1)}, u32[]{:S(2)}) copy-start(bf16[1,128,1024]{2,1,0:T(8,128)(2,1)} %param.11) | copy-start | bytes 786436
  10.6 8.6 %copy-start.1 = (bf16[1024,1024]{1,0:T(8,128)(2,1)S(1)}, bf16[1024,1024]{1,0:T(8,128)(2,1)}, u32[]{:S(2)}) copy-start(bf16[1024,1024]{1,0:T(8,128)(2,1)} %w_q.5) | copy-start | bytes 6291460
  10.6 8.6 %copy-start.3 = (bf16[1024,1024]{1,0:T(8,128)(2,1)S(1)}, bf16[1024,1024]{1,0:T(8,128)(2,1)}, u32[]{:S(2)}) copy-start(bf16[1024,1024]{1,0:T(8,128)(2,1)} %w_k.5) | copy-start | bytes 6291460
  10.6 8.6 %copy-start.5 = (bf16[1024,1024]{1,0:T(8,128)(2,1)S(1)}, bf16[1024,1024]{1,0:T(8,128)(2,1)}, u32[]{:S(2)}) copy-start(bf16[1024,1024]{1,0:T(8,128)(2,1)} %w_v.5) | copy-start | bytes 6291460
  17.3 1.9 %collective-permute-start.2 = (f32[128,1024]{1,0:T(8,128)S(1)}, f32[128,1024]{1,0:T(8,128)S(1)}, u32[]{:S(2)}, u32[]{:S(2)}) collective-permute-start(f32[128,1024]{1,0:T(8,128)S(1)} %collective-permute-done.1.first), channel_id=1, source_target_pairs={{0,2},{2,0},{4,6},{6,4},{8,10},{10,8},{12,14},{14,12},{1,3},{3,1},... | collective-permute-start | bytes 1572872 | tf_op jit(solution)/shard_map/ppermute | solution.py:297
  17.4 14.4 %collective-permute-start.5 = (f32[128,1024]{1,0:T(8,128)S(1)}, f32[128,1024]{1,0:T(8,128)S(1)}, u32[]{:S(2)}, u32[]{:S(2)}) collective-permute-start(f32[128,1024]{1,0:T(8,128)S(1)} %convert_element_type.10), channel_id=1, source_target_pairs={{0,4},{2,6},{4,0},{6,2},{8,12},{10,14},{12,8},{14,10},{1,5},{3,7},... | collective-permute-start | bytes 1572872 | tf_op jit(solution)/shard_map/ppermute | solution.py:286
  19.2 19.4 %copy-start.6 = (bf16[1024,1024]{1,0:T(8,128)(2,1)S(1)}, bf16[1024,1024]{1,0:T(8,128)(2,1)}, u32[]{:S(2)}) copy-start(bf16[1024,1024]{1,0:T(8,128)(2,1)} %w_o.3) | copy-start | bytes 6291460
  21.1 15.7 %collective-permute-start.3 = (f32[512,128]{1,0:T(8,128)S(1)}, f32[512,128]{1,0:T(8,128)S(1)}, u32[]{:S(2)}, u32[]{:S(2)}) collective-permute-start(f32[512,128]{1,0:T(8,128)S(1)} %get-tuple-element.88), channel_id=1, source_target_pairs={{0,8},{2,10},{4,12},{6,14},{1,9},{3,11},{5,13},{7,15},{16,24},{18,... | collective-permute-start | bytes 786440 | tf_op jit(solution)/shard_map/ppermute | solution.py:276
  25.8 11.0 %collective-permute-start.4 = (f32[128,1024]{1,0:T(8,128)S(1)}, f32[128,1024]{1,0:T(8,128)S(1)}, u32[]{:S(2)}, u32[]{:S(2)}) collective-permute-start(f32[128,1024]{1,0:T(8,128)S(1)} %convert_element_type.10), channel_id=1, source_target_pairs={{0,2},{2,0},{4,6},{6,4},{8,10},{10,8},{12,14},{14,12},{1,3},{3,1},... | collective-permute-start | bytes 1572872 | tf_op jit(solution)/shard_map/ppermute | solution.py:287
  36.7 1.9 %collective-permute-start.6 = (f32[128,1024]{1,0:T(8,128)S(1)}, f32[128,1024]{1,0:T(8,128)S(1)}, u32[]{:S(2)}, u32[]{:S(2)}) collective-permute-start(f32[128,1024]{1,0:T(8,128)S(1)} %collective-permute-done.5.c2), channel_id=1, source_target_pairs={{0,2},{2,0},{4,6},{6,4},{8,10},{10,8},{12,14},{14,12},{1,3},{3,1},... | collective-permute-start | bytes 1572872 | tf_op jit(solution)/shard_map/ppermute | solution.py:311
  40.9 1.6 %collective-permute-start.7 = (f32[512,128]{1,0:T(8,128)S(1)}, f32[512,128]{1,0:T(8,128)S(1)}, u32[]{:S(2)}, u32[]{:S(2)}) collective-permute-start(f32[512,128]{1,0:T(8,128)S(1)} %get-tuple-element.95.mine), channel_id=1, source_target_pairs={{0,2},{2,0},{4,6},{6,4},{8,10},{10,8},{12,14},{14,12},{1,3},{3,1},... | collective-permute-start | bytes 786440 | tf_op jit(solution)/shard_map/ppermute | solution.py:329
  43.9 12.6 %collective-permute-start.9 = (f32[512,512]{1,0:T(8,128)S(1)}, f32[512,512]{1,0:T(8,128)S(1)}, u32[]{:S(2)}, u32[]{:S(2)}) collective-permute-start(f32[512,512]{1,0:T(8,128)S(1)} %get-tuple-element.114.mine), channel_id=1, source_target_pairs={{0,2},{2,0},{4,6},{6,4},{8,10},{10,8},{12,14},{14,12},{1,3},{3,1},... | collective-permute-start | bytes 3145736 | tf_op jit(solution)/shard_map/ppermute | solution.py:339
  47.3 9.2 %collective-permute-start.8 = (f32[256,256]{1,0:T(8,128)S(1)}, f32[256,256]{1,0:T(8,128)S(1)}, u32[]{:S(2)}, u32[]{:S(2)}) collective-permute-start(f32[256,256]{1,0:T(8,128)S(1)} %get-tuple-element.104), channel_id=1, source_target_pairs={{0,1},{1,0},{2,3},{3,2},{4,5},{5,4},{6,7},{7,6},{8,9},{9,8},{10,11... | collective-permute-start | bytes 786440 | tf_op jit(solution)/shard_map/ppermute | solution.py:382
  48.8 13.9 %collective-permute-start.10 = (f32[256,256]{1,0:T(8,128)S(1)}, f32[256,256]{1,0:T(8,128)S(1)}, u32[]{:S(2)}, u32[]{:S(2)}) collective-permute-start(f32[256,256]{1,0:T(8,128)S(1)} %get-tuple-element.109), channel_id=1, source_target_pairs={{0,1},{1,0},{2,3},{3,2},{4,5},{5,4},{6,7},{7,6},{8,9},{9,8},{10,11... | collective-permute-start | bytes 786440 | tf_op jit(solution)/shard_map/ppermute | solution.py:382
  49.4 23.2 %collective-permute-start.13 = (f32[512,128]{1,0:T(8,128)S(1)}, f32[512,128]{1,0:T(8,128)S(1)}, u32[]{:S(2)}, u32[]{:S(2)}) collective-permute-start(f32[512,128]{1,0:T(8,128)S(1)} %get-tuple-element.115), channel_id=1, source_target_pairs={{8,0},{10,2},{12,4},{14,6},{9,1},{11,3},{13,5},{15,7},{24,16},{26,... | collective-permute-start | bytes 786440 | tf_op jit(solution)/shard_map/ppermute | solution.py:276
  57.7 19.9 %collective-permute-start.11 = (f32[256,256]{1,0:T(8,128)S(1)}, f32[256,256]{1,0:T(8,128)S(1)}, u32[]{:S(2)}, u32[]{:S(2)}) collective-permute-start(f32[256,256]{1,0:T(8,128)S(1)} %get-tuple-element.112), channel_id=1, source_target_pairs={{0,1},{1,0},{2,3},{3,2},{4,5},{5,4},{6,7},{7,6},{8,9},{9,8},{10,11... | collective-permute-start | bytes 786440 | tf_op jit(solution)/shard_map/ppermute | solution.py:382
  59.3 18.3 %collective-permute-start.12 = (f32[128,256]{1,0:T(8,128)S(1)}, f32[128,256]{1,0:T(8,128)S(1)}, u32[]{:S(2)}, u32[]{:S(2)}) collective-permute-start(f32[128,256]{1,0:T(8,128)S(1)} %get-tuple-element.169), channel_id=1, source_target_pairs={{0,8},{2,10},{4,12},{6,14},{8,0},{10,2},{12,4},{14,6},{1,9},{3,11}... | collective-permute-start | bytes 393224 | tf_op jit(solution)/shard_map/ppermute | solution.py:382
  62.8 19.5 %collective-permute-start.14 = (f32[256,256]{1,0:T(8,128)S(1)}, f32[256,256]{1,0:T(8,128)S(1)}, u32[]{:S(2)}, u32[]{:S(2)}) collective-permute-start(f32[256,256]{1,0:T(8,128)S(1)} %get-tuple-element.127), channel_id=1, source_target_pairs={{0,1},{1,0},{2,3},{3,2},{4,5},{5,4},{6,7},{7,6},{8,9},{9,8},{10,11... | collective-permute-start | bytes 786440 | tf_op jit(solution)/shard_map/ppermute | solution.py:382
  72.6 12.2 %collective-permute-start.15 = (f32[128,256]{1,0:T(8,128)S(1)}, f32[128,256]{1,0:T(8,128)S(1)}, u32[]{:S(2)}, u32[]{:S(2)}) collective-permute-start(f32[128,256]{1,0:T(8,128)S(1)} %get-tuple-element.167), channel_id=1, source_target_pairs={{0,8},{2,10},{4,12},{6,14},{8,0},{10,2},{12,4},{14,6},{1,9},{3,11}... | collective-permute-start | bytes 393224 | tf_op jit(solution)/shard_map/ppermute | solution.py:382
  79.4 11.7 %collective-permute-start.18 = (f32[128,256]{1,0:T(8,128)S(1)}, f32[128,256]{1,0:T(8,128)S(1)}, u32[]{:S(2)}, u32[]{:S(2)}) collective-permute-start(f32[128,256]{1,0:T(8,128)S(1)} %get-tuple-element.165), channel_id=1, source_target_pairs={{0,8},{2,10},{4,12},{6,14},{8,0},{10,2},{12,4},{14,6},{1,9},{3,11}... | collective-permute-start | bytes 393224 | tf_op jit(solution)/shard_map/ppermute | solution.py:382
  82.4 7.0 %collective-permute-start.16 = (f32[256,256]{1,0:T(8,128)S(1)}, f32[256,256]{1,0:T(8,128)S(1)}, u32[]{:S(2)}, u32[]{:S(2)}) collective-permute-start(f32[256,256]{1,0:T(8,128)S(1)} %get-tuple-element.131), channel_id=1, source_target_pairs={{0,1},{1,0},{2,3},{3,2},{4,5},{5,4},{6,7},{7,6},{8,9},{9,8},{10,11... | collective-permute-start | bytes 786440 | tf_op jit(solution)/shard_map/ppermute | solution.py:382
  84.0 12.6 %collective-permute-start.20 = (f32[128,256]{1,0:T(8,128)S(1)}, f32[128,256]{1,0:T(8,128)S(1)}, u32[]{:S(2)}, u32[]{:S(2)}) collective-permute-start(f32[128,256]{1,0:T(8,128)S(1)} %get-tuple-element.163), channel_id=1, source_target_pairs={{0,8},{2,10},{4,12},{6,14},{8,0},{10,2},{12,4},{14,6},{1,9},{3,11}... | collective-permute-start | bytes 393224 | tf_op jit(solution)/shard_map/ppermute | solution.py:382
  84.1 10.1 %collective-permute-start.19 = (f32[256,256]{1,0:T(8,128)S(1)}, f32[256,256]{1,0:T(8,128)S(1)}, u32[]{:S(2)}, u32[]{:S(2)}) collective-permute-start(f32[256,256]{1,0:T(8,128)S(1)} %get-tuple-element.140), channel_id=1, source_target_pairs={{0,1},{1,0},{2,3},{3,2},{4,5},{5,4},{6,7},{7,6},{8,9},{9,8},{10,11... | collective-permute-start | bytes 786440 | tf_op jit(solution)/shard_map/ppermute | solution.py:382
  94.3 6.4 %collective-permute-start.21 = (f32[256,256]{1,0:T(8,128)S(1)}, f32[256,256]{1,0:T(8,128)S(1)}, u32[]{:S(2)}, u32[]{:S(2)}) collective-permute-start(f32[256,256]{1,0:T(8,128)S(1)} %get-tuple-element.146), channel_id=1, source_target_pairs={{0,1},{1,0},{2,3},{3,2},{4,5},{5,4},{6,7},{7,6},{8,9},{9,8},{10,11... | collective-permute-start | bytes 786440 | tf_op jit(solution)/shard_map/ppermute | solution.py:382
  96.1 5.9 %collective-permute-start.22 = (f32[128,256]{1,0:T(8,128)S(1)}, f32[128,256]{1,0:T(8,128)S(1)}, u32[]{:S(2)}, u32[]{:S(2)}) collective-permute-start(f32[128,256]{1,0:T(8,128)S(1)} %get-tuple-element.161), channel_id=1, source_target_pairs={{0,8},{2,10},{4,12},{6,14},{8,0},{10,2},{12,4},{14,6},{1,9},{3,11}... | collective-permute-start | bytes 393224 | tf_op jit(solution)/shard_map/ppermute | solution.py:382
  96.2 7.3 %collective-permute-start.23 = (f32[256,256]{1,0:T(8,128)S(1)}, f32[256,256]{1,0:T(8,128)S(1)}, u32[]{:S(2)}, u32[]{:S(2)}) collective-permute-start(f32[256,256]{1,0:T(8,128)S(1)} %get-tuple-element.151), channel_id=1, source_target_pairs={{0,1},{1,0},{2,3},{3,2},{4,5},{5,4},{6,7},{7,6},{8,9},{9,8},{10,11... | collective-permute-start | bytes 786440 | tf_op jit(solution)/shard_map/ppermute | solution.py:382
  96.7 8.9 %collective-permute-start.24 = (f32[128,256]{1,0:T(8,128)S(1)}, f32[128,256]{1,0:T(8,128)S(1)}, u32[]{:S(2)}, u32[]{:S(2)}) collective-permute-start(f32[128,256]{1,0:T(8,128)S(1)} %get-tuple-element.159), channel_id=1, source_target_pairs={{0,8},{2,10},{4,12},{6,14},{8,0},{10,2},{12,4},{14,6},{1,9},{3,11}... | collective-permute-start | bytes 393224 | tf_op jit(solution)/shard_map/ppermute | solution.py:382
  99.5 15.4 %collective-permute-start.17 = (f32[128,1024]{1,0:T(8,128)S(1)}, f32[128,1024]{1,0:T(8,128)S(1)}, u32[]{:S(2)}, u32[]{:S(2)}) collective-permute-start(f32[128,1024]{1,0:T(8,128)S(1)} %get-tuple-element.135), channel_id=1, source_target_pairs={{0,2},{2,0},{4,6},{6,4},{8,10},{10,8},{12,14},{14,12},{1,3},{3,1},... | collective-permute-start | bytes 1572872 | tf_op jit(solution)/shard_map/ppermute | solution.py:469
  103.6 11.1 %collective-permute-start.26 = (f32[128,256]{1,0:T(8,128)S(1)}, f32[128,256]{1,0:T(8,128)S(1)}, u32[]{:S(2)}, u32[]{:S(2)}) collective-permute-start(f32[128,256]{1,0:T(8,128)S(1)} %get-tuple-element.155), channel_id=1, source_target_pairs={{0,8},{2,10},{4,12},{6,14},{8,0},{10,2},{12,4},{14,6},{1,9},{3,11}... | collective-permute-start | bytes 393224 | tf_op jit(solution)/shard_map/ppermute | solution.py:382
  105.6 9.0 %collective-permute-start.25 = (f32[128,256]{1,0:T(8,128)S(1)}, f32[128,256]{1,0:T(8,128)S(1)}, u32[]{:S(2)}, u32[]{:S(2)}) collective-permute-start(f32[128,256]{1,0:T(8,128)S(1)} %get-tuple-element.157), channel_id=1, source_target_pairs={{0,8},{2,10},{4,12},{6,14},{8,0},{10,2},{12,4},{14,6},{1,9},{3,11}... | collective-permute-start | bytes 393224 | tf_op jit(solution)/shard_map/ppermute | solution.py:382
  114.8 2.0 %collective-permute-start.27 = (f32[512,256]{1,0:T(8,128)S(1)}, f32[512,256]{1,0:T(8,128)S(1)}, u32[]{:S(2)}, u32[]{:S(2)}) collective-permute-start(f32[512,256]{1,0:T(8,128)S(1)} %get-tuple-element.171), channel_id=1, source_target_pairs={{0,2},{2,0},{4,6},{6,4},{8,10},{10,8},{12,14},{14,12},{1,3},{3,1},... | collective-permute-start | bytes 1572872 | tf_op jit(solution)/shard_map/ppermute | solution.py:390

commit v3 on v2

--- a/solution.py
+++ b/solution.py
@@ -9,7 +9,9 @@
 from jax.sharding import PartitionSpec as P
 
 H = 8
-LAG, WINDOW, AHEAD = 2.5, 2, 2
+WINDOW, AHEAD = 3, 2
+LAG = 1.5
+WIDTHS = ((256, 256), (512,), (512,), (256, 256))
 EPSILON = 1e-05
 PIECES = 4
 F32, BF16 = jnp.float32, jnp.bfloat16
@@ -131,29 +133,39 @@
     stats_out[...] = jnp.where(lane == 0, squares, cross)
 
 
-def norm_body(rows, size, width, info, q, mixed, back, mine, other, normed_out, d_out, state_out):
-    total = mine[...] + across(other, rows)
-    squares, cross = total[:, 0:1], total[:, 1:2]
+def norm_body(rows, size, pairs, n_dp, factor, info, q, k, v, mixed, back, mine, other, carried, r0, r1, *refs):
+    normed_out, d_out, state_out, dq_out, scores_out = refs[:5]
+    outs, total = refs[5:-1], refs[-1]
+    width = 2 * mixed.shape[1]
+    sums = mine[...] + across(other, rows)
+    squares, cross = sums[:, 0:1], sums[:, 1:2]
     scale = jnp.sqrt(squares * (1.0 / width) + EPSILON)
     normed = mixed[...] / scale
     normed_out[...] = normed.astype(BF16).astype(F32)
     mean = cross / scale * (1.0 / width)
     d_mixed = ((back[...] - normed * mean) / scale).astype(BF16)
     d_out[...] = d_mixed
-    for h in range(q.shape[1] // size):
-        state_out[h * size : (h + 1) * size] = dot(head(q, h, size), head(d_mixed, h, size), (0, 0))
-
-
-def back_query_body(rows, size, info, k, v, d_mixed, carried, dq_out, scores_out):
-    mask = causal(info, rows, k.shape[0])
-    for h in range(k.shape[1] // size):
+    mask = causal(info, rows, q.shape[0])
+    heads = q.shape[1] // size
+    states = []
+    for h in range(heads):
         at = slice(h * size, (h + 1) * size)
         d_head = d_mixed[:, at]
+        states.append(dot(q[:, at], d_head, (0, 0)))
         scores = dot(d_head, v[:, at], (1, 1))
         scores = jnp.where(mask, scores, 0.0).astype(BF16)
+        scores_out[h] = scores
         state = carried[at].astype(BF16)
-        scores_out[h] = scores
         dq_out[:, at] = (dot(scores, k[:, at]) + dot(d_head, state, (1, 1))).astype(BF16)
+    for h in range(heads // 2):
+        state_out[h * size : (h + 1) * size] = jnp.where(
+            info[3] == 0, states[h], states[heads // 2 + h]
+        )
+    half = r0.shape[0]
+    total[...] = (
+        dot(r0[...], dq_out[:half], (0, 0)) + dot(r1[...], dq_out[half:], (0, 0))
+    ) * factor
+    split_rows(info, pairs, n_dp, total, *outs)
 
 
 def back_rest_body(size, info, q, d_mixed, attn, scores, dk_out, dv_out):
@@ -163,17 +175,19 @@
         dv_out[:, at] = dot(attn[h], d_mixed[:, at], (0, 0))
 
 
-def finish_body(size, info, k, v, later, dk_in, dv_in, dk_out, dv_out):
-    for h in range(k.shape[1] // size):
+def finish_body(size, info, k, v, later, later_other, dk_in, dv_in, dk_out, dv_out):
+    heads = k.shape[1] // size
+    for h in range(heads):
         at = slice(h * size, (h + 1) * size)
-        state = later[at].astype(BF16)
+        half = slice(h % (heads // 2) * size, (h % (heads // 2) + 1) * size)
+        is_mine = info[3] == h // (heads // 2)
+        state = jnp.where(is_mine, later[half], later_other[half]).astype(BF16)
         dk_out[:, at] = (dk_in[:, at] + dot(v[:, at], state, (1, 1))).astype(BF16)
         dv_out[:, at] = (dv_in[:, at] + dot(k[:, at], state)).astype(BF16)
 
 
 def split_rows(info, pairs, n_dp, total, *outs):
     keep_outs, send_outs = outs[: len(outs) // 2], outs[len(outs) // 2 :]
-    columns = keep_outs[0].shape[1]
     kept = keep_outs[0].shape[0]
     block = total.shape[0] // (pairs * 2 * n_dp)
     seq, place = info[0], info[1]
@@ -185,8 +199,10 @@
         at = slot * block
         targets = keep_outs if at < kept else send_outs
         at = at % kept
-        for chunk, target in enumerate(targets):
-            target[at : at + block] = total[rows, chunk * columns : (chunk + 1) * columns]
+        start = 0
+        for target in targets:
+            target[at : at + block] = total[rows, start : start + target.shape[1]]
+            start += target.shape[1]
 
 
 def grad_body(pairs, n_dp, factor, info, r0, r1, grad, *outs):
@@ -236,14 +252,15 @@
     other_out[...] = total[rows:]
 
 
-def assemble_body(width, chunks, order, info, *refs):
+def assemble_body(width, starts, info, *refs):
     pieces, others, out = refs[:-2], refs[-2], refs[-1]
-    rows, block = pieces[0].shape
-    for at, ref in enumerate(pieces):
-        start = order[at // chunks] * width + at % chunks * block
-        for core, part in ((info[2], ref[...]), (1 - info[2], others[at * rows : (at + 1) * rows])):
-            column = pl.multiple_of(start + core * (width // 2), block)
-            out[:, pl.ds(column, block)] = part
+    at = 0
+    for start, ref in zip(starts, pieces):
+        columns = ref.shape[1]
+        for core, part in ((info[2], ref[...]), (1 - info[2], others[:, at : at + columns])):
+            column = pl.multiple_of(start + core * (width // 2), 128)
+            out[:, pl.ds(column, columns)] = part
+        at += columns
 
 
 def after(value, *others):
@@ -307,7 +324,7 @@
         name="inside",
         flops=4 * 4 * count * count * size,
     )
-    cot2 = after(cot2, carried, inner)
+    cot2 = after(cot2, carried)
     cot3 = swap(cot2, perm=core_links)
     cot_all, back = call(
         cotangent_body,
@@ -327,30 +344,30 @@
         flops=2 * count * half * size,
     )
     stats_other = swap(stats, perm=core_links)
-    normed, d_mixed, own_back = call(
-        functools.partial(norm_body, rows, size, width),
+    factor = 1.0 / math.sqrt(clip_count * n_dp * rows * n_seq)
+    chunk_shapes = [
+        [((half // 2, columns), F32) for columns in widths] * 2 for widths in WIDTHS
+    ]
+    scratch = [pltpu.VMEM((half, half), F32)]
+    grad_flops = 2 * count * half * half
+    normed, d_mixed, own_back, dq, back_scores, *parts_q = call(
+        functools.partial(norm_body, rows, size, pairs, n_dp, factor),
         info,
-        [(wide, F32), (wide, BF16), ((half, size), F32)],
-        [q, mixed, back, stats, stats_other],
+        [
+            (wide, F32),
+            (wide, BF16),
+            ((half // 2, size), F32),
+            (wide, BF16),
+            ((H // 2, count, count), BF16),
+            *chunk_shapes[0],
+        ],
+        [q, k, v, mixed, back, stats, stats_other, carried, rows0, rows1],
+        scratch,
         name="norm",
         flops=2 * count * half * size,
     )
     later = shift(own_back, False)
     normed_other = swap(normed, perm=core_links)
-    dq, back_scores = call(
-        functools.partial(back_query_body, rows, size),
-        info,
-        [(wide, BF16), ((H // 2, count, count), BF16)],
-        [k, v, d_mixed, carried],
-        name="back_query",
-        flops=4 * 4 * count * count * size,
-    )
-
-    factor = 1.0 / math.sqrt(clip_count * n_dp * rows * n_seq)
-    chunks = 2
-    chunk = [((half // 2, half // chunks), F32)] * (2 * chunks)
-    scratch = [pltpu.VMEM((half, half), F32)]
-    grad_flops = 2 * count * half * half
 
     hops = []
     bit = n_dp // 2
@@ -363,17 +380,19 @@
         bit //= 2
 
     def reduce_all(tensors, fillers):
-        total_chunks = len(tensors) * chunks
-        keeps, sends, made = {}, {}, {}
-        steps = [(p + LAG * hop, hop, p) for p in range(total_chunks) for hop in range(len(hops))]
+        owner = [n for n, widths in enumerate(WIDTHS) for _ in widths]
+        first = [owner.index(n) for n in range(len(tensors))]
+        keeps, sends, made = {}, {}, set()
+        steps = [(p + LAG * hop, hop, p) for p in range(len(owner)) for hop in range(len(hops))]
         last, first_hop = None, {}
         for at, (_, hop, p) in enumerate(sorted(steps)):
             for n in range(len(tensors)):
-                if n not in made and chunks * n <= (p if hop == 0 else 0) + AHEAD:
-                    made[n] = tensors[n](last)
-                    for c in range(chunks):
-                        keeps[n * chunks + c] = made[n][c]
-                        sends[n * chunks + c] = made[n][chunks + c]
+                if n not in made and first[n] <= (p if hop == 0 else 0) + AHEAD:
+                    made.add(n)
+                    parts = tensors[n](last)
+                    for c in range(len(parts) // 2):
+                        keeps[first[n] + c] = parts[c]
+                        sends[first[n] + c] = parts[len(parts) // 2 + c]
             axis, links = hops[hop]
             if hop == 0 and p - WINDOW in first_hop:
                 sends[p] = after(sends[p], first_hop[p - WINDOW])
@@ -386,14 +405,15 @@
                 first_hop[p] = total
             middle = total.shape[0] // 2
             keeps[p], sends[p] = total[:middle], total[middle:]
-        out = [keeps[p] for p in range(total_chunks)]
-        return out, swap(jnp.concatenate([sends[p] for p in range(total_chunks)]), perm=core_links)
-
-    def weight_grad(grad, name):
+        chunks = range(len(owner))
+        sent = jnp.concatenate([sends[p] for p in chunks], axis=1)
+        return [keeps[p] for p in chunks], swap(sent, perm=core_links)
+
+    def weight_grad(grad, name, shapes):
         return call(
             functools.partial(grad_body, pairs, n_dp, factor),
             info,
-            chunk,
+            shapes,
             [rows0, rows1, grad],
             scratch,
             name=name,
@@ -403,13 +423,13 @@
     results = {}
 
     def grad_query(last):
-        return weight_grad(dq, "grad_q")
+        return parts_q
 
     def grad_output(last):
         return call(
             functools.partial(grad_out_body, rows, pairs, n_dp, factor),
             info,
-            chunk,
+            chunk_shapes[1],
             [normed, normed_other, (cot_all, (count, half), columns)],
             scratch,
             name="grad_o",
@@ -425,19 +445,20 @@
             name="back_rest",
             flops=4 * 4 * count * count * size,
         )
+        late = after(later, last)
         results["dk"], results["dv"] = call(
             functools.partial(finish_body, size),
             info,
             [(wide, BF16)] * 2,
-            [k, v, after(later, last), dk_inner, dv_inner],
+            [k, v, late, swap(late, perm=chip_links), dk_inner, dv_inner],
             name="finish",
             flops=4 * count * half * size,
         )
-        results["key"] = weight_grad(results["dk"], "grad_k")
+        results["key"] = weight_grad(results["dk"], "grad_k", chunk_shapes[2])
         return results["key"]
 
     def grad_value(last):
-        return weight_grad(after(results["dv"], results["key"][0]), "grad_v")
+        return weight_grad(after(results["dv"], results["key"][0]), "grad_v", chunk_shapes[3])
 
 
     def attend(last):
@@ -467,8 +488,11 @@
     )
     attended, mine, other = results["attended"], results["mine"], results["other"]
     d_tokens = (mine + swap(other, perm=core_links)).astype(BF16)
+    starts = []
+    for tensor, widths in zip((0, 3, 1, 2), WIDTHS):
+        starts += [tensor * width + sum(widths[:c]) for c in range(len(widths))]
     (grads,) = call(
-        functools.partial(assemble_body, width, chunks, (0, 3, 1, 2)),
+        functools.partial(assemble_body, width, starts),
         info,
         [((width // (n_seq * n_dp), 4 * width), F32)],
         own + [other_core],

time: 119 us -> 116 us (0.975)
  starting transfers between devices: 33.3 us -> 30 us
  waiting for transfers between devices: 52.4 us -> 54.9 us
  Pallas kernels: 23.3 us -> 21.9 us
    ppermute x16 -> x12, waiting for transfers between devices: 25.2 us -> 33.4 us  [reduce_all(): got = lax.ppermute(sends[p], axis, links)]
    ppermute x2, waiting for transfers between devices: 13.8 us -> 8.25 us  [shift(): got = swap(value, perm=links)]
    ppermute x16 -> x12, starting transfers between devices: 21.6 us -> 17.6 us  [reduce_all(): got = lax.ppermute(sends[p], axis, links)]
    ppermute x1, waiting for transfers between devices: 4.01 us -> 5.96 us  [local(): cot2 = swap(cot_f32, perm=chip_links)]
    ppermute x1, waiting for transfers between devices: 1.9 us -> 0.01 us  [local(): cot3 = swap(cot2, perm=core_links)]
    pallas_call x16 -> x14, Pallas kernels: 23.3 us -> 21.9 us  [call(): pl.pallas_call(body, name=name, out_shape=shapes, grid_spec=pltpu.Prefetc...]
    unnamed x25 -> x23, local copies, waits for them, and re-layouts: 5.82 us -> 5.82 us
  transfers between devices with their start and end apart: 28 -> 25, of which waited for: 15 -> 13; matrix products, arithmetic and copies ran while one was open for 1% -> 1% of each run, Pallas kernels for 15% -> 13%
where the time goes in v3:
time: 116 us
  waiting for transfers between devices  54.9 us (47%)
  starting transfers between devices  30 us (26%)
  Pallas kernels  21.9 us (19%)
  local copies, waits for them, and re-layouts  5.97 us (5%)
  other arithmetic  2.31 us (2%)
    ppermute x12, waiting for transfers between devices, reduce_all(): got = lax.ppermute(sends[p], axis, links)  33.4 us
    pallas_call x14, Pallas kernels, call(): pl.pallas_call(body, name=name, out_shape=shapes, grid_spec=pltpu.Prefetc...  21.9 us
    ppermute x12, starting transfers between devices, reduce_all(): got = lax.ppermute(sends[p], axis, links)  17.6 us
    ppermute x2, waiting for transfers between devices, shift(): got = swap(value, perm=links)  8.25 us
    ppermute x2, starting transfers between devices, shift(): got = swap(value, perm=links)  6.15 us
    ppermute x1, waiting for transfers between devices, local(): cot2 = swap(cot_f32, perm=chip_links)  5.96 us
    unnamed x23, local copies, waits for them, and re-layouts  5.82 us
    ppermute x1, waiting for transfers between devices, local(): tok2 = swap(tok_f32, perm=chip_links)  4.9 us
  transfers between devices with their start and end apart: 25, of which 13 were waited for; matrix products, arithmetic and copies ran while one was open for 1% of the time, Pallas kernels for 13%

profile of v3, /device:TPU:0, one launch (start us, length us, event | category | flops | bytes accessed | tf_op | source)
XLA Modules:
  0.0 116.1 jit_solution(9242755118403136803)
XLA Ops:
  0.6 1.0 bitcast_convert_fusion
  2.1 2.6 %collective-permute-start.1 = (f32[128,1024]{1,0:T(8,128)S(1)}, f32[128,1024]{1,0:T(8,128)S(1)}, u32[]{:S(2)}, u32[]{:S(2)}) collective-permute-start(f32[128,1024]{1,0:T(8,128)S(1)} %bitcast_convert_fusion), channel_id=1, source_target_pairs={{0,4},{2,6},{4,0},{6,2},{8,12},{10,14},{12,8},{14,10},{1,5},{3,7},... | collective-permute-start | bytes 1572872 | tf_op jit(solution)/shard_map/ppermute | solution.py:300
  4.9 1.6 %copy-done = bf16[1024,1024]{1,0:T(8,128)(2,1)S(1)} copy-done((bf16[1024,1024]{1,0:T(8,128)(2,1)S(1)}, bf16[1024,1024]{1,0:T(8,128)(2,1)}, u32[]{:S(2)}) %copy-start) | copy-done | bytes 2097176
  6.5 1.6 %copy-done.2 = bf16[1024,1024]{1,0:T(8,128)(2,1)S(1)} copy-done((bf16[1024,1024]{1,0:T(8,128)(2,1)S(1)}, bf16[1024,1024]{1,0:T(8,128)(2,1)}, u32[]{:S(2)}) %copy-start.2) | copy-done | bytes 2097176
  8.1 1.6 %copy-done.4 = bf16[1024,1024]{1,0:T(8,128)(2,1)S(1)} copy-done((bf16[1024,1024]{1,0:T(8,128)(2,1)S(1)}, bf16[1024,1024]{1,0:T(8,128)(2,1)}, u32[]{:S(2)}) %copy-start.4) | copy-done | bytes 2097176
  9.7 0.9 copy-done.7
  10.6 1.8 %proj0.1 = (bf16[256,512]{1,0:T(8,128)(2,1)S(1)}, bf16[256,512]{1,0:T(8,128)(2,1)S(1)}, bf16[256,512]{1,0:T(8,128)(2,1)S(1)}, f32[512,128]{1,0:T(8,128)S(1)}, bf16[256,512]{1,0:T(8,128)(2,1)S(1)}) custom-call(s32[4]{0:T(128)S(1)} %pad_add_fusion.info, bf16[128,1024]{1,0:T(8,128)(2,1)S(1)} %bitcast.10, f32[128,1024]{1,0:T(8,128)S(1)} %collective-permute-done.second, ...), custom_call_target="tpu_custom_call" | custom-call | flops 1 | bytes 1 | tf_op jit(solution)/shard_map/proj0/pallas_call | solution.py:35
  12.4 4.9 %collective-permute-done.1.first = f32[128,1024]{1,0:T(8,128)S(1)} collective-permute-done((f32[128,1024]{1,0:T(8,128)S(1)}, f32[128,1024]{1,0:T(8,128)S(1)}, u32[]{:S(2)}, u32[]{:S(2)}) %collective-permute-start.1) | collective-permute-done | bytes 524320 | tf_op jit(solution)/shard_map/ppermute | solution.py:300
  17.4 1.8 %collective-permute-start.5 = (f32[128,1024]{1,0:T(8,128)S(1)}, f32[128,1024]{1,0:T(8,128)S(1)}, u32[]{:S(2)}, u32[]{:S(2)}) collective-permute-start(f32[128,1024]{1,0:T(8,128)S(1)} %convert_element_type.10), channel_id=1, source_target_pairs={{0,4},{2,6},{4,0},{6,2},{8,12},{10,14},{12,8},{14,10},{1,5},{3,7},... | collective-permute-start | bytes 1572872 | tf_op jit(solution)/shard_map/ppermute | solution.py:303
  19.2 1.8 %proj1.1 = (bf16[256,512]{1,0:T(8,128)(2,1)S(1)}, bf16[256,512]{1,0:T(8,128)(2,1)S(1)}, bf16[256,512]{1,0:T(8,128)(2,1)S(1)}, f32[512,128]{1,0:T(8,128)S(1)}, bf16[256,512]{1,0:T(8,128)(2,1)S(1)}) custom-call(s32[4]{0:T(128)S(1)} %pad_add_fusion.info, f32[128,1024]{1,0:T(8,128)S(1)} %collective-permute-done.1.first, ...), custom_call_target="tpu_custom_call" | custom-call | flops 1 | bytes 1 | tf_op jit(solution)/shard_map/proj1/pallas_call | solution.py:35
  21.1 4.7 %collective-permute-start.3 = (f32[512,128]{1,0:T(8,128)S(1)}, f32[512,128]{1,0:T(8,128)S(1)}, u32[]{:S(2)}, u32[]{:S(2)}) collective-permute-start(f32[512,128]{1,0:T(8,128)S(1)} %get-tuple-element.79), channel_id=1, source_target_pairs={{0,8},{2,10},{4,12},{6,14},{1,9},{3,11},{5,13},{7,15},{16,24},{18,... | collective-permute-start | bytes 786440 | tf_op jit(solution)/shard_map/ppermute | solution.py:293
  25.8 6.0 %collective-permute-done.5.c2 = f32[128,1024]{1,0:T(8,128)S(1)} collective-permute-done((f32[128,1024]{1,0:T(8,128)S(1)}, f32[128,1024]{1,0:T(8,128)S(1)}, u32[]{:S(2)}, u32[]{:S(2)}) %collective-permute-start.5) | collective-permute-done | bytes 524320 | tf_op jit(solution)/shard_map/ppermute | solution.py:303
  31.8 4.9 %collective-permute-done.3.carried = f32[512,128]{1,0:T(8,128)S(1)} collective-permute-done((f32[512,128]{1,0:T(8,128)S(1)}, f32[512,128]{1,0:T(8,128)S(1)}, u32[]{:S(2)}, u32[]{:S(2)}) %collective-permute-start.3) | collective-permute-done | bytes 262176 | tf_op jit(solution)/shard_map/ppermute | solution.py:293
  36.7 1.9 %inside.1 = (bf16[512,512]{1,0:T(8,128)(2,1)S(1)}, bf16[512,512]{1,0:T(8,128)(2,1)S(1)}, bf16[512,512]{1,0:T(8,128)(2,1)S(1)}, bf16[4,512,512]{2,1,0:T(8,128)(2,1)S(1)}, f32[512,512]{1,0:T(8,128)S(1)}) custom-call(s32[4]{0:T(128)S(1)} %pad_add_fusion.info, bf16[256,512]{1,0:T(8,128)(2,1)S(1)} %get-tuple-element.68.q0, ...), custom_call_target="tpu_custom_call" | custom-call | flops 1 | bytes 1 | tf_op jit(solution)/shard_map/inside/pallas_call | solution.py:35
  38.7 1.3 %cotangent.1 = (bf16[512,1024]{1,0:T(8,128)(2,1)S(1)}, f32[512,512]{1,0:T(8,128)S(1)}) custom-call(s32[4]{0:T(128)S(1)} %pad_add_fusion.info, bf16[128,1024]{1,0:T(8,128)(2,1)S(1)} %bitcast.12, f32[128,1024]{1,0:T(8,128)S(1)} %collective-permute-done.4.c1, f32[128,1024]{1,0:T(8,128)S(1)} %collective-permute-done.5.c2, ...), custom_call_target="tpu_custom_call" | custom-call | flops 1 | bytes 1 | tf_op jit(solution)/shard_map/cotangent/pallas_call | solution.py:35
  40.0 1.0 stats.1
  41.5 1.2 %collective-permute-done.7.other = f32[512,128]{1,0:T(8,128)S(1)} collective-permute-done((f32[512,128]{1,0:T(8,128)S(1)}, f32[512,128]{1,0:T(8,128)S(1)}, u32[]{:S(2)}, u32[]{:S(2)}) %collective-permute-start.7) | collective-permute-done | bytes 262176 | tf_op jit(solution)/shard_map/ppermute | solution.py:346
  42.7 3.2 %norm.1 = (f32[512,512]{1,0:T(8,128)S(1)}, bf16[512,512]{1,0:T(8,128)(2,1)S(1)}, f32[256,128]{1,0:T(8,128)S(1)}, bf16[512,512]{1,0:T(8,128)(2,1)S(1)}, bf16[4,51...) custom-call(s32[4]{0:T(128)S(1)} %pad_add_fusion.info, ...), custom_call_target="tpu_custom_call" | custom-call | flops 1 | bytes 1 | tf_op jit(solution)/shard_map/norm/pallas_call | solution.py:35
  46.3 1.5 %collective-permute-start.9 = (f32[256,256]{1,0:T(8,128)S(1)}, f32[256,256]{1,0:T(8,128)S(1)}, u32[]{:S(2)}, u32[]{:S(2)}) collective-permute-start(f32[256,256]{1,0:T(8,128)S(1)} %get-tuple-element.93), channel_id=1, source_target_pairs={{0,1},{1,0},{2,3},{3,2},{4,5},{5,4},{6,7},{7,6},{8,9},{9,8},{10,11... | collective-permute-start | bytes 786440 | tf_op jit(solution)/shard_map/ppermute | solution.py:401
  47.8 1.5 %collective-permute-start.13 = (f32[256,128]{1,0:T(8,128)S(1)}, f32[256,128]{1,0:T(8,128)S(1)}, u32[]{:S(2)}, u32[]{:S(2)}) collective-permute-start(f32[256,128]{1,0:T(8,128)S(1)} %get-tuple-element.102), channel_id=1, source_target_pairs={{8,0},{10,2},{12,4},{14,6},{9,1},{11,3},{13,5},{15,7},{24,16},{26,... | collective-permute-start | bytes 393224 | tf_op jit(solution)/shard_map/ppermute | solution.py:293
  49.3 0.6 collective-permute-start.10
  49.9 5.6 %collective-permute-done.9 = f32[256,256]{1,0:T(8,128)S(1)} collective-permute-done((f32[256,256]{1,0:T(8,128)S(1)}, f32[256,256]{1,0:T(8,128)S(1)}, u32[]{:S(2)}, u32[]{:S(2)}) %collective-permute-start.9) | collective-permute-done | bytes 262176 | tf_op jit(solution)/shard_map/ppermute | solution.py:401
  55.5 3.3 %collective-permute-done.13.later = f32[256,128]{1,0:T(8,128)S(1)} collective-permute-done((f32[256,128]{1,0:T(8,128)S(1)}, f32[256,128]{1,0:T(8,128)S(1)}, u32[]{:S(2)}, u32[]{:S(2)}) %collective-permute-start.13) | collective-permute-done | bytes 131104 | tf_op jit(solution)/shard_map/ppermute | solution.py:293
  58.8 1.2 %grad_o.1 = (f32[256,512]{1,0:T(8,128)S(1)}, f32[256,512]{1,0:T(8,128)S(1)}) custom-call(s32[4]{0:T(128)S(1)} %pad_add_fusion.info, f32[512,512]{1,0:T(8,128)S(1)} %get-tuple-element.100.mine, f32[512,512]{1,0:T(8,128)S(1)} %collective-permute-done.8.other, bf16[512,1024]{1,0:T(8,128)(2,1)S(1)} %get-tuple-element.90.cot), custom_call_target="tpu_custom_call" | custom-call | flops 1 | bytes 1 | tf_op jit(solution)/shard_map/grad_o/pallas_call | solution.py:35
  60.0 0.6 collective-permute-start.12
  60.6 3.2 %collective-permute-start.11 = (f32[128,256]{1,0:T(8,128)S(1)}, f32[128,256]{1,0:T(8,128)S(1)}, u32[]{:S(2)}, u32[]{:S(2)}) collective-permute-start(f32[128,256]{1,0:T(8,128)S(1)} %get-tuple-element.147), channel_id=1, source_target_pairs={{0,8},{2,10},{4,12},{6,14},{8,0},{10,2},{12,4},{14,6},{1,9},{3,11}... | collective-permute-start | bytes 393224 | tf_op jit(solution)/shard_map/ppermute | solution.py:401
  63.9 1.8 %back_rest.1 = (f32[512,512]{1,0:T(8,128)S(1)}, f32[512,512]{1,0:T(8,128)S(1)}) custom-call(s32[4]{0:T(128)S(1)} %pad_add_fusion.info, bf16[512,512]{1,0:T(8,128)(2,1)S(1)} %get-tuple-element.76.q, bf16[512,512]{1,0:T(8,128)(2,1)S(1)} %get-tuple-element.104.d_mixed, bf16[4,512,512]{2,1,0:T(8,128)(2,1)S(1)} %get-tuple-element.105.attn, ...), custom_call_target="tpu_custom_call" | custom-call | flops 1 | bytes 1 | tf_op jit(solution)/shard_map/back_rest/pallas_call | solution.py:35
  65.8 1.0 finish.1
  66.8 1.1 grad_k.1
  67.8 0.6 collective-permute-start.16
  68.5 1.4 %collective-permute-start.15 = (f32[128,256]{1,0:T(8,128)S(1)}, f32[128,256]{1,0:T(8,128)S(1)}, u32[]{:S(2)}, u32[]{:S(2)}) collective-permute-start(f32[128,256]{1,0:T(8,128)S(1)} %get-tuple-element.145), channel_id=1, source_target_pairs={{0,8},{2,10},{4,12},{6,14},{8,0},{10,2},{12,4},{14,6},{1,9},{3,11}... | collective-permute-start | bytes 393224 | tf_op jit(solution)/shard_map/ppermute | solution.py:401
  69.9 1.1 grad_v.1
  71.0 0.6 collective-permute-start.19
  71.6 3.4 %collective-permute-done.12 = f32[256,512]{1,0:T(8,128)S(1)} collective-permute-done((f32[256,512]{1,0:T(8,128)S(1)}, f32[256,512]{1,0:T(8,128)S(1)}, u32[]{:S(2)}, u32[]{:S(2)}) %collective-permute-start.12) | collective-permute-done | bytes 524320 | tf_op jit(solution)/shard_map/ppermute | solution.py:401
  75.0 1.7 %attended.1 = bf16[128,1024]{1,0:T(8,128)(2,1)} custom-call(s32[4]{0:T(128)S(1)} %pad_add_fusion.info, f32[512,512]{1,0:T(8,128)S(1)} %get-tuple-element.100.mine, f32[512,512]{1,0:T(8,128)S(1)} %collective-permute-done.8.other, bf16[1024,1024]{1,0:T(8,128)(2,1)S(1)} %copy-done.6), custom_call_target="tpu_custom_call" | custom-call | flops 1 | bytes 1 | tf_op jit(solution)/shard_map/attended/pallas_call | solution.py:35
  76.8 2.3 %collective-permute-start.17 = (f32[128,512]{1,0:T(8,128)S(1)}, f32[128,512]{1,0:T(8,128)S(1)}, u32[]{:S(2)}, u32[]{:S(2)}) collective-permute-start(f32[128,512]{1,0:T(8,128)S(1)} %get-tuple-element.135), channel_id=1, source_target_pairs={{0,8},{2,10},{4,12},{6,14},{8,0},{10,2},{12,4},{14,6},{1,9},{3,11}... | collective-permute-start | bytes 786440 | tf_op jit(solution)/shard_map/ppermute | solution.py:401
  79.1 7.1 %collective-permute-done.16 = f32[256,512]{1,0:T(8,128)S(1)} collective-permute-done((f32[256,512]{1,0:T(8,128)S(1)}, f32[256,512]{1,0:T(8,128)S(1)}, u32[]{:S(2)}, u32[]{:S(2)}) %collective-permute-start.16) | collective-permute-done | bytes 524320 | tf_op jit(solution)/shard_map/ppermute | solution.py:401
  86.3 2.3 %collective-permute-start.20 = (f32[128,512]{1,0:T(8,128)S(1)}, f32[128,512]{1,0:T(8,128)S(1)}, u32[]{:S(2)}, u32[]{:S(2)}) collective-permute-start(f32[128,512]{1,0:T(8,128)S(1)} %get-tuple-element.133), channel_id=1, source_target_pairs={{0,8},{2,10},{4,12},{6,14},{8,0},{10,2},{12,4},{14,6},{1,9},{3,11}... | collective-permute-start | bytes 786440 | tf_op jit(solution)/shard_map/ppermute | solution.py:401
  88.6 1.6 %collective-permute-start.21 = (f32[256,256]{1,0:T(8,128)S(1)}, f32[256,256]{1,0:T(8,128)S(1)}, u32[]{:S(2)}, u32[]{:S(2)}) collective-permute-start(f32[256,256]{1,0:T(8,128)S(1)} %get-tuple-element.130), channel_id=1, source_target_pairs={{0,1},{1,0},{2,3},{3,2},{4,5},{5,4},{6,7},{7,6},{8,9},{9,8},{10,11... | collective-permute-start | bytes 786440 | tf_op jit(solution)/shard_map/ppermute | solution.py:401
  90.1 5.1 %collective-permute-done.17 = f32[128,512]{1,0:T(8,128)S(1)} collective-permute-done((f32[128,512]{1,0:T(8,128)S(1)}, f32[128,512]{1,0:T(8,128)S(1)}, u32[]{:S(2)}, u32[]{:S(2)}) %collective-permute-start.17) | collective-permute-done | bytes 262176 | tf_op jit(solution)/shard_map/ppermute | solution.py:401
  95.3 1.6 %d_tokens.1 = (f32[128,1024]{1,0:T(8,128)S(1)}, f32[128,1024]{1,0:T(8,128)S(1)}) custom-call(s32[4]{0:T(128)S(1)} %pad_add_fusion.info, bf16[512,512]{1,0:T(8,128)(2,1)S(1)} %get-tuple-element.117.dq, bf16[512,512]{1,0:T(8,128)(2,1)S(1)} %get-tuple-element.110.grad.dk, bf16[512,512]{1,0:T(8,128)(2,1)S(1)} %get-tuple-element.121.dv.grad, ...), custom_call_target="tpu_custom_call" | custom-call | flops 1 | bytes 1 | tf_op jit(solution)/shard_map/d_tokens/pallas_call | solution.py:35
  97.0 2.2 %collective-permute-done.20 = f32[128,512]{1,0:T(8,128)S(1)} collective-permute-done((f32[128,512]{1,0:T(8,128)S(1)}, f32[128,512]{1,0:T(8,128)S(1)}, u32[]{:S(2)}, u32[]{:S(2)}) %collective-permute-start.20) | collective-permute-done | bytes 262176 | tf_op jit(solution)/shard_map/ppermute | solution.py:401
  99.5 2.9 %collective-permute-start.23 = (f32[128,256]{1,0:T(8,128)S(1)}, f32[128,256]{1,0:T(8,128)S(1)}, u32[]{:S(2)}, u32[]{:S(2)}) collective-permute-start(f32[128,256]{1,0:T(8,128)S(1)} %get-tuple-element.141), channel_id=1, source_target_pairs={{0,8},{2,10},{4,12},{6,14},{8,0},{10,2},{12,4},{14,6},{1,9},{3,11}... | collective-permute-start | bytes 393224 | tf_op jit(solution)/shard_map/ppermute | solution.py:401
  102.4 8.2 %collective-permute-done.22 = f32[128,256]{1,0:T(8,128)S(1)} collective-permute-done((f32[128,256]{1,0:T(8,128)S(1)}, f32[128,256]{1,0:T(8,128)S(1)}, u32[]{:S(2)}, u32[]{:S(2)}) %collective-permute-start.22) | collective-permute-done | bytes 131104 | tf_op jit(solution)/shard_map/ppermute | solution.py:401
  110.6 1.9 %collective-permute-done.23 = f32[128,256]{1,0:T(8,128)S(1)} collective-permute-done((f32[128,256]{1,0:T(8,128)S(1)}, f32[128,256]{1,0:T(8,128)S(1)}, u32[]{:S(2)}, u32[]{:S(2)}) %collective-permute-start.23) | collective-permute-done | bytes 131104 | tf_op jit(solution)/shard_map/ppermute | solution.py:401
  112.6 0.8 fusion
  113.4 1.1 collective-permute-done.24.refs_6_
  114.5 1.6 %assemble.1 = f32[64,4096]{1,0:T(8,128)} custom-call(s32[4]{0:T(128)S(1)} %pad_add_fusion.info, f32[64,256]{1,0:T(8,128)S(1)} %get-tuple-element.156.refs_0_, f32[64,256]{1,0:T(8,128)S(1)} %get-tuple-element.154.refs_1_, f32[64,512]{1,0:T(8,128)S(1)} %get-tuple-element.140.refs_2_, f32[64,512]{1,0:T(8,128)S(1)} %get-tuple-element.138.refs_3_, ...), custom_call_target="tpu_custom_call" | custom-call | flops 1 | bytes 1 | tf_op jit(solution)/shard_map/assemble/pallas_call | solution.py:35
  (62 shorter events, 2.7 us)
Async XLA Ops:
  1.6 3.2 %collective-permute-start = (f32[128,1024]{1,0:T(8,128)S(1)}, f32[128,1024]{1,0:T(8,128)S(1)}, u32[]{:S(2)}, u32[]{:S(2)}) collective-permute-start(f32[128,1024]{1,0:T(8,128)S(1)} %bitcast_convert_fusion), channel_id=1, source_target_pairs={{0,2},{2,0},{4,6},{6,4},{8,10},{10,8},{12,14},{14,12},{1,3},{3,1},... | collective-permute-start | bytes 1572872 | tf_op jit(solution)/shard_map/ppermute | solution.py:301
  2.1 15.2 %collective-permute-start.1 = (f32[128,1024]{1,0:T(8,128)S(1)}, f32[128,1024]{1,0:T(8,128)S(1)}, u32[]{:S(2)}, u32[]{:S(2)}) collective-permute-start(f32[128,1024]{1,0:T(8,128)S(1)} %bitcast_convert_fusion), channel_id=1, source_target_pairs={{0,4},{2,6},{4,0},{6,2},{8,12},{10,14},{12,8},{14,10},{1,5},{3,7},... | collective-permute-start | bytes 1572872 | tf_op jit(solution)/shard_map/ppermute | solution.py:300
  4.9 1.6 %copy-start = (bf16[1024,1024]{1,0:T(8,128)(2,1)S(1)}, bf16[1024,1024]{1,0:T(8,128)(2,1)}, u32[]{:S(2)}) copy-start(bf16[1024,1024]{1,0:T(8,128)(2,1)} %w_q.5) | copy-start | bytes 6291460
  6.5 1.6 %copy-start.2 = (bf16[1024,1024]{1,0:T(8,128)(2,1)S(1)}, bf16[1024,1024]{1,0:T(8,128)(2,1)}, u32[]{:S(2)}) copy-start(bf16[1024,1024]{1,0:T(8,128)(2,1)} %w_k.5) | copy-start | bytes 6291460
  8.1 1.6 %copy-start.4 = (bf16[1024,1024]{1,0:T(8,128)(2,1)S(1)}, bf16[1024,1024]{1,0:T(8,128)(2,1)}, u32[]{:S(2)}) copy-start(bf16[1024,1024]{1,0:T(8,128)(2,1)} %w_v.5) | copy-start | bytes 6291460
  9.7 0.9 copy-start.7
  10.6 6.7 %copy-start.8 = (bf16[1,128,1024]{2,1,0:T(8,128)(2,1)S(1)}, bf16[1,128,1024]{2,1,0:T(8,128)(2,1)}, u32[]{:S(2)}) copy-start(bf16[1,128,1024]{2,1,0:T(8,128)(2,1)} %param.11) | copy-start | bytes 786436
  10.6 8.6 %copy-start.1 = (bf16[1024,1024]{1,0:T(8,128)(2,1)S(1)}, bf16[1024,1024]{1,0:T(8,128)(2,1)}, u32[]{:S(2)}) copy-start(bf16[1024,1024]{1,0:T(8,128)(2,1)} %w_q.5) | copy-start | bytes 6291460
  10.6 8.6 %copy-start.3 = (bf16[1024,1024]{1,0:T(8,128)(2,1)S(1)}, bf16[1024,1024]{1,0:T(8,128)(2,1)}, u32[]{:S(2)}) copy-start(bf16[1024,1024]{1,0:T(8,128)(2,1)} %w_k.5) | copy-start | bytes 6291460
  10.6 8.6 %copy-start.5 = (bf16[1024,1024]{1,0:T(8,128)(2,1)S(1)}, bf16[1024,1024]{1,0:T(8,128)(2,1)}, u32[]{:S(2)}) copy-start(bf16[1024,1024]{1,0:T(8,128)(2,1)} %w_v.5) | copy-start | bytes 6291460
  17.3 1.9 %collective-permute-start.2 = (f32[128,1024]{1,0:T(8,128)S(1)}, f32[128,1024]{1,0:T(8,128)S(1)}, u32[]{:S(2)}, u32[]{:S(2)}) collective-permute-start(f32[128,1024]{1,0:T(8,128)S(1)} %collective-permute-done.1.first), channel_id=1, source_target_pairs={{0,2},{2,0},{4,6},{6,4},{8,10},{10,8},{12,14},{14,12},{1,3},{3,1},... | collective-permute-start | bytes 1572872 | tf_op jit(solution)/shard_map/ppermute | solution.py:314
  17.4 14.4 %collective-permute-start.5 = (f32[128,1024]{1,0:T(8,128)S(1)}, f32[128,1024]{1,0:T(8,128)S(1)}, u32[]{:S(2)}, u32[]{:S(2)}) collective-permute-start(f32[128,1024]{1,0:T(8,128)S(1)} %convert_element_type.10), channel_id=1, source_target_pairs={{0,4},{2,6},{4,0},{6,2},{8,12},{10,14},{12,8},{14,10},{1,5},{3,7},... | collective-permute-start | bytes 1572872 | tf_op jit(solution)/shard_map/ppermute | solution.py:303
  19.2 19.4 %copy-start.6 = (bf16[1024,1024]{1,0:T(8,128)(2,1)S(1)}, bf16[1024,1024]{1,0:T(8,128)(2,1)}, u32[]{:S(2)}) copy-start(bf16[1024,1024]{1,0:T(8,128)(2,1)} %w_o.3) | copy-start | bytes 6291460
  21.1 15.7 %collective-permute-start.3 = (f32[512,128]{1,0:T(8,128)S(1)}, f32[512,128]{1,0:T(8,128)S(1)}, u32[]{:S(2)}, u32[]{:S(2)}) collective-permute-start(f32[512,128]{1,0:T(8,128)S(1)} %get-tuple-element.79), channel_id=1, source_target_pairs={{0,8},{2,10},{4,12},{6,14},{1,9},{3,11},{5,13},{7,15},{16,24},{18,... | collective-permute-start | bytes 786440 | tf_op jit(solution)/shard_map/ppermute | solution.py:293
  25.8 12.9 %collective-permute-start.4 = (f32[128,1024]{1,0:T(8,128)S(1)}, f32[128,1024]{1,0:T(8,128)S(1)}, u32[]{:S(2)}, u32[]{:S(2)}) collective-permute-start(f32[128,1024]{1,0:T(8,128)S(1)} %convert_element_type.10), channel_id=1, source_target_pairs={{0,2},{2,0},{4,6},{6,4},{8,10},{10,8},{12,14},{14,12},{1,3},{3,1},... | collective-permute-start | bytes 1572872 | tf_op jit(solution)/shard_map/ppermute | solution.py:304
  36.7 2.0 %collective-permute-start.6 = (f32[128,1024]{1,0:T(8,128)S(1)}, f32[128,1024]{1,0:T(8,128)S(1)}, u32[]{:S(2)}, u32[]{:S(2)}) collective-permute-start(f32[128,1024]{1,0:T(8,128)S(1)} %collective-permute-done.5.c2), channel_id=1, source_target_pairs={{0,2},{2,0},{4,6},{6,4},{8,10},{10,8},{12,14},{14,12},{1,3},{3,1},... | collective-permute-start | bytes 1572872 | tf_op jit(solution)/shard_map/ppermute | solution.py:328
  41.0 1.7 %collective-permute-start.7 = (f32[512,128]{1,0:T(8,128)S(1)}, f32[512,128]{1,0:T(8,128)S(1)}, u32[]{:S(2)}, u32[]{:S(2)}) collective-permute-start(f32[512,128]{1,0:T(8,128)S(1)} %get-tuple-element.86.mine), channel_id=1, source_target_pairs={{0,2},{2,0},{4,6},{6,4},{8,10},{10,8},{12,14},{14,12},{1,3},{3,1},... | collective-permute-start | bytes 786440 | tf_op jit(solution)/shard_map/ppermute | solution.py:346
  45.9 13.0 %collective-permute-start.8 = (f32[512,512]{1,0:T(8,128)S(1)}, f32[512,512]{1,0:T(8,128)S(1)}, u32[]{:S(2)}, u32[]{:S(2)}) collective-permute-start(f32[512,512]{1,0:T(8,128)S(1)} %get-tuple-element.100.mine), channel_id=1, source_target_pairs={{0,2},{2,0},{4,6},{6,4},{8,10},{10,8},{12,14},{14,12},{1,3},{3,1},... | collective-permute-start | bytes 3145736 | tf_op jit(solution)/shard_map/ppermute | solution.py:370
  46.3 9.2 %collective-permute-start.9 = (f32[256,256]{1,0:T(8,128)S(1)}, f32[256,256]{1,0:T(8,128)S(1)}, u32[]{:S(2)}, u32[]{:S(2)}) collective-permute-start(f32[256,256]{1,0:T(8,128)S(1)} %get-tuple-element.93), channel_id=1, source_target_pairs={{0,1},{1,0},{2,3},{3,2},{4,5},{5,4},{6,7},{7,6},{8,9},{9,8},{10,11... | collective-permute-start | bytes 786440 | tf_op jit(solution)/shard_map/ppermute | solution.py:401
  47.8 11.0 %collective-permute-start.13 = (f32[256,128]{1,0:T(8,128)S(1)}, f32[256,128]{1,0:T(8,128)S(1)}, u32[]{:S(2)}, u32[]{:S(2)}) collective-permute-start(f32[256,128]{1,0:T(8,128)S(1)} %get-tuple-element.102), channel_id=1, source_target_pairs={{8,0},{10,2},{12,4},{14,6},{9,1},{11,3},{13,5},{15,7},{24,16},{26,... | collective-permute-start | bytes 393224 | tf_op jit(solution)/shard_map/ppermute | solution.py:293
  49.3 14.6 %collective-permute-start.10 = (f32[256,256]{1,0:T(8,128)S(1)}, f32[256,256]{1,0:T(8,128)S(1)}, u32[]{:S(2)}, u32[]{:S(2)}) collective-permute-start(f32[256,256]{1,0:T(8,128)S(1)} %get-tuple-element.96), channel_id=1, source_target_pairs={{0,1},{1,0},{2,3},{3,2},{4,5},{5,4},{6,7},{7,6},{8,9},{9,8},{10,11... | collective-permute-start | bytes 786440 | tf_op jit(solution)/shard_map/ppermute | solution.py:401
  58.8 6.9 %collective-permute-start.14 = (f32[256,128]{1,0:T(8,128)S(1)}, f32[256,128]{1,0:T(8,128)S(1)}, u32[]{:S(2)}, u32[]{:S(2)}) collective-permute-start(f32[256,128]{1,0:T(8,128)S(1)} %collective-permute-done.13.later), channel_id=1, source_target_pairs={{0,4},{2,6},{4,0},{6,2},{8,12},{10,14},{12,8},{14,10},{1,5},{3,7},... | collective-permute-start | bytes 393224 | tf_op jit(solution)/shard_map/ppermute | solution.py:453
  60.0 14.9 %collective-permute-start.12 = (f32[256,512]{1,0:T(8,128)S(1)}, f32[256,512]{1,0:T(8,128)S(1)}, u32[]{:S(2)}, u32[]{:S(2)}) collective-permute-start(f32[256,512]{1,0:T(8,128)S(1)} %get-tuple-element.99), channel_id=1, source_target_pairs={{0,1},{1,0},{2,3},{3,2},{4,5},{5,4},{6,7},{7,6},{8,9},{9,8},{10,11... | collective-permute-start | bytes 1572872 | tf_op jit(solution)/shard_map/ppermute | solution.py:401
  60.6 9.2 %collective-permute-start.11 = (f32[128,256]{1,0:T(8,128)S(1)}, f32[128,256]{1,0:T(8,128)S(1)}, u32[]{:S(2)}, u32[]{:S(2)}) collective-permute-start(f32[128,256]{1,0:T(8,128)S(1)} %get-tuple-element.147), channel_id=1, source_target_pairs={{0,8},{2,10},{4,12},{6,14},{8,0},{10,2},{12,4},{14,6},{1,9},{3,11}... | collective-permute-start | bytes 393224 | tf_op jit(solution)/shard_map/ppermute | solution.py:401
  67.8 18.3 %collective-permute-start.16 = (f32[256,512]{1,0:T(8,128)S(1)}, f32[256,512]{1,0:T(8,128)S(1)}, u32[]{:S(2)}, u32[]{:S(2)}) collective-permute-start(f32[256,512]{1,0:T(8,128)S(1)} %get-tuple-element.115), channel_id=1, source_target_pairs={{0,1},{1,0},{2,3},{3,2},{4,5},{5,4},{6,7},{7,6},{8,9},{9,8},{10,11... | collective-permute-start | bytes 1572872 | tf_op jit(solution)/shard_map/ppermute | solution.py:401
  68.5 8.3 %collective-permute-start.15 = (f32[128,256]{1,0:T(8,128)S(1)}, f32[128,256]{1,0:T(8,128)S(1)}, u32[]{:S(2)}, u32[]{:S(2)}) collective-permute-start(f32[128,256]{1,0:T(8,128)S(1)} %get-tuple-element.145), channel_id=1, source_target_pairs={{0,8},{2,10},{4,12},{6,14},{8,0},{10,2},{12,4},{14,6},{1,9},{3,11}... | collective-permute-start | bytes 393224 | tf_op jit(solution)/shard_map/ppermute | solution.py:401
  71.0 26.0 %collective-permute-start.19 = (f32[256,256]{1,0:T(8,128)S(1)}, f32[256,256]{1,0:T(8,128)S(1)}, u32[]{:S(2)}, u32[]{:S(2)}) collective-permute-start(f32[256,256]{1,0:T(8,128)S(1)} %get-tuple-element.125), channel_id=1, source_target_pairs={{0,1},{1,0},{2,3},{3,2},{4,5},{5,4},{6,7},{7,6},{8,9},{9,8},{10,11... | collective-permute-start | bytes 786440 | tf_op jit(solution)/shard_map/ppermute | solution.py:401
  76.8 18.5 %collective-permute-start.17 = (f32[128,512]{1,0:T(8,128)S(1)}, f32[128,512]{1,0:T(8,128)S(1)}, u32[]{:S(2)}, u32[]{:S(2)}) collective-permute-start(f32[128,512]{1,0:T(8,128)S(1)} %get-tuple-element.135), channel_id=1, source_target_pairs={{0,8},{2,10},{4,12},{6,14},{8,0},{10,2},{12,4},{14,6},{1,9},{3,11}... | collective-permute-start | bytes 786440 | tf_op jit(solution)/shard_map/ppermute | solution.py:401
  86.3 12.9 %collective-permute-start.20 = (f32[128,512]{1,0:T(8,128)S(1)}, f32[128,512]{1,0:T(8,128)S(1)}, u32[]{:S(2)}, u32[]{:S(2)}) collective-permute-start(f32[128,512]{1,0:T(8,128)S(1)} %get-tuple-element.133), channel_id=1, source_target_pairs={{0,8},{2,10},{4,12},{6,14},{8,0},{10,2},{12,4},{14,6},{1,9},{3,11}... | collective-permute-start | bytes 786440 | tf_op jit(solution)/shard_map/ppermute | solution.py:401
  88.6 10.7 %collective-permute-start.21 = (f32[256,256]{1,0:T(8,128)S(1)}, f32[256,256]{1,0:T(8,128)S(1)}, u32[]{:S(2)}, u32[]{:S(2)}) collective-permute-start(f32[256,256]{1,0:T(8,128)S(1)} %get-tuple-element.130), channel_id=1, source_target_pairs={{0,1},{1,0},{2,3},{3,2},{4,5},{5,4},{6,7},{7,6},{8,9},{9,8},{10,11... | collective-permute-start | bytes 786440 | tf_op jit(solution)/shard_map/ppermute | solution.py:401
  96.9 15.7 %collective-permute-start.18 = (f32[128,1024]{1,0:T(8,128)S(1)}, f32[128,1024]{1,0:T(8,128)S(1)}, u32[]{:S(2)}, u32[]{:S(2)}) collective-permute-start(f32[128,1024]{1,0:T(8,128)S(1)} %get-tuple-element.120), channel_id=1, source_target_pairs={{0,2},{2,0},{4,6},{6,4},{8,10},{10,8},{12,14},{14,12},{1,3},{3,1},... | collective-permute-start | bytes 1572872 | tf_op jit(solution)/shard_map/ppermute | solution.py:490
  99.4 11.2 %collective-permute-start.22 = (f32[128,256]{1,0:T(8,128)S(1)}, f32[128,256]{1,0:T(8,128)S(1)}, u32[]{:S(2)}, u32[]{:S(2)}) collective-permute-start(f32[128,256]{1,0:T(8,128)S(1)} %get-tuple-element.143), channel_id=1, source_target_pairs={{0,8},{2,10},{4,12},{6,14},{8,0},{10,2},{12,4},{14,6},{1,9},{3,11}... | collective-permute-start | bytes 393224 | tf_op jit(solution)/shard_map/ppermute | solution.py:401
  99.5 13.0 %collective-permute-start.23 = (f32[128,256]{1,0:T(8,128)S(1)}, f32[128,256]{1,0:T(8,128)S(1)}, u32[]{:S(2)}, u32[]{:S(2)}) collective-permute-start(f32[128,256]{1,0:T(8,128)S(1)} %get-tuple-element.141), channel_id=1, source_target_pairs={{0,8},{2,10},{4,12},{6,14},{8,0},{10,2},{12,4},{14,6},{1,9},{3,11}... | collective-permute-start | bytes 393224 | tf_op jit(solution)/shard_map/ppermute | solution.py:401
  112.5 2.0 %collective-permute-start.24 = (f32[64,2048]{1,0:T(8,128)S(1)}, f32[64,2048]{1,0:T(8,128)S(1)}, u32[]{:S(2)}, u32[]{:S(2)}) collective-permute-start(f32[64,2048]{1,0:T(8,128)S(1)} %get-tuple-element.149), channel_id=1, source_target_pairs={{0,2},{2,0},{4,6},{6,4},{8,10},{10,8},{12,14},{14,12},{1,3},{3,1},... | collective-permute-start | bytes 1572872 | tf_op jit(solution)/shard_map/ppermute | solution.py:410

commit v4 on v3

--- a/solution.py
+++ b/solution.py
@@ -10,6 +10,7 @@
 
 H = 8
 WINDOW, AHEAD = 3, 2
+LATE = -1
 LAG = 1.5
 WIDTHS = ((256, 256), (512,), (512,), (256, 256))
 EPSILON = 1e-05
@@ -253,10 +254,13 @@
 
 
 def assemble_body(width, starts, info, *refs):
-    pieces, others, out = refs[:-2], refs[-2], refs[-1]
+    pieces, (early, late), out = refs[:-3], refs[-3:-1], refs[-1]
     at = 0
-    for start, ref in zip(starts, pieces):
+    for n, (start, ref) in enumerate(zip(starts, pieces)):
         columns = ref.shape[1]
+        others = early if n < len(pieces) + LATE else late
+        if n == len(pieces) + LATE:
+            at = 0
         for core, part in ((info[2], ref[...]), (1 - info[2], others[:, at : at + columns])):
             column = pl.multiple_of(start + core * (width // 2), 128)
             out[:, pl.ds(column, columns)] = part
@@ -406,8 +410,11 @@
             middle = total.shape[0] // 2
             keeps[p], sends[p] = total[:middle], total[middle:]
         chunks = range(len(owner))
-        sent = jnp.concatenate([sends[p] for p in chunks], axis=1)
-        return [keeps[p] for p in chunks], swap(sent, perm=core_links)
+        sent = [
+            swap(jnp.concatenate([sends[p] for p in group], axis=1), perm=core_links)
+            for group in (chunks[:LATE], chunks[LATE:])
+        ]
+        return [keeps[p] for p in chunks], sent
 
     def weight_grad(grad, name, shapes):
         return call(
@@ -484,7 +491,7 @@
         return results["mine"]
 
     own, other_core = reduce_all(
-        [grad_query, grad_output, grad_key, grad_value], {4: attend, 7: back_tokens}
+        [grad_query, grad_output, grad_key, grad_value], {3: attend, 6: back_tokens}
     )
     attended, mine, other = results["attended"], results["mine"], results["other"]
     d_tokens = (mine + swap(other, perm=core_links)).astype(BF16)
@@ -495,7 +502,7 @@
         functools.partial(assemble_body, width, starts),
         info,
         [((width // (n_seq * n_dp), 4 * width), F32)],
-        own + [other_core],
+        own + other_core,
         name="assemble",
     )
     return (

time: 116 us -> 114 us (0.983)
  waiting for transfers between devices: 54.9 us -> 53.2 us
    unnamed x23 -> x22, local copies, waits for them, and re-layouts: 5.82 us -> 5.81 us
  transfers between devices with their start and end apart: 25 -> 26, of which waited for: 13 -> 13; matrix products, arithmetic and copies ran while one was open for 1% -> 1% of each run, Pallas kernels for 13% -> 13%
where the time goes in v4:
time: 114 us
  waiting for transfers between devices  53.2 us (47%)
  starting transfers between devices  29.3 us (26%)
  Pallas kernels  21.9 us (19%)
  local copies, waits for them, and re-layouts  5.98 us (5%)
  other arithmetic  2.31 us (2%)
    ppermute x12, waiting for transfers between devices, reduce_all(): got = lax.ppermute(sends[p], axis, links)  32.4 us
    pallas_call x14, Pallas kernels, call(): pl.pallas_call(body, name=name, out_shape=shapes, grid_spec=pltpu.Prefetc...  21.9 us
    ppermute x12, starting transfers between devices, reduce_all(): got = lax.ppermute(sends[p], axis, links)  16.9 us
    ppermute x2, waiting for transfers between devices, shift(): got = swap(value, perm=links)  8.25 us
    ppermute x2, starting transfers between devices, shift(): got = swap(value, perm=links)  6.15 us
    ppermute x1, waiting for transfers between devices, local(): cot2 = swap(cot_f32, perm=chip_links)  5.96 us
    unnamed x22, local copies, waits for them, and re-layouts  5.81 us
    ppermute x1, waiting for transfers between devices, local(): tok2 = swap(tok_f32, perm=chip_links)  4.9 us
  transfers between devices with their start and end apart: 26, of which 13 were waited for; matrix products, arithmetic and copies ran while one was open for 1% of the time, Pallas kernels for 13%

profile of v4, /device:TPU:0, one launch (start us, length us, event | category | flops | bytes accessed | tf_op | source)
XLA Modules:
  0.0 113.7 jit_solution(17518209942669442209)
XLA Ops:
  0.6 1.0 bitcast_convert_fusion
  2.1 2.6 %collective-permute-start.1 = (f32[128,1024]{1,0:T(8,128)S(1)}, f32[128,1024]{1,0:T(8,128)S(1)}, u32[]{:S(2)}, u32[]{:S(2)}) collective-permute-start(f32[128,1024]{1,0:T(8,128)S(1)} %bitcast_convert_fusion), channel_id=1, source_target_pairs={{0,4},{2,6},{4,0},{6,2},{8,12},{10,14},{12,8},{14,10},{1,5},{3,7},... | collective-permute-start | bytes 1572872 | tf_op jit(solution)/shard_map/ppermute | solution.py:304
  4.9 1.6 %copy-done = bf16[1024,1024]{1,0:T(8,128)(2,1)S(1)} copy-done((bf16[1024,1024]{1,0:T(8,128)(2,1)S(1)}, bf16[1024,1024]{1,0:T(8,128)(2,1)}, u32[]{:S(2)}) %copy-start) | copy-done | bytes 2097176
  6.5 1.6 %copy-done.2 = bf16[1024,1024]{1,0:T(8,128)(2,1)S(1)} copy-done((bf16[1024,1024]{1,0:T(8,128)(2,1)S(1)}, bf16[1024,1024]{1,0:T(8,128)(2,1)}, u32[]{:S(2)}) %copy-start.2) | copy-done | bytes 2097176
  8.1 1.6 %copy-done.4 = bf16[1024,1024]{1,0:T(8,128)(2,1)S(1)} copy-done((bf16[1024,1024]{1,0:T(8,128)(2,1)S(1)}, bf16[1024,1024]{1,0:T(8,128)(2,1)}, u32[]{:S(2)}) %copy-start.4) | copy-done | bytes 2097176
  9.7 0.9 copy-done.7
  10.6 1.8 %proj0.1 = (bf16[256,512]{1,0:T(8,128)(2,1)S(1)}, bf16[256,512]{1,0:T(8,128)(2,1)S(1)}, bf16[256,512]{1,0:T(8,128)(2,1)S(1)}, f32[512,128]{1,0:T(8,128)S(1)}, bf16[256,512]{1,0:T(8,128)(2,1)S(1)}) custom-call(s32[4]{0:T(128)S(1)} %pad_add_fusion.info, bf16[128,1024]{1,0:T(8,128)(2,1)S(1)} %bitcast.10, f32[128,1024]{1,0:T(8,128)S(1)} %collective-permute-done.second, ...), custom_call_target="tpu_custom_call" | custom-call | flops 1 | bytes 1 | tf_op jit(solution)/shard_map/proj0/pallas_call | solution.py:36
  12.4 4.9 %collective-permute-done.1.first = f32[128,1024]{1,0:T(8,128)S(1)} collective-permute-done((f32[128,1024]{1,0:T(8,128)S(1)}, f32[128,1024]{1,0:T(8,128)S(1)}, u32[]{:S(2)}, u32[]{:S(2)}) %collective-permute-start.1) | collective-permute-done | bytes 524320 | tf_op jit(solution)/shard_map/ppermute | solution.py:304
  17.4 1.8 %collective-permute-start.5 = (f32[128,1024]{1,0:T(8,128)S(1)}, f32[128,1024]{1,0:T(8,128)S(1)}, u32[]{:S(2)}, u32[]{:S(2)}) collective-permute-start(f32[128,1024]{1,0:T(8,128)S(1)} %convert_element_type.10), channel_id=1, source_target_pairs={{0,4},{2,6},{4,0},{6,2},{8,12},{10,14},{12,8},{14,10},{1,5},{3,7},... | collective-permute-start | bytes 1572872 | tf_op jit(solution)/shard_map/ppermute | solution.py:307
  19.2 1.8 %proj1.1 = (bf16[256,512]{1,0:T(8,128)(2,1)S(1)}, bf16[256,512]{1,0:T(8,128)(2,1)S(1)}, bf16[256,512]{1,0:T(8,128)(2,1)S(1)}, f32[512,128]{1,0:T(8,128)S(1)}, bf16[256,512]{1,0:T(8,128)(2,1)S(1)}) custom-call(s32[4]{0:T(128)S(1)} %pad_add_fusion.info, f32[128,1024]{1,0:T(8,128)S(1)} %collective-permute-done.1.first, ...), custom_call_target="tpu_custom_call" | custom-call | flops 1 | bytes 1 | tf_op jit(solution)/shard_map/proj1/pallas_call | solution.py:36
  21.1 4.7 %collective-permute-start.3 = (f32[512,128]{1,0:T(8,128)S(1)}, f32[512,128]{1,0:T(8,128)S(1)}, u32[]{:S(2)}, u32[]{:S(2)}) collective-permute-start(f32[512,128]{1,0:T(8,128)S(1)} %get-tuple-element.79), channel_id=1, source_target_pairs={{0,8},{2,10},{4,12},{6,14},{1,9},{3,11},{5,13},{7,15},{16,24},{18,... | collective-permute-start | bytes 786440 | tf_op jit(solution)/shard_map/ppermute | solution.py:297
  25.8 6.0 %collective-permute-done.5.c2 = f32[128,1024]{1,0:T(8,128)S(1)} collective-permute-done((f32[128,1024]{1,0:T(8,128)S(1)}, f32[128,1024]{1,0:T(8,128)S(1)}, u32[]{:S(2)}, u32[]{:S(2)}) %collective-permute-start.5) | collective-permute-done | bytes 524320 | tf_op jit(solution)/shard_map/ppermute | solution.py:307
  31.8 4.9 %collective-permute-done.3.carried = f32[512,128]{1,0:T(8,128)S(1)} collective-permute-done((f32[512,128]{1,0:T(8,128)S(1)}, f32[512,128]{1,0:T(8,128)S(1)}, u32[]{:S(2)}, u32[]{:S(2)}) %collective-permute-start.3) | collective-permute-done | bytes 262176 | tf_op jit(solution)/shard_map/ppermute | solution.py:297
  36.7 1.9 %inside.1 = (bf16[512,512]{1,0:T(8,128)(2,1)S(1)}, bf16[512,512]{1,0:T(8,128)(2,1)S(1)}, bf16[512,512]{1,0:T(8,128)(2,1)S(1)}, bf16[4,512,512]{2,1,0:T(8,128)(2,1)S(1)}, f32[512,512]{1,0:T(8,128)S(1)}) custom-call(s32[4]{0:T(128)S(1)} %pad_add_fusion.info, bf16[256,512]{1,0:T(8,128)(2,1)S(1)} %get-tuple-element.68.q0, ...), custom_call_target="tpu_custom_call" | custom-call | flops 1 | bytes 1 | tf_op jit(solution)/shard_map/inside/pallas_call | solution.py:36
  38.7 1.3 %cotangent.1 = (bf16[512,1024]{1,0:T(8,128)(2,1)S(1)}, f32[512,512]{1,0:T(8,128)S(1)}) custom-call(s32[4]{0:T(128)S(1)} %pad_add_fusion.info, bf16[128,1024]{1,0:T(8,128)(2,1)S(1)} %bitcast.12, f32[128,1024]{1,0:T(8,128)S(1)} %collective-permute-done.4.c1, f32[128,1024]{1,0:T(8,128)S(1)} %collective-permute-done.5.c2, ...), custom_call_target="tpu_custom_call" | custom-call | flops 1 | bytes 1 | tf_op jit(solution)/shard_map/cotangent/pallas_call | solution.py:36
  40.0 1.0 stats.1
  41.0 0.6 collective-permute-start.7
  41.5 1.2 %collective-permute-done.7.other = f32[512,128]{1,0:T(8,128)S(1)} collective-permute-done((f32[512,128]{1,0:T(8,128)S(1)}, f32[512,128]{1,0:T(8,128)S(1)}, u32[]{:S(2)}, u32[]{:S(2)}) %collective-permute-start.7) | collective-permute-done | bytes 262176 | tf_op jit(solution)/shard_map/ppermute | solution.py:350
  42.7 3.2 %norm.1 = (f32[512,512]{1,0:T(8,128)S(1)}, bf16[512,512]{1,0:T(8,128)(2,1)S(1)}, f32[256,128]{1,0:T(8,128)S(1)}, bf16[512,512]{1,0:T(8,128)(2,1)S(1)}, bf16[4,51...) custom-call(s32[4]{0:T(128)S(1)} %pad_add_fusion.info, ...), custom_call_target="tpu_custom_call" | custom-call | flops 1 | bytes 1 | tf_op jit(solution)/shard_map/norm/pallas_call | solution.py:36
  46.3 1.5 %collective-permute-start.8 = (f32[256,256]{1,0:T(8,128)S(1)}, f32[256,256]{1,0:T(8,128)S(1)}, u32[]{:S(2)}, u32[]{:S(2)}) collective-permute-start(f32[256,256]{1,0:T(8,128)S(1)} %get-tuple-element.91), channel_id=1, source_target_pairs={{0,1},{1,0},{2,3},{3,2},{4,5},{5,4},{6,7},{7,6},{8,9},{9,8},{10,11... | collective-permute-start | bytes 786440 | tf_op jit(solution)/shard_map/ppermute | solution.py:405
  47.8 1.5 %collective-permute-start.12 = (f32[256,128]{1,0:T(8,128)S(1)}, f32[256,128]{1,0:T(8,128)S(1)}, u32[]{:S(2)}, u32[]{:S(2)}) collective-permute-start(f32[256,128]{1,0:T(8,128)S(1)} %get-tuple-element.98), channel_id=1, source_target_pairs={{8,0},{10,2},{12,4},{14,6},{9,1},{11,3},{13,5},{15,7},{24,16},{26,... | collective-permute-start | bytes 393224 | tf_op jit(solution)/shard_map/ppermute | solution.py:297
  49.3 0.6 collective-permute-start.9
  49.9 5.6 %collective-permute-done.8 = f32[256,256]{1,0:T(8,128)S(1)} collective-permute-done((f32[256,256]{1,0:T(8,128)S(1)}, f32[256,256]{1,0:T(8,128)S(1)}, u32[]{:S(2)}, u32[]{:S(2)}) %collective-permute-start.8) | collective-permute-done | bytes 262176 | tf_op jit(solution)/shard_map/ppermute | solution.py:405
  55.5 3.3 %collective-permute-done.12.later = f32[256,128]{1,0:T(8,128)S(1)} collective-permute-done((f32[256,128]{1,0:T(8,128)S(1)}, f32[256,128]{1,0:T(8,128)S(1)}, u32[]{:S(2)}, u32[]{:S(2)}) %collective-permute-start.12) | collective-permute-done | bytes 131104 | tf_op jit(solution)/shard_map/ppermute | solution.py:297
  58.8 1.2 %grad_o.1 = (f32[256,512]{1,0:T(8,128)S(1)}, f32[256,512]{1,0:T(8,128)S(1)}) custom-call(s32[4]{0:T(128)S(1)} %pad_add_fusion.info, f32[512,512]{1,0:T(8,128)S(1)} %get-tuple-element.96.mine, f32[512,512]{1,0:T(8,128)S(1)} %collective-permute-done.11.other, bf16[512,1024]{1,0:T(8,128)(2,1)S(1)} %get-tuple-element.108.cot), custom_call_target="tpu_custom_call" | custom-call | flops 1 | bytes 1 | tf_op jit(solution)/shard_map/grad_o/pallas_call | solution.py:36
  60.0 0.6 collective-permute-start.14
  60.6 3.2 %collective-permute-start.10 = (f32[128,256]{1,0:T(8,128)S(1)}, f32[128,256]{1,0:T(8,128)S(1)}, u32[]{:S(2)}, u32[]{:S(2)}) collective-permute-start(f32[128,256]{1,0:T(8,128)S(1)} %get-tuple-element.147), channel_id=1, source_target_pairs={{0,8},{2,10},{4,12},{6,14},{8,0},{10,2},{12,4},{14,6},{1,9},{3,11}... | collective-permute-start | bytes 393224 | tf_op jit(solution)/shard_map/ppermute | solution.py:405
  63.9 1.8 %back_rest.1 = (f32[512,512]{1,0:T(8,128)S(1)}, f32[512,512]{1,0:T(8,128)S(1)}) custom-call(s32[4]{0:T(128)S(1)} %pad_add_fusion.info, bf16[512,512]{1,0:T(8,128)(2,1)S(1)} %get-tuple-element.76.q, bf16[512,512]{1,0:T(8,128)(2,1)S(1)} %get-tuple-element.100.d_mixed, bf16[4,512,512]{2,1,0:T(8,128)(2,1)S(1)} %get-tuple-element.101.attn, ...), custom_call_target="tpu_custom_call" | custom-call | flops 1 | bytes 1 | tf_op jit(solution)/shard_map/back_rest/pallas_call | solution.py:36
  65.8 1.0 finish.1
  66.8 1.1 grad_k.1
  67.8 0.6 collective-permute-start.16
  68.5 1.4 %collective-permute-start.15 = (f32[128,256]{1,0:T(8,128)S(1)}, f32[128,256]{1,0:T(8,128)S(1)}, u32[]{:S(2)}, u32[]{:S(2)}) collective-permute-start(f32[128,256]{1,0:T(8,128)S(1)} %get-tuple-element.145), channel_id=1, source_target_pairs={{0,8},{2,10},{4,12},{6,14},{8,0},{10,2},{12,4},{14,6},{1,9},{3,11}... | collective-permute-start | bytes 393224 | tf_op jit(solution)/shard_map/ppermute | solution.py:405
  69.9 1.1 grad_v.1
  71.0 1.7 %attended.1 = bf16[128,1024]{1,0:T(8,128)(2,1)} custom-call(s32[4]{0:T(128)S(1)} %pad_add_fusion.info, f32[512,512]{1,0:T(8,128)S(1)} %get-tuple-element.96.mine, f32[512,512]{1,0:T(8,128)S(1)} %collective-permute-done.11.other, bf16[1024,1024]{1,0:T(8,128)(2,1)S(1)} %copy-done.6), custom_call_target="tpu_custom_call" | custom-call | flops 1 | bytes 1 | tf_op jit(solution)/shard_map/attended/pallas_call | solution.py:36
  72.7 0.5 collective-permute-start.19
  73.2 1.7 %collective-permute-done.14 = f32[256,512]{1,0:T(8,128)S(1)} collective-permute-done((f32[256,512]{1,0:T(8,128)S(1)}, f32[256,512]{1,0:T(8,128)S(1)}, u32[]{:S(2)}, u32[]{:S(2)}) %collective-permute-start.14) | collective-permute-done | bytes 524320 | tf_op jit(solution)/shard_map/ppermute | solution.py:405
  75.1 2.3 %collective-permute-start.18 = (f32[128,512]{1,0:T(8,128)S(1)}, f32[128,512]{1,0:T(8,128)S(1)}, u32[]{:S(2)}, u32[]{:S(2)}) collective-permute-start(f32[128,512]{1,0:T(8,128)S(1)} %get-tuple-element.135), channel_id=1, source_target_pairs={{0,8},{2,10},{4,12},{6,14},{8,0},{10,2},{12,4},{14,6},{1,9},{3,11}... | collective-permute-start | bytes 786440 | tf_op jit(solution)/shard_map/ppermute | solution.py:405
  77.4 1.6 %collective-permute-start.21 = (f32[256,256]{1,0:T(8,128)S(1)}, f32[256,256]{1,0:T(8,128)S(1)}, u32[]{:S(2)}, u32[]{:S(2)}) collective-permute-start(f32[256,256]{1,0:T(8,128)S(1)} %get-tuple-element.130), channel_id=1, source_target_pairs={{0,1},{1,0},{2,3},{3,2},{4,5},{5,4},{6,7},{7,6},{8,9},{9,8},{10,11... | collective-permute-start | bytes 786440 | tf_op jit(solution)/shard_map/ppermute | solution.py:405
  78.9 7.2 %collective-permute-done.16 = f32[256,512]{1,0:T(8,128)S(1)} collective-permute-done((f32[256,512]{1,0:T(8,128)S(1)}, f32[256,512]{1,0:T(8,128)S(1)}, u32[]{:S(2)}, u32[]{:S(2)}) %collective-permute-start.16) | collective-permute-done | bytes 524320 | tf_op jit(solution)/shard_map/ppermute | solution.py:405
  86.3 1.6 %d_tokens.1 = (f32[128,1024]{1,0:T(8,128)S(1)}, f32[128,1024]{1,0:T(8,128)S(1)}) custom-call(s32[4]{0:T(128)S(1)} %pad_add_fusion.info, bf16[512,512]{1,0:T(8,128)(2,1)S(1)} %get-tuple-element.116.dq, bf16[512,512]{1,0:T(8,128)(2,1)S(1)} %get-tuple-element.106.grad.dk, bf16[512,512]{1,0:T(8,128)(2,1)S(1)} %get-tuple-element.121.dv.grad, ...), custom_call_target="tpu_custom_call" | custom-call | flops 1 | bytes 1 | tf_op jit(solution)/shard_map/d_tokens/pallas_call | solution.py:36
  87.9 2.3 %collective-permute-start.20 = (f32[128,512]{1,0:T(8,128)S(1)}, f32[128,512]{1,0:T(8,128)S(1)}, u32[]{:S(2)}, u32[]{:S(2)}) collective-permute-start(f32[128,512]{1,0:T(8,128)S(1)} %get-tuple-element.133), channel_id=1, source_target_pairs={{0,8},{2,10},{4,12},{6,14},{8,0},{10,2},{12,4},{14,6},{1,9},{3,11}... | collective-permute-start | bytes 786440 | tf_op jit(solution)/shard_map/ppermute | solution.py:405
  90.2 1.5 %collective-permute-done.19 = f32[256,256]{1,0:T(8,128)S(1)} collective-permute-done((f32[256,256]{1,0:T(8,128)S(1)}, f32[256,256]{1,0:T(8,128)S(1)}, u32[]{:S(2)}, u32[]{:S(2)}) %collective-permute-start.19) | collective-permute-done | bytes 262176 | tf_op jit(solution)/shard_map/ppermute | solution.py:405
  91.8 2.3 %collective-permute-start.22 = (f32[128,256]{1,0:T(8,128)S(1)}, f32[128,256]{1,0:T(8,128)S(1)}, u32[]{:S(2)}, u32[]{:S(2)}) collective-permute-start(f32[128,256]{1,0:T(8,128)S(1)} %get-tuple-element.143), channel_id=1, source_target_pairs={{0,8},{2,10},{4,12},{6,14},{8,0},{10,2},{12,4},{14,6},{1,9},{3,11}... | collective-permute-start | bytes 393224 | tf_op jit(solution)/shard_map/ppermute | solution.py:405
  94.1 9.2 %collective-permute-done.20 = f32[128,512]{1,0:T(8,128)S(1)} collective-permute-done((f32[128,512]{1,0:T(8,128)S(1)}, f32[128,512]{1,0:T(8,128)S(1)}, u32[]{:S(2)}, u32[]{:S(2)}) %collective-permute-start.20) | collective-permute-done | bytes 262176 | tf_op jit(solution)/shard_map/ppermute | solution.py:405
  103.5 3.4 %collective-permute-done.22 = f32[128,256]{1,0:T(8,128)S(1)} collective-permute-done((f32[128,256]{1,0:T(8,128)S(1)}, f32[128,256]{1,0:T(8,128)S(1)}, u32[]{:S(2)}, u32[]{:S(2)}) %collective-permute-start.22) | collective-permute-done | bytes 131104 | tf_op jit(solution)/shard_map/ppermute | solution.py:405
  107.1 3.7 %collective-permute-done.23 = f32[128,256]{1,0:T(8,128)S(1)} collective-permute-done((f32[128,256]{1,0:T(8,128)S(1)}, f32[128,256]{1,0:T(8,128)S(1)}, u32[]{:S(2)}, u32[]{:S(2)}) %collective-permute-start.23) | collective-permute-done | bytes 131104 | tf_op jit(solution)/shard_map/ppermute | solution.py:405
  110.9 0.8 fusion
  112.2 1.6 %assemble.1 = f32[64,4096]{1,0:T(8,128)} custom-call(s32[4]{0:T(128)S(1)} %pad_add_fusion.info, f32[64,256]{1,0:T(8,128)S(1)} %get-tuple-element.156.refs_0_, f32[64,256]{1,0:T(8,128)S(1)} %get-tuple-element.154.refs_1_, f32[64,512]{1,0:T(8,128)S(1)} %get-tuple-element.140.refs_2_, f32[64,512]{1,0:T(8,128)S(1)} %get-tuple-element.138.refs_3_, ...), custom_call_target="tpu_custom_call" | custom-call | flops 1 | bytes 1 | tf_op jit(solution)/shard_map/assemble/pallas_call | solution.py:36
  (64 shorter events, 2.6 us)
Async XLA Ops:
  1.6 3.2 %collective-permute-start = (f32[128,1024]{1,0:T(8,128)S(1)}, f32[128,1024]{1,0:T(8,128)S(1)}, u32[]{:S(2)}, u32[]{:S(2)}) collective-permute-start(f32[128,1024]{1,0:T(8,128)S(1)} %bitcast_convert_fusion), channel_id=1, source_target_pairs={{0,2},{2,0},{4,6},{6,4},{8,10},{10,8},{12,14},{14,12},{1,3},{3,1},... | collective-permute-start | bytes 1572872 | tf_op jit(solution)/shard_map/ppermute | solution.py:305
  2.1 15.2 %collective-permute-start.1 = (f32[128,1024]{1,0:T(8,128)S(1)}, f32[128,1024]{1,0:T(8,128)S(1)}, u32[]{:S(2)}, u32[]{:S(2)}) collective-permute-start(f32[128,1024]{1,0:T(8,128)S(1)} %bitcast_convert_fusion), channel_id=1, source_target_pairs={{0,4},{2,6},{4,0},{6,2},{8,12},{10,14},{12,8},{14,10},{1,5},{3,7},... | collective-permute-start | bytes 1572872 | tf_op jit(solution)/shard_map/ppermute | solution.py:304
  4.9 1.6 %copy-start = (bf16[1024,1024]{1,0:T(8,128)(2,1)S(1)}, bf16[1024,1024]{1,0:T(8,128)(2,1)}, u32[]{:S(2)}) copy-start(bf16[1024,1024]{1,0:T(8,128)(2,1)} %w_q.5) | copy-start | bytes 6291460
  6.5 1.6 %copy-start.2 = (bf16[1024,1024]{1,0:T(8,128)(2,1)S(1)}, bf16[1024,1024]{1,0:T(8,128)(2,1)}, u32[]{:S(2)}) copy-start(bf16[1024,1024]{1,0:T(8,128)(2,1)} %w_k.5) | copy-start | bytes 6291460
  8.1 1.6 %copy-start.4 = (bf16[1024,1024]{1,0:T(8,128)(2,1)S(1)}, bf16[1024,1024]{1,0:T(8,128)(2,1)}, u32[]{:S(2)}) copy-start(bf16[1024,1024]{1,0:T(8,128)(2,1)} %w_v.5) | copy-start | bytes 6291460
  9.7 0.9 copy-start.7
  10.6 6.7 %copy-start.8 = (bf16[1,128,1024]{2,1,0:T(8,128)(2,1)S(1)}, bf16[1,128,1024]{2,1,0:T(8,128)(2,1)}, u32[]{:S(2)}) copy-start(bf16[1,128,1024]{2,1,0:T(8,128)(2,1)} %param.11) | copy-start | bytes 786436
  10.6 8.6 %copy-start.1 = (bf16[1024,1024]{1,0:T(8,128)(2,1)S(1)}, bf16[1024,1024]{1,0:T(8,128)(2,1)}, u32[]{:S(2)}) copy-start(bf16[1024,1024]{1,0:T(8,128)(2,1)} %w_q.5) | copy-start | bytes 6291460
  10.6 8.6 %copy-start.3 = (bf16[1024,1024]{1,0:T(8,128)(2,1)S(1)}, bf16[1024,1024]{1,0:T(8,128)(2,1)}, u32[]{:S(2)}) copy-start(bf16[1024,1024]{1,0:T(8,128)(2,1)} %w_k.5) | copy-start | bytes 6291460
  10.6 8.6 %copy-start.5 = (bf16[1024,1024]{1,0:T(8,128)(2,1)S(1)}, bf16[1024,1024]{1,0:T(8,128)(2,1)}, u32[]{:S(2)}) copy-start(bf16[1024,1024]{1,0:T(8,128)(2,1)} %w_v.5) | copy-start | bytes 6291460
  17.3 1.9 %collective-permute-start.2 = (f32[128,1024]{1,0:T(8,128)S(1)}, f32[128,1024]{1,0:T(8,128)S(1)}, u32[]{:S(2)}, u32[]{:S(2)}) collective-permute-start(f32[128,1024]{1,0:T(8,128)S(1)} %collective-permute-done.1.first), channel_id=1, source_target_pairs={{0,2},{2,0},{4,6},{6,4},{8,10},{10,8},{12,14},{14,12},{1,3},{3,1},... | collective-permute-start | bytes 1572872 | tf_op jit(solution)/shard_map/ppermute | solution.py:318
  17.4 14.4 %collective-permute-start.5 = (f32[128,1024]{1,0:T(8,128)S(1)}, f32[128,1024]{1,0:T(8,128)S(1)}, u32[]{:S(2)}, u32[]{:S(2)}) collective-permute-start(f32[128,1024]{1,0:T(8,128)S(1)} %convert_element_type.10), channel_id=1, source_target_pairs={{0,4},{2,6},{4,0},{6,2},{8,12},{10,14},{12,8},{14,10},{1,5},{3,7},... | collective-permute-start | bytes 1572872 | tf_op jit(solution)/shard_map/ppermute | solution.py:307
  19.2 19.4 %copy-start.6 = (bf16[1024,1024]{1,0:T(8,128)(2,1)S(1)}, bf16[1024,1024]{1,0:T(8,128)(2,1)}, u32[]{:S(2)}) copy-start(bf16[1024,1024]{1,0:T(8,128)(2,1)} %w_o.3) | copy-start | bytes 6291460
  21.1 15.7 %collective-permute-start.3 = (f32[512,128]{1,0:T(8,128)S(1)}, f32[512,128]{1,0:T(8,128)S(1)}, u32[]{:S(2)}, u32[]{:S(2)}) collective-permute-start(f32[512,128]{1,0:T(8,128)S(1)} %get-tuple-element.79), channel_id=1, source_target_pairs={{0,8},{2,10},{4,12},{6,14},{1,9},{3,11},{5,13},{7,15},{16,24},{18,... | collective-permute-start | bytes 786440 | tf_op jit(solution)/shard_map/ppermute | solution.py:297
  25.8 12.9 %collective-permute-start.4 = (f32[128,1024]{1,0:T(8,128)S(1)}, f32[128,1024]{1,0:T(8,128)S(1)}, u32[]{:S(2)}, u32[]{:S(2)}) collective-permute-start(f32[128,1024]{1,0:T(8,128)S(1)} %convert_element_type.10), channel_id=1, source_target_pairs={{0,2},{2,0},{4,6},{6,4},{8,10},{10,8},{12,14},{14,12},{1,3},{3,1},... | collective-permute-start | bytes 1572872 | tf_op jit(solution)/shard_map/ppermute | solution.py:308
  36.7 2.0 %collective-permute-start.6 = (f32[128,1024]{1,0:T(8,128)S(1)}, f32[128,1024]{1,0:T(8,128)S(1)}, u32[]{:S(2)}, u32[]{:S(2)}) collective-permute-start(f32[128,1024]{1,0:T(8,128)S(1)} %collective-permute-done.5.c2), channel_id=1, source_target_pairs={{0,2},{2,0},{4,6},{6,4},{8,10},{10,8},{12,14},{14,12},{1,3},{3,1},... | collective-permute-start | bytes 1572872 | tf_op jit(solution)/shard_map/ppermute | solution.py:332
  41.0 1.7 %collective-permute-start.7 = (f32[512,128]{1,0:T(8,128)S(1)}, f32[512,128]{1,0:T(8,128)S(1)}, u32[]{:S(2)}, u32[]{:S(2)}) collective-permute-start(f32[512,128]{1,0:T(8,128)S(1)} %get-tuple-element.86.mine), channel_id=1, source_target_pairs={{0,2},{2,0},{4,6},{6,4},{8,10},{10,8},{12,14},{14,12},{1,3},{3,1},... | collective-permute-start | bytes 786440 | tf_op jit(solution)/shard_map/ppermute | solution.py:350
  45.9 13.0 %collective-permute-start.11 = (f32[512,512]{1,0:T(8,128)S(1)}, f32[512,512]{1,0:T(8,128)S(1)}, u32[]{:S(2)}, u32[]{:S(2)}) collective-permute-start(f32[512,512]{1,0:T(8,128)S(1)} %get-tuple-element.96.mine), channel_id=1, source_target_pairs={{0,2},{2,0},{4,6},{6,4},{8,10},{10,8},{12,14},{14,12},{1,3},{3,1},... | collective-permute-start | bytes 3145736 | tf_op jit(solution)/shard_map/ppermute | solution.py:374
  46.3 9.2 %collective-permute-start.8 = (f32[256,256]{1,0:T(8,128)S(1)}, f32[256,256]{1,0:T(8,128)S(1)}, u32[]{:S(2)}, u32[]{:S(2)}) collective-permute-start(f32[256,256]{1,0:T(8,128)S(1)} %get-tuple-element.91), channel_id=1, source_target_pairs={{0,1},{1,0},{2,3},{3,2},{4,5},{5,4},{6,7},{7,6},{8,9},{9,8},{10,11... | collective-permute-start | bytes 786440 | tf_op jit(solution)/shard_map/ppermute | solution.py:405
  47.8 11.0 %collective-permute-start.12 = (f32[256,128]{1,0:T(8,128)S(1)}, f32[256,128]{1,0:T(8,128)S(1)}, u32[]{:S(2)}, u32[]{:S(2)}) collective-permute-start(f32[256,128]{1,0:T(8,128)S(1)} %get-tuple-element.98), channel_id=1, source_target_pairs={{8,0},{10,2},{12,4},{14,6},{9,1},{11,3},{13,5},{15,7},{24,16},{26,... | collective-permute-start | bytes 393224 | tf_op jit(solution)/shard_map/ppermute | solution.py:297
  49.3 14.6 %collective-permute-start.9 = (f32[256,256]{1,0:T(8,128)S(1)}, f32[256,256]{1,0:T(8,128)S(1)}, u32[]{:S(2)}, u32[]{:S(2)}) collective-permute-start(f32[256,256]{1,0:T(8,128)S(1)} %get-tuple-element.94), channel_id=1, source_target_pairs={{0,1},{1,0},{2,3},{3,2},{4,5},{5,4},{6,7},{7,6},{8,9},{9,8},{10,11... | collective-permute-start | bytes 786440 | tf_op jit(solution)/shard_map/ppermute | solution.py:405
  58.8 6.9 %collective-permute-start.13 = (f32[256,128]{1,0:T(8,128)S(1)}, f32[256,128]{1,0:T(8,128)S(1)}, u32[]{:S(2)}, u32[]{:S(2)}) collective-permute-start(f32[256,128]{1,0:T(8,128)S(1)} %collective-permute-done.12.later), channel_id=1, source_target_pairs={{0,4},{2,6},{4,0},{6,2},{8,12},{10,14},{12,8},{14,10},{1,5},{3,7},... | collective-permute-start | bytes 393224 | tf_op jit(solution)/shard_map/ppermute | solution.py:460
  60.0 14.9 %collective-permute-start.14 = (f32[256,512]{1,0:T(8,128)S(1)}, f32[256,512]{1,0:T(8,128)S(1)}, u32[]{:S(2)}, u32[]{:S(2)}) collective-permute-start(f32[256,512]{1,0:T(8,128)S(1)} %get-tuple-element.111), channel_id=1, source_target_pairs={{0,1},{1,0},{2,3},{3,2},{4,5},{5,4},{6,7},{7,6},{8,9},{9,8},{10,11... | collective-permute-start | bytes 1572872 | tf_op jit(solution)/shard_map/ppermute | solution.py:405
  60.6 9.2 %collective-permute-start.10 = (f32[128,256]{1,0:T(8,128)S(1)}, f32[128,256]{1,0:T(8,128)S(1)}, u32[]{:S(2)}, u32[]{:S(2)}) collective-permute-start(f32[128,256]{1,0:T(8,128)S(1)} %get-tuple-element.147), channel_id=1, source_target_pairs={{0,8},{2,10},{4,12},{6,14},{8,0},{10,2},{12,4},{14,6},{1,9},{3,11}... | collective-permute-start | bytes 393224 | tf_op jit(solution)/shard_map/ppermute | solution.py:405
  67.8 18.3 %collective-permute-start.16 = (f32[256,512]{1,0:T(8,128)S(1)}, f32[256,512]{1,0:T(8,128)S(1)}, u32[]{:S(2)}, u32[]{:S(2)}) collective-permute-start(f32[256,512]{1,0:T(8,128)S(1)} %get-tuple-element.115), channel_id=1, source_target_pairs={{0,1},{1,0},{2,3},{3,2},{4,5},{5,4},{6,7},{7,6},{8,9},{9,8},{10,11... | collective-permute-start | bytes 1572872 | tf_op jit(solution)/shard_map/ppermute | solution.py:405
  68.5 8.9 %collective-permute-start.15 = (f32[128,256]{1,0:T(8,128)S(1)}, f32[128,256]{1,0:T(8,128)S(1)}, u32[]{:S(2)}, u32[]{:S(2)}) collective-permute-start(f32[128,256]{1,0:T(8,128)S(1)} %get-tuple-element.145), channel_id=1, source_target_pairs={{0,8},{2,10},{4,12},{6,14},{8,0},{10,2},{12,4},{14,6},{1,9},{3,11}... | collective-permute-start | bytes 393224 | tf_op jit(solution)/shard_map/ppermute | solution.py:405
  72.7 19.1 %collective-permute-start.19 = (f32[256,256]{1,0:T(8,128)S(1)}, f32[256,256]{1,0:T(8,128)S(1)}, u32[]{:S(2)}, u32[]{:S(2)}) collective-permute-start(f32[256,256]{1,0:T(8,128)S(1)} %get-tuple-element.125), channel_id=1, source_target_pairs={{0,1},{1,0},{2,3},{3,2},{4,5},{5,4},{6,7},{7,6},{8,9},{9,8},{10,11... | collective-permute-start | bytes 786440 | tf_op jit(solution)/shard_map/ppermute | solution.py:405
  75.1 15.1 %collective-permute-start.18 = (f32[128,512]{1,0:T(8,128)S(1)}, f32[128,512]{1,0:T(8,128)S(1)}, u32[]{:S(2)}, u32[]{:S(2)}) collective-permute-start(f32[128,512]{1,0:T(8,128)S(1)} %get-tuple-element.135), channel_id=1, source_target_pairs={{0,8},{2,10},{4,12},{6,14},{8,0},{10,2},{12,4},{14,6},{1,9},{3,11}... | collective-permute-start | bytes 786440 | tf_op jit(solution)/shard_map/ppermute | solution.py:405
  77.4 26.0 %collective-permute-start.21 = (f32[256,256]{1,0:T(8,128)S(1)}, f32[256,256]{1,0:T(8,128)S(1)}, u32[]{:S(2)}, u32[]{:S(2)}) collective-permute-start(f32[256,256]{1,0:T(8,128)S(1)} %get-tuple-element.130), channel_id=1, source_target_pairs={{0,1},{1,0},{2,3},{3,2},{4,5},{5,4},{6,7},{7,6},{8,9},{9,8},{10,11... | collective-permute-start | bytes 786440 | tf_op jit(solution)/shard_map/ppermute | solution.py:405
  87.9 15.4 %collective-permute-start.20 = (f32[128,512]{1,0:T(8,128)S(1)}, f32[128,512]{1,0:T(8,128)S(1)}, u32[]{:S(2)}, u32[]{:S(2)}) collective-permute-start(f32[128,512]{1,0:T(8,128)S(1)} %get-tuple-element.133), channel_id=1, source_target_pairs={{0,8},{2,10},{4,12},{6,14},{8,0},{10,2},{12,4},{14,6},{1,9},{3,11}... | collective-permute-start | bytes 786440 | tf_op jit(solution)/shard_map/ppermute | solution.py:405
  90.2 20.7 %collective-permute-start.17 = (f32[128,1024]{1,0:T(8,128)S(1)}, f32[128,1024]{1,0:T(8,128)S(1)}, u32[]{:S(2)}, u32[]{:S(2)}) collective-permute-start(f32[128,1024]{1,0:T(8,128)S(1)} %get-tuple-element.119), channel_id=1, source_target_pairs={{0,2},{2,0},{4,6},{6,4},{8,10},{10,8},{12,14},{14,12},{1,3},{3,1},... | collective-permute-start | bytes 1572872 | tf_op jit(solution)/shard_map/ppermute | solution.py:497
  91.8 15.1 %collective-permute-start.22 = (f32[128,256]{1,0:T(8,128)S(1)}, f32[128,256]{1,0:T(8,128)S(1)}, u32[]{:S(2)}, u32[]{:S(2)}) collective-permute-start(f32[128,256]{1,0:T(8,128)S(1)} %get-tuple-element.143), channel_id=1, source_target_pairs={{0,8},{2,10},{4,12},{6,14},{8,0},{10,2},{12,4},{14,6},{1,9},{3,11}... | collective-permute-start | bytes 393224 | tf_op jit(solution)/shard_map/ppermute | solution.py:405
  103.5 7.3 %collective-permute-start.23 = (f32[128,256]{1,0:T(8,128)S(1)}, f32[128,256]{1,0:T(8,128)S(1)}, u32[]{:S(2)}, u32[]{:S(2)}) collective-permute-start(f32[128,256]{1,0:T(8,128)S(1)} %get-tuple-element.141), channel_id=1, source_target_pairs={{0,8},{2,10},{4,12},{6,14},{8,0},{10,2},{12,4},{14,6},{1,9},{3,11}... | collective-permute-start | bytes 393224 | tf_op jit(solution)/shard_map/ppermute | solution.py:405
  107.0 5.2 %collective-permute-start.24 = (f32[64,1792]{1,0:T(8,128)S(1)}, f32[64,1792]{1,0:T(8,128)S(1)}, u32[]{:S(2)}, u32[]{:S(2)}) collective-permute-start(f32[64,1792]{1,0:T(8,128)S(1)} %get-tuple-element.151), channel_id=1, source_target_pairs={{0,2},{2,0},{4,6},{6,4},{8,10},{10,8},{12,14},{14,12},{1,3},{3,1},... | collective-permute-start | bytes 1376264 | tf_op jit(solution)/shard_map/ppermute | solution.py:414
  110.8 1.3 %collective-permute-start.25 = (f32[64,256]{1,0:T(8,128)S(1)}, f32[64,256]{1,0:T(8,128)S(1)}, u32[]{:S(2)}, u32[]{:S(2)}) collective-permute-start(f32[64,256]{1,0:T(8,128)S(1)} %get-tuple-element.149), channel_id=1, source_target_pairs={{0,2},{2,0},{4,6},{6,4},{8,10},{10,8},{12,14},{14,12},{1,3},{3,1},... | collective-permute-start | bytes 196616 | tf_op jit(solution)/shard_map/ppermute | solution.py:414
